TPU v7x, 32 devices: a whole 2x2x4 slice. The times are simulated.
32 devices in a mesh: dp: 8 (over z, x), tensor: 4 (over y, core).
Axes of the slice: x: 2, y: 2, z: 4, core: 2. Of those that a mesh axis runs over, the one named last changes fastest.
Arguments:
- tokens: bfloat16 [8192, 1024], P('dp'), may hold values from -6 to 6
- w_query: bfloat16 [1024, 1024], P(None, 'tensor'), may hold values from -0.1875 to 0.1875
- w_key: bfloat16 [1024, 1024], P(None, 'tensor'), may hold values from -0.1875 to 0.1875
- w_value: bfloat16 [1024, 1024], P(None, 'tensor'), may hold values from -0.1875 to 0.1875
- w_output: bfloat16 [1024, 1024], P('tensor'), may hold values from -1.5 to 1.5
- w_gate: bfloat16 [1024, 2816], P(None, 'tensor'), may hold values from -0.1875 to 0.1875
- w_up: bfloat16 [1024, 2816], P(None, 'tensor'), may hold values from -0.1875 to 0.1875
- w_down: bfloat16 [2816, 1024], P('tensor'), may hold values from -0.109375 to 0.109375
- gain_attn: float32 [1024], replicated, may hold values from 0.1 to 1.9
- gain_mlp: float32 [1024], replicated, may hold values from 0.1 to 1.9
- cache_keys: bfloat16 [8, 8, 4096, 128], P('dp', 'tensor'), may hold values from -6 to 6
- cache_values: bfloat16 [8, 8, 4096, 128], P('dp', 'tensor'), may hold values from -6 to 6
- knn_index: int32 [8192, 128], P('dp'), may hold values from 0 to 8191, as said below
- memory_flag: int32 [8], P('dp'), may hold values from 0 to 1, as said below
- pairing: int32 [8], P('dp'), may hold values from 0 to 7, as said below
- cotangent: bfloat16 [8192, 1024], P('dp'), may hold values from -6 to 6
Outputs:
- output: bfloat16 [8192, 1024], P(('dp', 'tensor'))
- grad_tokens: bfloat16 [8192, 1024], P(('dp', 'tensor'))
- grad_w_query: float32 [1024, 1024], P('dp', 'tensor')
- grad_w_key: float32 [1024, 1024], P('dp', 'tensor')
- grad_w_value: float32 [1024, 1024], P('dp', 'tensor')
- grad_w_output: float32 [1024, 1024], P('tensor', 'dp')
- grad_w_gate: float32 [1024, 2816], P('dp', 'tensor')
- grad_w_up: float32 [1024, 2816], P('dp', 'tensor')
- grad_w_down: float32 [2816, 1024], P('tensor', 'dp')
- grad_gain_attn: float32 [1024], P('dp')
- grad_gain_mlp: float32 [1024], P('dp')
Inputs may be any that keep to these rules, and one draw needn't show every extreme that they name: `knn_index`: in every row, entry j lies in [j * 2 * 32, (j + 1) * 2 * 32); values below 4096 name rows of the document's own cache, the others row (value - 4096) of its partner's cache. `memory_flag`: exactly half of the documents have 1, among them documents 0, 4 and 7. pairing[pairing[b]] = b, and pairing[b] differs from b in exactly one bit of its binary number.
All inputs are finite; a program needn't handle non-finite values.
Results may differ from a plain program's by a relative error of at most 0.017.
Values may be sent and summed in bfloat16 or wider, within the bound.
No kernel may reach another device: no remote copies, remote signals or barrier semaphores. Data moves between devices by JAX's collectives and lax.ppermute only.
A program may use at most 256 MiB of HBM per device.

v0:
```python
import jax
import jax.numpy as jnp
from jax import lax
from jax.sharding import PartitionSpec as P

epsilon = 1e-05
negative_big = -1e30


def from_partner(array, axis, bit):
    return lax.ppermute(array, axis, [(i, i ^ 1 << bit) for i in range(lax.axis_size(axis))])


def norm_forward(values, gain):
    factor = lax.rsqrt(jnp.mean(values * values, axis=-1, keepdims=True) + epsilon)
    return (values * factor * gain, factor)


def norm_backward(values, factor, gain, grad_normed):
    scaled = gain * grad_normed
    return factor * scaled - values * (factor * factor * factor) * jnp.mean(
        values * scaled, axis=-1, keepdims=True
    )


def gain_part(grad_normed, values, factor):
    return jnp.sum(grad_normed * values * factor, axis=0)


def take_rows(values, row_offset, share):
    return lax.dynamic_slice_in_dim(values, row_offset, share, 0)


def rotate_tables(sequence_length, head_dim):
    half_dim = head_dim // 2
    position = jnp.arange(sequence_length, dtype=jnp.float32)
    inverse = jnp.exp(-jnp.log(10000.0) * jnp.arange(half_dim, dtype=jnp.float32) * 2.0 / head_dim)
    angles = position[:, None] * inverse[None, :]
    return (jnp.cos(angles)[:, None, :], jnp.sin(angles)[:, None, :])


def rotate(values, cos_table, sin_table, direction):
    half_dim = values.shape[-1] // 2
    front = values[..., :half_dim]
    back_part = values[..., half_dim:]
    return jnp.concatenate(
        [
            front * cos_table - direction * back_part * sin_table,
            back_part * cos_table + direction * front * sin_table,
        ],
        axis=-1,
    )


def scores_for(query_matrix, keys, stored_keys, index_rows, row_start, with_memory):
    width = query_matrix.shape[1]
    sequence_length = keys.shape[1]
    scale_factor = query_matrix.shape[-1] ** (-0.5)
    local = (
        jnp.einsum("hqd,hkd->hqk", query_matrix, keys, preferred_element_type=jnp.float32)
        * scale_factor
    )
    positions = row_start + jnp.arange(width, dtype=jnp.int32)
    causal = positions[:, None] >= jnp.arange(sequence_length, dtype=jnp.int32)[None, :]
    local = jnp.where(causal[None], local, negative_big)
    memory = None
    if with_memory:
        memory = (
            jnp.einsum(
                "uik,uwk->uiw", query_matrix, stored_keys, preferred_element_type=jnp.float32
            )
            * scale_factor
        )
        chosen = (
            jnp.zeros((width, stored_keys.shape[1]), bool)
            .at[jnp.arange(width, dtype=jnp.int32)[:, None], index_rows]
            .set(True)
        )
        memory = jnp.where(chosen[None], memory, negative_big)
    return (local, memory)


def forward_block(
    row_start, queries, keys, values, stored_keys, stored_values, knn_index, with_memory
):
    width = min(512, keys.shape[1])
    query_matrix = lax.dynamic_slice_in_dim(queries, row_start, width, 1)
    index_rows = lax.dynamic_slice_in_dim(knn_index, row_start, width, 0)
    local, memory = scores_for(query_matrix, keys, stored_keys, index_rows, row_start, with_memory)
    peak = jnp.max(local, axis=-1, keepdims=True)
    if with_memory:
        peak = jnp.maximum(peak, jnp.max(memory, axis=-1, keepdims=True))
    local_exp = jnp.exp(local - peak)
    total = jnp.sum(local_exp, axis=-1, keepdims=True)
    if with_memory:
        memory_exp = jnp.exp(memory - peak)
        total = total + jnp.sum(memory_exp, axis=-1, keepdims=True)
    attended = jnp.einsum(
        "hqk,hkd->hqd",
        (local_exp / total).astype(jnp.bfloat16),
        values,
        preferred_element_type=jnp.float32,
    )
    if with_memory:
        attended = attended + jnp.einsum(
            "xuj,xjg->xug",
            (memory_exp / total).astype(jnp.bfloat16),
            stored_values,
            preferred_element_type=jnp.float32,
        )
    return (attended, peak + jnp.log(total))


def backward_block(
    carry,
    row_start,
    queries,
    keys,
    values,
    stored_keys,
    stored_values,
    knn_index,
    grad_attended,
    log_total,
    with_memory,
):
    grad_keys, grad_values = carry
    width = min(512, keys.shape[1])
    scale_factor = queries.shape[-1] ** (-0.5)
    query_matrix = lax.dynamic_slice_in_dim(queries, row_start, width, 1)
    gradient_rows = lax.dynamic_slice_in_dim(grad_attended, row_start, width, 1)
    log_rows = lax.dynamic_slice_in_dim(log_total, row_start, width, 1)
    index_rows = lax.dynamic_slice_in_dim(knn_index, row_start, width, 0)
    local, memory = scores_for(query_matrix, keys, stored_keys, index_rows, row_start, with_memory)
    local_prob = jnp.exp(local - log_rows)
    local_dprob = jnp.einsum(
        "hqd,hkd->hqk", gradient_rows, values, preferred_element_type=jnp.float32
    )
    delta = jnp.sum(local_prob * local_dprob, axis=-1, keepdims=True)
    if with_memory:
        memory_prob = jnp.exp(memory - log_rows)
        memory_dprob = jnp.einsum(
            "uik,uwk->uiw", gradient_rows, stored_values, preferred_element_type=jnp.float32
        )
        delta = delta + jnp.sum(memory_prob * memory_dprob, axis=-1, keepdims=True)
    local_ds = (local_prob * (local_dprob - delta)).astype(jnp.bfloat16)
    grad_query = jnp.einsum("hqk,hkd->hqd", local_ds, keys, preferred_element_type=jnp.float32)
    if with_memory:
        memory_score_gradient = (memory_prob * (memory_dprob - delta)).astype(jnp.bfloat16)
        grad_query = grad_query + jnp.einsum(
            "xuj,xjg->xug", memory_score_gradient, stored_keys, preferred_element_type=jnp.float32
        )
    grad_keys = grad_keys + scale_factor * jnp.einsum(
        "hqk,hqd->hkd", local_ds, query_matrix, preferred_element_type=jnp.float32
    )
    grad_values = grad_values + jnp.einsum(
        "hqk,hqd->hkd",
        local_prob.astype(jnp.bfloat16),
        gradient_rows,
        preferred_element_type=jnp.float32,
    )
    return ((grad_keys, grad_values), grad_query * scale_factor)


def per_device(
    tokens,
    w_query,
    w_key,
    w_value,
    w_output,
    w_gate,
    w_up,
    w_down,
    gain_attn,
    gain_mlp,
    cache_keys,
    cache_values,
    knn_index,
    memory_flag,
    pairing,
    cotangent,
):
    sequence_length = tokens.shape[0]
    parts = lax.axis_size("tensor")
    share = sequence_length // parts
    row_offset = lax.axis_index("tensor") * share
    heads_here = cache_keys.shape[1]
    head_dim = cache_keys.shape[3]
    columns = heads_here * head_dim
    tokens_full = tokens.astype(jnp.float32)
    flag_on = memory_flag[0]
    own_keys = cache_keys[0]
    own_values = cache_values[0]
    partner = pairing[0]
    myself = lax.axis_index("dp")
    far_keys = jnp.zeros_like(own_keys)
    far_values = jnp.zeros_like(own_values)
    for bit_place in range(lax.axis_size("dp").bit_length() - 1):
        got_keys, got_values = from_partner((own_keys, own_values), "dp", bit_place)
        found = partner == jnp.bitwise_xor(myself, 1 << bit_place)
        far_keys = jnp.where(found, got_keys, far_keys)
        far_values = jnp.where(found, got_values, far_values)
    stored_keys = jnp.concatenate([own_keys, far_keys], axis=1)
    stored_values = jnp.concatenate([own_values, far_values], axis=1)
    normed_attn, factor_attn = norm_forward(tokens_full, gain_attn)
    normed_low = normed_attn.astype(jnp.bfloat16)
    cos_table, sin_table = rotate_tables(sequence_length, head_dim)

    def project_heads(matrix):
        return jnp.dot(normed_low, matrix, preferred_element_type=jnp.float32).reshape(
            sequence_length, heads_here, head_dim
        )

    queries = (
        rotate(project_heads(w_query), cos_table, sin_table, 1.0)
        .astype(jnp.bfloat16)
        .transpose(1, 0, 2)
    )
    keys = (
        rotate(project_heads(w_key), cos_table, sin_table, 1.0)
        .astype(jnp.bfloat16)
        .transpose(1, 0, 2)
    )
    values = project_heads(w_value).astype(jnp.bfloat16).transpose(1, 0, 2)
    width = min(512, sequence_length)
    blocks_count = sequence_length // width
    starts = jnp.arange(blocks_count, dtype=jnp.int32) * width

    def run_forward(with_memory):
        return lax.map(
            lambda row_start: forward_block(
                row_start, queries, keys, values, stored_keys, stored_values, knn_index, with_memory
            ),
            starts,
        )

    attended_blocks, log_blocks = lax.cond(
        flag_on > 0, lambda: run_forward(True), lambda: run_forward(False)
    )
    attended_heads = attended_blocks.transpose(1, 0, 2, 3).reshape(
        heads_here, sequence_length, head_dim
    )
    log_total = log_blocks.transpose(1, 0, 2, 3).reshape(heads_here, sequence_length, 1)
    attended_low = (
        attended_heads.transpose(1, 0, 2).reshape(sequence_length, columns).astype(jnp.bfloat16)
    )
    branch_part = jnp.dot(attended_low, w_output, preferred_element_type=jnp.float32)
    branch_rows = lax.psum_scatter(branch_part, "tensor", scatter_dimension=0, tiled=True)
    middle_rows = take_rows(tokens_full, row_offset, share) + branch_rows
    normed_rows, factor_rows = norm_forward(middle_rows, gain_mlp)
    normed_mlp = lax.all_gather(normed_rows.astype(jnp.bfloat16), "tensor", axis=0, tiled=True)
    gate = jnp.dot(normed_mlp, w_gate, preferred_element_type=jnp.float32)
    upper = jnp.dot(normed_mlp, w_up, preferred_element_type=jnp.float32)
    sigmoid_gate = jax.nn.sigmoid(gate)
    silu_gate = gate * sigmoid_gate
    hidden = (silu_gate * upper).astype(jnp.bfloat16)
    down_part = jnp.dot(hidden, w_down, preferred_element_type=jnp.float32)
    output_rows = middle_rows + lax.psum_scatter(
        down_part.astype(jnp.bfloat16), "tensor", scatter_dimension=0, tiled=True
    ).astype(jnp.float32)
    grad_hidden = jnp.dot(cotangent, w_down.T, preferred_element_type=jnp.float32)
    grad_gate = (grad_hidden * upper * sigmoid_gate * (1.0 + gate * (1.0 - sigmoid_gate))).astype(
        jnp.bfloat16
    )
    grad_upper = (grad_hidden * silu_gate).astype(jnp.bfloat16)
    grad_w_down = jnp.dot(hidden.T, cotangent, preferred_element_type=jnp.float32)
    grad_w_gate = jnp.dot(normed_mlp.T, grad_gate, preferred_element_type=jnp.float32)
    grad_w_up = jnp.dot(normed_mlp.T, grad_upper, preferred_element_type=jnp.float32)
    grad_normed_part = jnp.dot(grad_gate, w_gate.T, preferred_element_type=jnp.float32) + jnp.dot(
        grad_upper, w_up.T, preferred_element_type=jnp.float32
    )
    grad_normed_rows = lax.psum_scatter(grad_normed_part, "tensor", scatter_dimension=0, tiled=True)
    grad_middle_rows = take_rows(cotangent, row_offset, share).astype(jnp.float32) + norm_backward(
        middle_rows, factor_rows, gain_mlp, grad_normed_rows
    )
    gain_mlp_part = gain_part(grad_normed_rows, middle_rows, factor_rows)
    grad_branch = lax.all_gather(
        grad_middle_rows.astype(jnp.bfloat16), "tensor", axis=0, tiled=True
    )
    grad_w_output = jnp.dot(attended_low.T, grad_branch, preferred_element_type=jnp.float32)
    grad_attended = jnp.dot(grad_branch, w_output.T, preferred_element_type=jnp.float32).astype(
        jnp.bfloat16
    )
    grad_attended = grad_attended.reshape(sequence_length, heads_here, head_dim).transpose(1, 0, 2)
    empty_grad = jnp.zeros((heads_here, sequence_length, head_dim), jnp.float32)

    def run_backward(with_memory):
        return lax.scan(
            lambda carry, row_start: backward_block(
                carry,
                row_start,
                queries,
                keys,
                values,
                stored_keys,
                stored_values,
                knn_index,
                grad_attended,
                log_total,
                with_memory,
            ),
            (empty_grad, empty_grad),
            starts,
        )

    (grad_keys, grad_values), query_blocks = lax.cond(
        flag_on > 0, lambda: run_backward(True), lambda: run_backward(False)
    )
    grad_queries = query_blocks.transpose(1, 0, 2, 3).reshape(heads_here, sequence_length, head_dim)

    def unrotate(grad_heads):
        return (
            rotate(grad_heads.transpose(1, 0, 2), cos_table, sin_table, -1.0)
            .reshape(sequence_length, columns)
            .astype(jnp.bfloat16)
        )

    grad_query_low = unrotate(grad_queries)
    grad_key_low = unrotate(grad_keys)
    grad_value_low = (
        grad_values.transpose(1, 0, 2).reshape(sequence_length, columns).astype(jnp.bfloat16)
    )
    grad_w_query = jnp.dot(normed_low.T, grad_query_low, preferred_element_type=jnp.float32)
    grad_w_key = jnp.dot(normed_low.T, grad_key_low, preferred_element_type=jnp.float32)
    grad_w_value = jnp.dot(normed_low.T, grad_value_low, preferred_element_type=jnp.float32)
    grad_normed_attn = jnp.dot(grad_query_low, w_query.T, preferred_element_type=jnp.float32)
    grad_normed_attn = grad_normed_attn + jnp.dot(
        grad_key_low, w_key.T, preferred_element_type=jnp.float32
    )
    grad_normed_attn = grad_normed_attn + jnp.dot(
        grad_value_low, w_value.T, preferred_element_type=jnp.float32
    )
    grad_attn_rows = lax.psum_scatter(
        grad_normed_attn.astype(jnp.bfloat16), "tensor", scatter_dimension=0, tiled=True
    ).astype(jnp.float32)
    tokens_rows = take_rows(tokens_full, row_offset, share)
    factor_attn_rows = take_rows(factor_attn, row_offset, share)
    grad_tokens_rows = grad_middle_rows + norm_backward(
        tokens_rows, factor_attn_rows, gain_attn, grad_attn_rows
    )
    gain_attn_part = gain_part(grad_attn_rows, tokens_rows, factor_attn_rows)
    gain_attn_sum, gain_mlp_sum = lax.psum((gain_attn_part, gain_mlp_part), "tensor")
    summed = (
        lax.psum_scatter(grad_w_query, "dp", scatter_dimension=0, tiled=True),
        lax.psum_scatter(grad_w_key, "dp", scatter_dimension=0, tiled=True),
        lax.psum_scatter(grad_w_value, "dp", scatter_dimension=0, tiled=True),
        lax.psum_scatter(grad_w_output, "dp", scatter_dimension=1, tiled=True),
        lax.psum_scatter(grad_w_gate, "dp", scatter_dimension=0, tiled=True),
        lax.psum_scatter(grad_w_up, "dp", scatter_dimension=0, tiled=True),
        lax.psum_scatter(grad_w_down, "dp", scatter_dimension=1, tiled=True),
        lax.psum_scatter(gain_attn_sum, "dp", scatter_dimension=0, tiled=True),
        lax.psum_scatter(gain_mlp_sum, "dp", scatter_dimension=0, tiled=True),
    )
    return (
        output_rows.astype(jnp.bfloat16),
        grad_tokens_rows.astype(jnp.bfloat16),
        summed[0],
        summed[1],
        summed[2],
        summed[3],
        summed[4],
        summed[5],
        summed[6],
        summed[7],
        summed[8],
    )


def solution(mesh):
    placed = (
        P("dp", None),
        P(None, "tensor"),
        P(None, "tensor"),
        P(None, "tensor"),
        P("tensor", None),
        P(None, "tensor"),
        P(None, "tensor"),
        P("tensor", None),
        P(),
        P(),
        P("dp", "tensor", None, None),
        P("dp", "tensor", None, None),
        P("dp", None),
        P("dp"),
        P("dp"),
        P("dp", None),
    )
    return jax.shard_map(
        per_device,
        mesh=mesh,
        in_specs=placed,
        out_specs=(
            P(("dp", "tensor"), None),
            P(("dp", "tensor"), None),
            P("dp", "tensor"),
            P("dp", "tensor"),
            P("dp", "tensor"),
            P("tensor", "dp"),
            P("dp", "tensor"),
            P("dp", "tensor"),
            P("tensor", "dp"),
            P("dp"),
            P("dp"),
        ),
        check_vma=False,
    )
```

profile of v0, /device:TPU:0, one launch (start us, length us, event | category | flops | bytes accessed | tf_op | source)
XLA Modules:
  0.0 2433.7 jit_solution(4716152038861643467)
XLA Ops:
  60.2 44.2 %collective-permute-done.1 = bf16[2,4096,128]{2,1,0:T(8,128)(2,1)} collective-permute-done((bf16[2,4096,128]{2,1,0:T(8,128)(2,1)}, bf16[2,4096,128]{2,1,0:T(8,128)(2,1)}, u32[]{:S(2)}, u32[]{:S(2)}) %collective-permute-start.1) | collective-permute-done | bytes 2097184 | tf_op jit(solution)/shard_map/ppermute | solution.py:11
  110.4 82.0 %collective-permute-done.4 = bf16[2,4096,128]{2,1,0:T(8,128)(2,1)} collective-permute-done((bf16[2,4096,128]{2,1,0:T(8,128)(2,1)}, bf16[2,4096,128]{2,1,0:T(8,128)(2,1)}, u32[]{:S(2)}, u32[]{:S(2)}) %collective-permute-start.4) | collective-permute-done | bytes 2097184 | tf_op jit(solution)/shard_map/ppermute | solution.py:11
  198.8 726.4 %conditional.2 = (bf16[2,2,512,128]{3,2,1,0:T(8,128)(2,1)}, f32[2,2,512,1]{2,1,3,0:T(2,128)}) conditional(s32[]{:T(128)} %bitcast.8, (s32[2]{0:T(128)S(1)}, bf16[2,1024,128]{2,1,0:T(8,128)(2,1)S(1)}, bf16[2,1024,128]{2,1,0:T(8,128)(2,1)S(1)}, bf16[2,1024,128]{2,1,0:T(8,128)(2,1)}) %tuple.169, (s32[2]{0:T(128)S(1)}, ...), branch_computations={%region_1.6_spmd, %region_6.14_spmd} | conditional | flops 4946918912 | bytes 173814224 | solution.py:237
  198.8 726.1 %while.51 = (s32[]{:T(128)}, bf16[2,2,512,128]{3,2,1,0:T(8,128)(2,1)}, f32[2,2,512,1]{2,1,3,0:T(2,128)}, s32[2]{0:T(128)S(1)}, bf16[2,1024,128]{2,1,0:T(8,128)(2...) while((s32[]{:T(128)}, ...), condition=%wide.region_13.13_spmd, body=%wide.region_7.12_spmd.sunk | while | flops 4946918912 | bytes 173814064 | solution.py:230
  221.3 276.6 %scatter_custom_fusion.12 = pred[4194304]{0:T(1024)(128)(4,1)} fusion(s32[65536]{0:T(1024)S(1)} %select_bitcast_fusion.5, pred[65536]{0:T(1024)(128)(4,1)S(1)} %broadcast.470, pred[]{:T(512)} %constant.54.clone.1..sunk), kind=kCustom, calls=%fused_computation.24.clone.1 | custom fusion | bytes 4194305 | tf_op jit(solution)/shard_map/cond/branch_1_fun/while
  576.2 276.6 %scatter_custom_fusion.12 = pred[4194304]{0:T(1024)(128)(4,1)} fusion(s32[65536]{0:T(1024)S(1)} %select_bitcast_fusion.5, pred[65536]{0:T(1024)(128)(4,1)S(1)} %broadcast.470, pred[]{:T(512)} %constant.54.clone.1..sunk), kind=kCustom, calls=%fused_computation.24.clone.1 | custom fusion | bytes 4194305 | tf_op jit(solution)/shard_map/cond/branch_1_fun/while
  936.5 39.8 %reduce-scatter.12.cloned.1.call-done = f32[256,1024]{1,0:T(8,128)} async-done(((f32[1024,1024]{1,0:T(8,128)}), f32[256,1024]{1,0:T(8,128)}) %reduce-scatter.12.cloned.1.call-update) | async-done | bytes 1048592 | tf_op jit(solution)/shard_map/reduce_scatter | solution.py:248
  1023.4 40.0 %reduce-scatter.16.cloned.1.call-done = f32[256,1024]{1,0:T(8,128)} async-done(((f32[1024,1024]{1,0:T(8,128)}), f32[256,1024]{1,0:T(8,128)}) %reduce-scatter.16.cloned.1.call-update) | async-done | bytes 1048592 | tf_op jit(solution)/shard_map/reduce_scatter | solution.py:272
  1065.7 31.2 %reduce-scatter.14.cloned.1.call-done = bf16[256,1024]{1,0:T(8,128)(2,1)} async-done(((bf16[1024,1024]{1,0:T(8,128)(2,1)}), bf16[256,1024]{1,0:T(8,128)(2,1)}) %reduce-scatter.14.cloned.1.call-update) | async-done | bytes 524304 | tf_op jit(solution)/shard_map/reduce_scatter | solution.py:258
  1125.5 761.0 %conditional.3 = (f32[2,1024,128]{2,1,0:T(8,128)}, f32[2,1024,128]{2,1,0:T(8,128)}, f32[2,2,512,128]{3,2,1,0:T(8,128)}) conditional(s32[]{:T(128)} %bitcast.8, (s32[2]{0:T(128)S(1)}, bf16[2,1024,128]{2,1,0:T(8,128)(2,1)S(1)}, bf16[2,1024,128]{2,1,0:T(8,128)(2,1)S(1)}, f32[2,1024,1]{1,0,2:T(2,128)}, bf16[2,1024,128]{2,1,0:T(8,128)(2,1)S(1)}, ...), branch_computations={%region_19.23_spmd, %region_23.0_spmd} | conditional | flops 7895907840 | bytes 320074496 | solution.py:306
  1125.6 752.3 %while.53 = (s32[]{:T(128)}, f32[2,1024,128]{2,1,0:T(8,128)}, f32[2,1024,128]{2,1,0:T(8,128)}, f32[2,2,512,128]{3,2,1,0:T(8,128)}, s32[2]{0:T(128)S(1)}, /*index...) while((s32[]{:T(128)}, f32[2,1024,128]{2,1,0:T(8,128)}, ...), condition=%wide.region_28.28_spmd.clone, body=%wide.region_24.27_spmd.clone.sunk | while | flops 7895907840 | bytes 320074304 | solution.py:288
  1133.0 276.7 %scatter_custom_fusion.10 = pred[4194304]{0:T(1024)(128)(4,1)} fusion(s32[65536]{0:T(1024)S(1)} %select_bitcast_fusion.4, pred[65536]{0:T(1024)(128)(4,1)S(1)} %broadcast.447, pred[]{:T(512)} %constant.86.clone.2..sunk), kind=kCustom, calls=%fused_computation.89.clone.1 | custom fusion | bytes 4194305 | tf_op jit(solution)/shard_map/cond/branch_1_fun/while
  1441.4 27.3 %multiply_reduce_fusion.16 = (f32[2,512]{1,0:T(2,128)S(1)}, f32[2,512,8192]{2,1,0:T(8,128)}) fusion(f32[2,512,8192]{2,1,0:T(8,128)} %fusion.252, f32[2,512]{1,0:T(2,128)S(1)} %dynamic-slice_bitcast_fusion.4, pred[512,8192]{1,0:T(8,128)(4,1)} %reshape.360, bf16[2,8192,128]{2,1,0:T(8,128)(2,1)} %get-tuple-element.845, ...), kind=kOutput, calls=%fused_computation.85.clone.1 | convolution fusion | flops 2189425664 | bytes 75767808 | tf_op jit(solution)/shard_map/cond/branch_1_fun/while/body/eval_jaxpr/uik,uwk->uiw/dot_general | solution.py:142
  1468.7 26.6 %fusion.256 = f32[2,512,128]{2,1,0:T(8,128)} fusion(bf16[2,8192,128]{2,1,0:T(8,128)(2,1)} %get-tuple-element.844, f32[2,512,8192]{2,1,0:T(8,128)} %get-tuple-element.755, f32[2,512,8192]{2,1,0:T(8,128)} %fusion.252, f32[2,512]{1,0:T(2,128)S(1)} %add.415, f32[2,512]{1,0:T(2,128)S(1)} %dynamic-slice_bitcast_fusion.4, pred[512,8192]{1,0:T(8,128)(4,1)} %reshape.360), kind=kOutput, calls=%fused_computation.87.clone.1 | convolution fusion | flops 2197815296 | bytes 76029952 | tf_op jit(solution)/shard_map/cond/branch_1_fun/while/body/eval_jaxpr/xuj,xjg->xug/dot_general | solution.py:150
  1508.2 276.7 %scatter_custom_fusion.10 = pred[4194304]{0:T(1024)(128)(4,1)} fusion(s32[65536]{0:T(1024)S(1)} %select_bitcast_fusion.4, pred[65536]{0:T(1024)(128)(4,1)S(1)} %broadcast.447, pred[]{:T(512)} %constant.86.clone.2..sunk), kind=kCustom, calls=%fused_computation.89.clone.1 | custom fusion | bytes 4194305 | tf_op jit(solution)/shard_map/cond/branch_1_fun/while
  1816.6 27.3 %multiply_reduce_fusion.16 = (f32[2,512]{1,0:T(2,128)S(1)}, f32[2,512,8192]{2,1,0:T(8,128)}) fusion(f32[2,512,8192]{2,1,0:T(8,128)} %fusion.252, f32[2,512]{1,0:T(2,128)S(1)} %dynamic-slice_bitcast_fusion.4, pred[512,8192]{1,0:T(8,128)(4,1)} %reshape.360, bf16[2,8192,128]{2,1,0:T(8,128)(2,1)} %get-tuple-element.845, ...), kind=kOutput, calls=%fused_computation.85.clone.1 | convolution fusion | flops 2189425664 | bytes 75767808 | tf_op jit(solution)/shard_map/cond/branch_1_fun/while/body/eval_jaxpr/uik,uwk->uiw/dot_general | solution.py:142
  1843.9 26.6 %fusion.256 = f32[2,512,128]{2,1,0:T(8,128)} fusion(bf16[2,8192,128]{2,1,0:T(8,128)(2,1)} %get-tuple-element.844, f32[2,512,8192]{2,1,0:T(8,128)} %get-tuple-element.755, f32[2,512,8192]{2,1,0:T(8,128)} %fusion.252, f32[2,512]{1,0:T(2,128)S(1)} %add.415, f32[2,512]{1,0:T(2,128)S(1)} %dynamic-slice_bitcast_fusion.4, pred[512,8192]{1,0:T(8,128)(4,1)} %reshape.360), kind=kOutput, calls=%fused_computation.87.clone.1 | convolution fusion | flops 2197815296 | bytes 76029952 | tf_op jit(solution)/shard_map/cond/branch_1_fun/while/body/eval_jaxpr/xuj,xjg->xug/dot_general | solution.py:150
  1961.6 43.7 %reduce-scatter.32.cloned.1.call-done = f32[704,128]{1,0:T(8,128)} async-done(((f32[704,1024]{1,0:T(8,128)}), f32[704,128]{1,0:T(8,128)}) %reduce-scatter.32.cloned.1.call-update) | async-done | bytes 360464 | tf_op jit(solution)/shard_map/reduce_scatter | solution.py:350
  2005.3 76.3 %reduce-scatter.30.cloned.1.call-done = f32[128,704]{0,1:T(8,128)} async-done(((f32[1024,704]{0,1:T(8,128)}), f32[128,704]{0,1:T(8,128)}) %reduce-scatter.30.cloned.1.call-update) | async-done | bytes 360464 | tf_op jit(solution)/shard_map/reduce_scatter | solution.py:349
  2081.6 76.5 %reduce-scatter.28.cloned.1.call-done = f32[128,704]{0,1:T(8,128)} async-done(((f32[1024,704]{0,1:T(8,128)}), f32[128,704]{0,1:T(8,128)}) %reduce-scatter.28.cloned.1.call-update) | async-done | bytes 360464 | tf_op jit(solution)/shard_map/reduce_scatter | solution.py:348
  2158.1 67.7 %reduce-scatter.26.cloned.1.call-done = f32[256,128]{1,0:T(8,128)} async-done(((f32[256,1024]{1,0:T(8,128)}), f32[256,128]{1,0:T(8,128)}) %reduce-scatter.26.cloned.1.call-update) | async-done | bytes 131088 | tf_op jit(solution)/shard_map/reduce_scatter | solution.py:347
  2225.8 67.1 %reduce-scatter.24.cloned.1.call-done = f32[128,256]{1,0:T(8,128)} async-done(((f32[1024,256]{1,0:T(8,128)}), f32[128,256]{1,0:T(8,128)}) %reduce-scatter.24.cloned.1.call-update) | async-done | bytes 131088 | tf_op jit(solution)/shard_map/reduce_scatter | solution.py:346
  2292.9 67.0 %reduce-scatter.22.cloned.1.call-done = f32[128,256]{1,0:T(8,128)} async-done(((f32[1024,256]{1,0:T(8,128)}), f32[128,256]{1,0:T(8,128)}) %reduce-scatter.22.cloned.1.call-update) | async-done | bytes 131088 | tf_op jit(solution)/shard_map/reduce_scatter | solution.py:345
  2359.9 67.1 %reduce-scatter.20.cloned.1.call-done = f32[128,256]{1,0:T(8,128)} async-done(((f32[1024,256]{1,0:T(8,128)}), f32[128,256]{1,0:T(8,128)}) %reduce-scatter.20.cloned.1.call-update) | async-done | bytes 131088 | tf_op jit(solution)/shard_map/reduce_scatter | solution.py:344
  (301 shorter events, 466.3 us)
Async XLA Ops:
  7.2 1001.2 %copy-start = (bf16[704,1024]{1,0:T(8,128)(2,1)S(1)}, bf16[704,1024]{1,0:T(8,128)(2,1)}, u32[]{:S(2)}) copy-start(bf16[704,1024]{1,0:T(8,128)(2,1)} %param.35) | copy-start | bytes 4325380
  7.2 969.0 %reduce-scatter.12.cloned.1.call-start = ((), (), s32[]{:S(2)}) async-start(), calls=%async_computation.11 | async-start | bytes 5242880 | tf_op jit(solution)/shard_map/reduce_scatter | solution.py:248
  7.2 49.8 %collective-permute-start.2 = (bf16[2,4096,128]{2,1,0:T(8,128)(2,1)}, bf16[2,4096,128]{2,1,0:T(8,128)(2,1)}, u32[]{:S(2)}, u32[]{:S(2)}) collective-permute-start(bf16[2,4096,128]{2,1,0:T(8,128)(2,1)} %bitcast.227), channel_id=1, source_target_pairs={{0,4},{4,0},{8,12},{12,8},{16,20},{20,16},{24,28},{28,24},{1,5},{5... | collective-permute-start | bytes 6291464 | tf_op jit(solution)/shard_map/ppermute | solution.py:11
  10.3 94.1 %collective-permute-start.1 = (bf16[2,4096,128]{2,1,0:T(8,128)(2,1)}, bf16[2,4096,128]{2,1,0:T(8,128)(2,1)}, u32[]{:S(2)}, u32[]{:S(2)}) collective-permute-start(bf16[2,4096,128]{2,1,0:T(8,128)(2,1)} %bitcast.228), channel_id=1, source_target_pairs={{0,8},{4,12},{8,0},{12,4},{16,24},{20,28},{24,16},{28,20},{1,9},{5... | collective-permute-start | bytes 6291464 | tf_op jit(solution)/shard_map/ppermute | solution.py:11
  11.8 94.4 %collective-permute-start = (bf16[2,4096,128]{2,1,0:T(8,128)(2,1)}, bf16[2,4096,128]{2,1,0:T(8,128)(2,1)}, u32[]{:S(2)}, u32[]{:S(2)}) collective-permute-start(bf16[2,4096,128]{2,1,0:T(8,128)(2,1)} %bitcast.229), channel_id=1, source_target_pairs={{0,16},{4,20},{8,24},{12,28},{16,0},{20,4},{24,8},{28,12},{1,17},{... | collective-permute-start | bytes 6291464 | tf_op jit(solution)/shard_map/ppermute | solution.py:11
  14.4 95.9 %collective-permute-start.5 = (bf16[2,4096,128]{2,1,0:T(8,128)(2,1)}, bf16[2,4096,128]{2,1,0:T(8,128)(2,1)}, u32[]{:S(2)}, u32[]{:S(2)}) collective-permute-start(bf16[2,4096,128]{2,1,0:T(8,128)(2,1)} %bitcast.231), channel_id=1, source_target_pairs={{0,4},{4,0},{8,12},{12,8},{16,20},{20,16},{24,28},{28,24},{1,5},{5... | collective-permute-start | bytes 6291464 | tf_op jit(solution)/shard_map/ppermute | solution.py:11
  15.0 177.4 %collective-permute-start.4 = (bf16[2,4096,128]{2,1,0:T(8,128)(2,1)}, bf16[2,4096,128]{2,1,0:T(8,128)(2,1)}, u32[]{:S(2)}, u32[]{:S(2)}) collective-permute-start(bf16[2,4096,128]{2,1,0:T(8,128)(2,1)} %bitcast.232), channel_id=1, source_target_pairs={{0,8},{4,12},{8,0},{12,4},{16,24},{20,28},{24,16},{28,20},{1,9},{5... | collective-permute-start | bytes 6291464 | tf_op jit(solution)/shard_map/ppermute | solution.py:11
  57.1 137.6 %collective-permute-start.3 = (bf16[2,4096,128]{2,1,0:T(8,128)(2,1)S(1)}, bf16[2,4096,128]{2,1,0:T(8,128)(2,1)S(1)}, u32[]{:S(2)}, u32[]{:S(2)}) collective-permute-start(bf16[2,4096,128]{2,1,0:T(8,128)(2,1)S(1)} %bitcast.233), channel_id=1, source_target_pairs={{0,16},{4,20},{8,24},{12,28},{16,0},{20,4},{24,8},{28,12},{1,17},{... | collective-permute-start | bytes 6291464 | tf_op jit(solution)/shard_map/ppermute | solution.py:11
  932.4 70.4 %all-gather.3.cloned.1.call-start = ((), (), s32[]{:S(2)}) async-start(), calls=%async_computation.12 | async-start | bytes 2621440 | tf_op jit(solution)/shard_map/all_gather | solution.py:251
  980.0 83.3 %reduce-scatter.16.cloned.1.call-start = ((), (), s32[]{:S(2)}) async-start(), calls=%async_computation.14 | async-start | bytes 5242880 | tf_op jit(solution)/shard_map/reduce_scatter | solution.py:272
  1018.6 78.3 %reduce-scatter.14.cloned.1.call-start = ((), (), s32[]{:S(2)}) async-start(), calls=%async_computation.13 | async-start | bytes 2621440 | tf_op jit(solution)/shard_map/reduce_scatter | solution.py:258
  1023.3 99.6 %copy-start.35 = (bf16[256,1024]{1,0:T(8,128)(2,1)S(1)}, bf16[256,1024]{1,0:T(8,128)(2,1)}, u32[]{:S(2)}) copy-start(bf16[256,1024]{1,0:T(8,128)(2,1)} %param.32) | copy-start | bytes 1572868
  1023.3 99.6 %all-gather.5.cloned.1.call-start = ((), (), s32[]{:S(2)}) async-start(), calls=%async_computation.15 | async-start | bytes 2621440 | tf_op jit(solution)/shard_map/all_gather | solution.py:277
  1100.2 828.0 %reduce-scatter.18.cloned.1.call-start = ((), (), s32[]{:S(2)}) async-start(), calls=%async_computation.16 | async-start | bytes 2621440 | tf_op jit(solution)/shard_map/reduce_scatter | solution.py:333
  1125.9 315.5 %copy-start.10 = (bf16[2,1024,128]{2,1,0:T(8,128)(2,1)}, bf16[2,1024,128]{2,1,0:T(8,128)(2,1)S(1)}, u32[]{:S(2)}) copy-start(bf16[2,1024,128]{2,1,0:T(8,128)(2,1)S(1)} %get-tuple-element.841) | copy-start | bytes 1572868 | tf_op jit(solution)/shard_map/cond/branch_1_fun/while
  1501.1 315.5 %copy-start.10 = (bf16[2,1024,128]{2,1,0:T(8,128)(2,1)}, bf16[2,1024,128]{2,1,0:T(8,128)(2,1)S(1)}, u32[]{:S(2)}) copy-start(bf16[2,1024,128]{2,1,0:T(8,128)(2,1)S(1)} %get-tuple-element.841) | copy-start | bytes 1572868 | tf_op jit(solution)/shard_map/cond/branch_1_fun/while
  1896.9 108.4 %reduce-scatter.32.cloned.1.call-start = ((), (), s32[]{:S(2)}) async-start(), calls=%async_computation.23 | async-start | bytes 3244032 | tf_op jit(solution)/shard_map/reduce_scatter | solution.py:350
  1902.4 179.2 %reduce-scatter.30.cloned.1.call-start = ((), (), s32[]{:S(2)}) async-start(), calls=%async_computation.22 | async-start | bytes 3244032 | tf_op jit(solution)/shard_map/reduce_scatter | solution.py:349
  1907.1 251.0 %reduce-scatter.28.cloned.1.call-start = ((), (), s32[]{:S(2)}) async-start(), calls=%async_computation.21 | async-start | bytes 3244032 | tf_op jit(solution)/shard_map/reduce_scatter | solution.py:348
  1911.9 313.9 %reduce-scatter.26.cloned.1.call-start = ((), (), s32[]{:S(2)}) async-start(), calls=%async_computation.20 | async-start | bytes 1179648 | tf_op jit(solution)/shard_map/reduce_scatter | solution.py:347
  1915.4 377.5 %reduce-scatter.24.cloned.1.call-start = ((), (), s32[]{:S(2)}) async-start(), calls=%async_computation.19 | async-start | bytes 1179648 | tf_op jit(solution)/shard_map/reduce_scatter | solution.py:346
  1917.3 442.6 %reduce-scatter.22.cloned.1.call-start = ((), (), s32[]{:S(2)}) async-start(), calls=%async_computation.18 | async-start | bytes 1179648 | tf_op jit(solution)/shard_map/reduce_scatter | solution.py:345
  1919.1 507.9 %reduce-scatter.20.cloned.1.call-start = ((), (), s32[]{:S(2)}) async-start(), calls=%async_computation.17 | async-start | bytes 1179648 | tf_op jit(solution)/shard_map/reduce_scatter | solution.py:344
  1919.2 507.8 %copy-start.1 = (bf16[704,1024]{1,0:T(8,128)(2,1)S(1)}, bf16[704,1024]{1,0:T(8,128)(2,1)}, u32[]{:S(2)}) copy-start(bf16[704,1024]{1,0:T(8,128)(2,1)} %param.35) | copy-start | bytes 4325380
  (53 other events, 477.5 us)
Sparse Core Ops, SparseCore 0:
  932.5 43.6 reduce-scatter.11
  980.1 22.5 all-gather.2
  1018.7 44.5 reduce-scatter.15
  1065.7 31.1 reduce-scatter.13
  1100.3 22.5 all-gather.4
  1897.0 31.1 reduce-scatter.17
  1932.3 72.9 reduce-scatter.31
  2009.4 72.1 reduce-scatter.29
  2085.7 72.2 reduce-scatter.27
  2161.9 63.8 reduce-scatter.25
  2229.8 63.0 reduce-scatter.23
  2296.7 63.1 reduce-scatter.21
  2363.9 63.0 reduce-scatter.19
where the time goes:
time: 2440 us; the launch traced here: 2430 us
  local copies, waits for them, and re-layouts  1180 us (48%)
  waiting for transfers between devices  768 us (31%)
  matrix products  297 us (12%)
  other arithmetic  94.6 us (4%)
  loops' own time  33.8 us (1%)
  blocking collectives  28.7 us (1%)
    while x56, local copies, waits for them, and re-layouts  1110 us
    ppermute x6, waiting for transfers between devices, from_partner(): lax.ppermute(array, axis, [(i, i ^ 1 << bit) for i in range(lax.axis_size...  142 us
    reduce_scatter x1, waiting for transfers between devices, per_device(): lax.psum_scatter(grad_w_gate, 'dp', scatter_dimension=0, tiled=True)  76.5 us
    reduce_scatter x1, waiting for transfers between devices, per_device(): lax.psum_scatter(grad_w_up, 'dp', scatter_dimension=0, tiled=True)  76.3 us
    reduce_scatter x1, waiting for transfers between devices, per_device(): lax.psum_scatter(grad_w_output, 'dp', scatter_dimension=1, tiled=True)  67.7 us
    reduce_scatter x1, waiting for transfers between devices, per_device(): lax.psum_scatter(grad_w_value, 'dp', scatter_dimension=0, tiled=True)  67.1 us
    reduce_scatter x1, waiting for transfers between devices, per_device(): lax.psum_scatter(grad_w_query, 'dp', scatter_dimension=0, tiled=True)  67.1 us
    reduce_scatter x1, waiting for transfers between devices, per_device(): lax.psum_scatter(grad_w_key, 'dp', scatter_dimension=0, tiled=True)  67 us
  transfers between devices with their start and end apart: 19, of which 18 were waited for; matrix products, arithmetic and copies ran while one was open for 3% of the time, Pallas kernels for 0%

commit v1 on v0

v1 whole, which is shorter than its diff:
```python
import functools

import jax
import jax.numpy as jnp
import numpy as np
from jax import lax
from jax.experimental import pallas as pl
from jax.experimental.pallas import tpu as pltpu
from jax.sharding import PartitionSpec as P

epsilon = 1e-05
negative_big = -1e30
F = jnp.float32
B = jnp.bfloat16
GROUP_BLOCK = 16


def dot(a, b, da, db):
    return lax.dot_general(a, b, (((da,), (db,)), ((), ())), preferred_element_type=F)


def swap(array, axis, bit):
    return lax.ppermute(array, axis, [(i, i ^ bit) for i in range(lax.axis_size(axis))])


def axis_bits(axis):
    return lax.axis_size(axis).bit_length() - 1


def pick(block_scores, offsets, heads, spread, gb):
    picked = [s[:gb] for s in block_scores]
    for t in range(1, spread):
        here = offsets == float(t)
        for h in range(heads):
            picked[h] = jnp.where(here, block_scores[h][t * gb : (t + 1) * gb], picked[h])
    return picked


def expand(picked, offsets, spread):
    zero = jnp.zeros_like(picked)
    return jnp.concatenate(
        [jnp.where(offsets == jnp.asarray(t, B), picked, zero) for t in range(spread)], axis=0
    )


def spread_dot(rows_ref, h, picked, offsets, spread, gb):
    rows = gb * spread
    total = None
    for b in range(offsets.shape[0] // gb):
        wide = expand(picked[b * gb : (b + 1) * gb], offsets[b * gb : (b + 1) * gb], spread)
        part = dot(rows_ref[h, b * rows : (b + 1) * rows, :], wide, 0, 0)
        total = part if total is None else total + part
    return total


def memory_forward_body(
    flag_ref, q_ref, off_ref, k_ref, v_ref, o_ref, lse_ref, sel_ref, *, heads, hd, spread, gb
):
    scale = hd**-0.5
    groups = off_ref.shape[0]
    rows = gb * spread

    @pl.when(flag_ref[0] > 0)
    def _():
        offs = off_ref[...]
        wide_offs = offs.astype(F)
        for b in range(groups // gb):
            scores = [
                dot(
                    k_ref[h, b * rows : (b + 1) * rows, :],
                    q_ref[:, h * hd : (h + 1) * hd],
                    1,
                    1,
                )
                for h in range(heads)
            ]
            picked = pick(scores, wide_offs[b * gb : (b + 1) * gb], heads, spread, gb)
            for h in range(heads):
                sel_ref[h, b * gb : (b + 1) * gb, :] = picked[h] * scale
        for h in range(heads):
            x = sel_ref[h]
            peak = jnp.max(x, axis=0, keepdims=True)
            p = jnp.exp(x - peak)
            total = jnp.sum(p, axis=0, keepdims=True)
            lse_ref[h : h + 1, :] = peak + jnp.log(total)
            out = spread_dot(v_ref, h, p.astype(B), offs, spread, gb)
            o_ref[:, h * hd : (h + 1) * hd] = (out / total).T.astype(B)

    @pl.when(flag_ref[0] <= 0)
    def _():
        o_ref[...] = jnp.zeros_like(o_ref)
        lse_ref[...] = jnp.full_like(lse_ref, negative_big)
        sel_ref[...] = jnp.full_like(sel_ref, negative_big)


def memory_backward_body(
    flag_ref, g_ref, st_ref, sel_ref, off_ref, k_ref, v_ref, dq_ref, *, heads, hd, spread, gb
):
    scale = hd**-0.5
    groups = off_ref.shape[0]
    rows = gb * spread

    @pl.when(flag_ref[0] > 0)
    def _():
        offs = off_ref[...]
        wide_offs = offs.astype(F)
        grads = [[] for _ in range(heads)]
        for b in range(groups // gb):
            dprobs = [
                dot(
                    v_ref[h, b * rows : (b + 1) * rows, :],
                    g_ref[:, h * hd : (h + 1) * hd],
                    1,
                    1,
                )
                for h in range(heads)
            ]
            picked = pick(dprobs, wide_offs[b * gb : (b + 1) * gb], heads, spread, gb)
            for h in range(heads):
                p = jnp.exp(sel_ref[h, b * gb : (b + 1) * gb, :] - st_ref[h : h + 1, :])
                delta = st_ref[heads + h : heads + h + 1, :]
                grads[h].append((p * (picked[h] - delta)).astype(B))
        for h in range(heads):
            out = spread_dot(k_ref, h, jnp.concatenate(grads[h], axis=0), offs, spread, gb)
            dq_ref[:, h * hd : (h + 1) * hd] = (out * scale).T.astype(dq_ref.dtype)

    @pl.when(flag_ref[0] <= 0)
    def _():
        dq_ref[...] = jnp.zeros_like(dq_ref)


def row_block(length):
    return min(512, length)


def memory_forward(flag, q, off, k, v, spread):
    length = q.shape[0]
    heads, rows, hd = k.shape
    groups = off.shape[0]
    tq = row_block(length)
    return pl.pallas_call(
        functools.partial(memory_forward_body, heads=heads, hd=hd, spread=spread, gb=GROUP_BLOCK),
        grid=(length // tq,),
        in_specs=[
            pl.BlockSpec(memory_space=pltpu.SMEM),
            pl.BlockSpec((tq, heads * hd), lambda i: (i, 0)),
            pl.BlockSpec((groups, tq), lambda i: (0, i)),
            pl.BlockSpec((heads, rows, hd), lambda i: (0, 0, 0)),
            pl.BlockSpec((heads, rows, hd), lambda i: (0, 0, 0)),
        ],
        out_specs=[
            pl.BlockSpec((tq, heads * hd), lambda i: (i, 0)),
            pl.BlockSpec((heads, tq), lambda i: (0, i)),
            pl.BlockSpec((heads, groups, tq), lambda i: (0, 0, i)),
        ],
        out_shape=[
            jax.ShapeDtypeStruct((length, heads * hd), B),
            jax.ShapeDtypeStruct((heads, length), F),
            jax.ShapeDtypeStruct((heads, groups, length), F),
        ],
        cost_estimate=pl.CostEstimate(
            flops=8 * length * heads * rows * hd,
            transcendentals=0,
            bytes_accessed=4 * heads * rows * hd,
        ),
        name="memory_forward",
    )(flag, q, off, k, v)


def memory_backward(flag, g, stats, sel, off, k, v, spread, dtype):
    length = g.shape[0]
    heads, rows, hd = k.shape
    groups = off.shape[0]
    tq = row_block(length)
    return pl.pallas_call(
        functools.partial(memory_backward_body, heads=heads, hd=hd, spread=spread, gb=GROUP_BLOCK),
        grid=(length // tq,),
        in_specs=[
            pl.BlockSpec(memory_space=pltpu.SMEM),
            pl.BlockSpec((tq, heads * hd), lambda i: (i, 0)),
            pl.BlockSpec((2 * heads, tq), lambda i: (0, i)),
            pl.BlockSpec((heads, groups, tq), lambda i: (0, 0, i)),
            pl.BlockSpec((groups, tq), lambda i: (0, i)),
            pl.BlockSpec((heads, rows, hd), lambda i: (0, 0, 0)),
            pl.BlockSpec((heads, rows, hd), lambda i: (0, 0, 0)),
        ],
        out_specs=pl.BlockSpec((tq, heads * hd), lambda i: (i, 0)),
        out_shape=jax.ShapeDtypeStruct((length, heads * hd), dtype),
        cost_estimate=pl.CostEstimate(
            flops=8 * length * heads * rows * hd,
            transcendentals=0,
            bytes_accessed=4 * heads * rows * hd,
        ),
        name="memory_backward",
    )(flag, g, stats, sel, off, k, v)


def causal_scores(k, q, w, scale):
    s = dot(k, q, 1, 1) * scale
    n = k.shape[0]
    key = lax.broadcasted_iota(jnp.int32, (w, w), 0)
    query = lax.broadcasted_iota(jnp.int32, (w, w), 1)
    diagonal = jnp.where(key <= query, s[n - w :], negative_big)
    return diagonal if n == w else jnp.concatenate([s[: n - w], diagonal], axis=0)


def local_forward_body(q_ref, k_ref, v_ref, o_ref, lse_ref, *, heads, hd, w):
    scale = hd**-0.5
    for h in range(heads):
        c = slice(h * hd, (h + 1) * hd)
        for i in range(q_ref.shape[0] // w):
            n = (i + 1) * w
            r = slice(i * w, n)
            s = causal_scores(k_ref[:n, c], q_ref[r, c], w, scale)
            peak = jnp.max(s, axis=0, keepdims=True)
            p = jnp.exp(s - peak)
            total = jnp.sum(p, axis=0, keepdims=True)
            lse_ref[h : h + 1, r] = peak + jnp.log(total)
            out = dot(v_ref[:n, c], p.astype(B), 0, 0)
            o_ref[r, c] = (out / total).T.astype(B)


def local_forward(q, k, v, heads):
    length, columns = q.shape
    return pl.pallas_call(
        functools.partial(
            local_forward_body, heads=heads, hd=columns // heads, w=min(256, length)
        ),
        out_shape=[
            jax.ShapeDtypeStruct((length, columns), B),
            jax.ShapeDtypeStruct((heads, length), F),
        ],
        name="local_forward",
    )(q, k, v)


def local_backward_body(
    q_ref, k_ref, v_ref, g_ref, st_ref, dq_ref, dk_ref, dv_ref, *, heads, hd, w
):
    scale = hd**-0.5
    for h in range(heads):
        c = slice(h * hd, (h + 1) * hd)
        count = q_ref.shape[0] // w
        for i in reversed(range(count)):
            n = (i + 1) * w
            r = slice(i * w, n)
            s = causal_scores(k_ref[:n, c], q_ref[r, c], w, scale)
            p = jnp.exp(s - st_ref[h : h + 1, r])
            dp = dot(v_ref[:n, c], g_ref[r, c], 1, 1)
            ds = (p * (dp - st_ref[heads + h : heads + h + 1, r])).astype(B)
            dq_ref[r, c] = (dot(k_ref[:n, c], ds, 0, 0) * scale).T
            dk = dot(ds, q_ref[r, c], 1, 0) * scale
            dv = dot(p.astype(B), g_ref[r, c], 1, 0)
            if i == count - 1:
                dk_ref[:n, c] = dk
                dv_ref[:n, c] = dv
            else:
                dk_ref[:n, c] += dk
                dv_ref[:n, c] += dv


def local_backward(q, k, v, g, stats, heads):
    length, columns = q.shape
    return pl.pallas_call(
        functools.partial(
            local_backward_body, heads=heads, hd=columns // heads, w=min(256, length)
        ),
        out_shape=[jax.ShapeDtypeStruct((length, columns), F)] * 3,
        name="local_backward",
    )(q, k, v, g, stats)


def norm_forward(values, gain):
    factor = lax.rsqrt(jnp.mean(values * values, axis=-1, keepdims=True) + epsilon)
    return (values * factor * gain, factor)


def norm_backward(values, factor, gain, grad_normed):
    scaled = gain * grad_normed
    return factor * scaled - values * (factor * factor * factor) * jnp.mean(
        values * scaled, axis=-1, keepdims=True
    )


def rotate_tables(length, hd, heads):
    half = hd // 2
    position = np.arange(length, dtype=np.float32)
    inverse = np.exp(
        -np.log(np.float32(10000.0)) * np.arange(half, dtype=np.float32) * np.float32(2.0) / hd
    ).astype(np.float32)
    angles = position[:, None] * inverse[None, :]
    cos = np.cos(angles)
    sin = np.sin(angles)
    return (
        jnp.asarray(np.concatenate([cos, cos], axis=1)[:, None, :]),
        jnp.asarray(np.concatenate([-sin, sin], axis=1)[:, None, :]),
    )


def rotate(values, heads, tables, direction):
    length, columns = values.shape
    hd = columns // heads
    x = values.reshape(length, heads, hd)
    flipped = jnp.concatenate([x[..., hd // 2 :], x[..., : hd // 2]], axis=-1)
    return (x * tables[0] + direction * flipped * tables[1]).reshape(length, columns).astype(B)


def to_partner(arrays, chosen):
    got = [[swap(a, "dp", 1 << b) for a in arrays] for b in reversed(range(len(chosen)))]
    got.reverse()
    out = []
    for j in range(len(arrays)):
        value = got[0][j]
        for b in range(1, len(chosen)):
            value = jnp.where(chosen[b], got[b][j], value)
        out.append(value)
    return out


def gather_tensor(value):
    pieces, offsets = [value], [0]
    for b in reversed(range(axis_bits("tensor"))):
        pieces = pieces + [swap(p, "tensor", 1 << b) for p in pieces]
        offsets = offsets + [k ^ (1 << b) for k in offsets]
    return pieces, offsets


def in_order(pieces, offsets, me):
    share = pieces[0].shape[0]
    out = jnp.zeros((len(pieces) * share,) + pieces[0].shape[1:], pieces[0].dtype)
    for piece, k in zip(pieces, offsets):
        out = lax.dynamic_update_slice_in_dim(out, piece, (me ^ k) * share, 0)
    return out


def scatter_sum(value, axis, bit_order):
    me = lax.axis_index(axis)
    bits = axis_bits(axis)
    tail = value.shape[1:]
    value = value.reshape((2,) * bits + tail)
    alive = list(reversed(range(bits)))
    for b in bit_order:
        where = alive.index(b)
        mine = (me >> b) & 1
        keep = lax.dynamic_index_in_dim(value, mine, where, keepdims=False)
        send = lax.dynamic_index_in_dim(value, 1 - mine, where, keepdims=False)
        value = keep.astype(F) + swap(send.astype(B), axis, 1 << b).astype(F)
        alive.pop(where)
    return value


def per_device(
    tokens,
    w_query,
    w_key,
    w_value,
    w_output,
    w_gate,
    w_up,
    w_down,
    gain_attn,
    gain_mlp,
    cache_keys,
    cache_values,
    knn_index,
    memory_flag,
    pairing,
    cotangent,
):
    length, width = tokens.shape
    parts = lax.axis_size("tensor")
    docs = lax.axis_size("dp")
    share = length // parts
    me = lax.axis_index("tensor")
    row_offset = me * share
    heads = cache_keys.shape[1]
    rows = cache_keys.shape[2]
    hd = cache_keys.shape[3]
    columns = heads * hd
    topk = knn_index.shape[1]
    groups = topk // 2
    spread = rows // groups
    flag = memory_flag[:1].astype(jnp.int32)
    difference = jnp.bitwise_xor(pairing[0], lax.axis_index("dp"))
    chosen = [difference == (1 << b) for b in range(axis_bits("dp"))]
    dp_order = list(range(axis_bits("dp")))
    tensor_order = list(range(axis_bits("tensor")))

    offsets = (knn_index - jnp.arange(topk, dtype=jnp.int32)[None, :] * spread).T.astype(B)
    own_off = offsets[:groups]
    far_off = jnp.where(flag[0] > 0, offsets[groups:], jnp.asarray(-1, B))
    (their_off,) = to_partner([far_off], chosen)
    their_flag = (their_off[0, :1].astype(F) >= 0).astype(jnp.int32)
    out_weights, weight_offsets = gather_tensor(w_output)

    def ordered_rows(cache):
        return (
            cache.reshape(heads, groups // GROUP_BLOCK, GROUP_BLOCK, spread, hd)
            .transpose(0, 1, 3, 2, 4)
            .reshape(heads, rows, hd)
        )

    tokens_full = tokens.astype(F)
    normed_attn, factor_attn = norm_forward(tokens_full, gain_attn)
    normed_low = normed_attn.astype(B)
    tables = rotate_tables(length, hd, heads)
    queries = rotate(dot(normed_low, w_query, 1, 0), heads, tables, 1.0)
    (their_queries,) = to_partner([queries], chosen)
    keys = rotate(dot(normed_low, w_key, 1, 0), heads, tables, 1.0)
    values = dot(normed_low, w_value, 1, 0).astype(B)
    stored_keys = ordered_rows(cache_keys[0])
    stored_values = ordered_rows(cache_values[0])
    own_out, own_lse, own_sel = memory_forward(
        flag, queries, own_off, stored_keys, stored_values, spread
    )
    local_out, local_lse = local_forward(queries, keys, values, heads)
    their_out, their_lse, their_sel = memory_forward(
        their_flag, their_queries, their_off, stored_keys, stored_values, spread
    )
    far_out, far_lse = to_partner([their_out, their_lse], chosen)
    log_total = jnp.logaddexp(jnp.logaddexp(local_lse, own_lse), far_lse)

    def weighted(out, lse):
        weight = jnp.exp(lse - log_total).T
        return out.reshape(length, heads, hd).astype(F) * weight[:, :, None]

    attended = (
        weighted(local_out, local_lse) + weighted(own_out, own_lse) + weighted(far_out, far_lse)
    )
    attended_low = attended.reshape(length, columns).astype(B)

    pieces, _ = gather_tensor(attended_low)
    middle = tokens_full
    for piece, weight in zip(pieces, out_weights):
        middle = middle + dot(piece, weight, 1, 0)
    normed, factor = norm_forward(middle, gain_mlp)
    normed_mlp = normed.astype(B)
    gate = dot(normed_mlp, w_gate, 1, 0)
    upper = dot(normed_mlp, w_up, 1, 0)
    sigmoid_gate = jax.nn.sigmoid(gate)
    silu_gate = gate * sigmoid_gate
    hidden = (silu_gate * upper).astype(B)
    grad_hidden = dot(cotangent, w_down, 1, 1)
    grad_gate = (grad_hidden * upper * sigmoid_gate * (1.0 + gate * (1.0 - sigmoid_gate))).astype(B)
    grad_upper = (grad_hidden * silu_gate).astype(B)
    grad_normed_part = dot(grad_gate, w_gate, 1, 1) + dot(grad_upper, w_up, 1, 1)
    middle_rows = lax.dynamic_slice_in_dim(middle, row_offset, share, 0)
    factor_rows = lax.dynamic_slice_in_dim(factor, row_offset, share, 0)
    grad_normed_rows = scatter_sum(
        grad_normed_part.reshape(parts, share, width), "tensor", tensor_order
    )
    grad_middle_rows = lax.dynamic_slice_in_dim(cotangent, row_offset, share, 0).astype(
        F
    ) + norm_backward(middle_rows, factor_rows, gain_mlp, grad_normed_rows)
    gain_mlp_part = jnp.sum(grad_normed_rows * middle_rows * factor_rows, axis=0)
    branch_pieces, branch_offsets = gather_tensor(grad_middle_rows.astype(B))
    grad_branch = in_order(branch_pieces, branch_offsets, me)

    grad_attended = dot(grad_branch, w_output, 1, 1).astype(B)
    delta = jnp.sum(
        (grad_attended.astype(F) * attended_low.astype(F)).reshape(length, heads, hd), axis=-1
    ).T
    stats = jnp.concatenate([log_total, delta], axis=0)
    their_grad, their_stats = to_partner([grad_attended, stats], chosen)
    local_dq, grad_keys, grad_values = local_backward(
        queries, keys, values, grad_attended, stats, heads
    )
    own_dq = memory_backward(
        flag, grad_attended, stats, own_sel, own_off, stored_keys, stored_values, spread, F
    )
    their_dq = memory_backward(
        their_flag, their_grad, their_stats, their_sel, their_off, stored_keys, stored_values,
        spread, B
    )
    (far_dq,) = to_partner([their_dq], chosen)

    mlp_grads = jnp.concatenate(
        [
            dot(normed_mlp, grad_gate, 0, 0),
            dot(normed_mlp, grad_upper, 0, 0),
            dot(cotangent, hidden, 0, 0),
            dot(grad_branch, attended_low, 0, 0),
        ],
        axis=1,
    )
    mlp_sum = scatter_sum(mlp_grads.reshape(docs, width // docs, -1), "dp", dp_order)
    ff = w_gate.shape[1]
    grad_w_gate = mlp_sum[:, :ff]
    grad_w_up = mlp_sum[:, ff : 2 * ff]
    grad_w_down = mlp_sum[:, 2 * ff : 3 * ff].T
    grad_w_output = mlp_sum[:, 3 * ff :].T

    down_part = dot(hidden, w_down, 1, 0).reshape(parts, share, width)
    output_rows = middle_rows + scatter_sum(down_part, "tensor", tensor_order)

    grad_key_low = rotate(grad_keys, heads, tables, -1.0)
    grad_value_low = grad_values.astype(B)
    grad_query_low = rotate(local_dq + own_dq + far_dq.astype(F), heads, tables, -1.0)
    grad_normed_attn = (
        dot(grad_key_low, w_key, 1, 1)
        + dot(grad_value_low, w_value, 1, 1)
        + dot(grad_query_low, w_query, 1, 1)
    )
    attn_grads = jnp.concatenate(
        [
            dot(normed_low, grad_query_low, 0, 0),
            dot(normed_low, grad_key_low, 0, 0),
            dot(normed_low, grad_value_low, 0, 0),
        ],
        axis=1,
    )
    attn_sum = scatter_sum(attn_grads.reshape(docs, width // docs, -1), "dp", dp_order)
    grad_attn_rows = scatter_sum(
        grad_normed_attn.reshape(parts, share, width), "tensor", tensor_order
    )
    tokens_rows = lax.dynamic_slice_in_dim(tokens, row_offset, share, 0).astype(F)
    factor_attn_rows = lax.dynamic_slice_in_dim(factor_attn, row_offset, share, 0)
    grad_tokens_rows = grad_middle_rows + norm_backward(
        tokens_rows, factor_attn_rows, gain_attn, grad_attn_rows
    )
    gain_attn_part = jnp.sum(grad_attn_rows * tokens_rows * factor_attn_rows, axis=0)
    gains = jnp.stack([gain_attn_part, gain_mlp_part], axis=0)
    for b in tensor_order:
        gains = gains + swap(gains, "tensor", 1 << b)
    gains = gains.reshape(2, docs, width // docs).transpose(1, 0, 2)
    gains = gain_scatter(gains, dp_order)
    return (
        output_rows.astype(B),
        grad_tokens_rows.astype(B),
        attn_sum[:, :columns],
        attn_sum[:, columns : 2 * columns],
        attn_sum[:, 2 * columns :],
        grad_w_output,
        grad_w_gate,
        grad_w_up,
        grad_w_down,
        gains[0],
        gains[1],
    )


def gain_scatter(gains, order):
    me = lax.axis_index("dp")
    total = gains
    for b in order:
        total = total + swap(total, "dp", 1 << b)
    return lax.dynamic_index_in_dim(total, me, 0, keepdims=False)


def solution(mesh):
    placed = (
        P("dp", None),
        P(None, "tensor"),
        P(None, "tensor"),
        P(None, "tensor"),
        P("tensor", None),
        P(None, "tensor"),
        P(None, "tensor"),
        P("tensor", None),
        P(),
        P(),
        P("dp", "tensor", None, None),
        P("dp", "tensor", None, None),
        P("dp", None),
        P("dp"),
        P("dp"),
        P("dp", None),
    )
    return jax.shard_map(
        per_device,
        mesh=mesh,
        in_specs=placed,
        out_specs=(
            P(("dp", "tensor"), None),
            P(("dp", "tensor"), None),
            P("dp", "tensor"),
            P("dp", "tensor"),
            P("dp", "tensor"),
            P("tensor", "dp"),
            P("dp", "tensor"),
            P("dp", "tensor"),
            P("tensor", "dp"),
            P("dp"),
            P("dp"),
        ),
        check_vma=False,
    )
```

time: 2440 us -> 540 us (0.22)
  local copies, waits for them, and re-layouts: 1180 us -> 158 us
  waiting for transfers between devices: 768 us -> 173 us
  matrix products: 297 us -> 48.6 us
  starting transfers between devices: 12 us -> 56.9 us
  other arithmetic: 94.6 us -> 50.4 us
  Pallas kernels: 0 us -> 41.2 us
  loops' own time: 33.8 us -> 0 us
  blocking collectives: 28.7 us -> 0 us
    while x56 -> x0, local copies, waits for them, and re-layouts: 1110 us -> none
    reduce_scatter x11 -> x0, waiting for transfers between devices: 580 us -> none  [the longest x1 76.5 us: per_device(): lax.psum_scatter(grad_w_gate, 'dp', scatter_dimension=0, tiled=True)]
    dot_general x45 -> x24, matrix products: 297 us -> 48.6 us  [dot(): lax.dot_general(a, b, (((da,), (db,)), ((), ())), preferred_element_type=F)]
    scatter x4 -> x0, local copies, waits for them, and re-layouts: 48.1 us -> none  [scores_for(): chosen = jnp.zeros((width, stored_keys.shape[1]), bool).at[jnp.arange(wid...]
    ppermute x6 -> x47, starting transfers between devices: 11.3 us -> 56.9 us  [swap(): lax.ppermute(array, axis, [(i, i ^ bit) for i in range(lax.axis_size(axis...]
    all_gather x2 -> x0, waiting for transfers between devices: 45.2 us -> none  [the longest x1 22.7 us: per_device(): lax.all_gather(normed_rows.astype(jnp.bfloat16), 'tensor', axis=0, tiled=...]
    dynamic_slice x4 -> x14, local copies, waits for them, and re-layouts: 2.51 us -> 47.3 us  [the longest x9 33 us: scatter_sum(): keep = lax.dynamic_index_in_dim(value, mine, where, keepdims=False)]
    pallas_call x0 -> x6, Pallas kernels: none -> 41.2 us  [the longest x2 14.1 us: memory_forward(): pl.pallas_call(functools.partial(memory_forward_body, heads=heads, hd=hd,...]
  transfers between devices with their start and end apart: 19 -> 47, of which waited for: 18 -> 14; matrix products, arithmetic and copies ran while one was open for 3% -> 34% of each run, Pallas kernels for 0% -> 7%
where the time goes in v1:
time: 540 us; the launch traced here: 532 us
  waiting for transfers between devices  173 us (32%)
  local copies, waits for them, and re-layouts  158 us (29%)
  starting transfers between devices  56.9 us (11%)
  other arithmetic  50.4 us (9%)
  matrix products  48.6 us (9%)
  Pallas kernels  41.2 us (8%)
    ppermute x47, waiting for transfers between devices, swap(): lax.ppermute(array, axis, [(i, i ^ bit) for i in range(lax.axis_size(axis...  173 us
    ppermute x47, starting transfers between devices, swap(): lax.ppermute(array, axis, [(i, i ^ bit) for i in range(lax.axis_size(axis...  56.9 us
    dot_general x24, matrix products, dot(): lax.dot_general(a, b, (((da,), (db,)), ((), ())), preferred_element_type=F)  48.6 us
    unnamed x150, local copies, waits for them, and re-layouts  41.5 us
    dynamic_slice x9, local copies, waits for them, and re-layouts, scatter_sum(): keep = lax.dynamic_index_in_dim(value, mine, where, keepdims=False)  33 us
    another operation x2, local copies, waits for them, and re-layouts, scatter_sum(): value = value.reshape((2,) * bits + tail)  19 us
    mul x3, local copies, waits for them, and re-layouts, weighted(): return out.reshape(length, heads, hd).astype(F) * weight[:, :, None]  14.5 us
    pallas_call x2, Pallas kernels, memory_forward(): pl.pallas_call(functools.partial(memory_forward_body, heads=heads, hd=hd,...  14.1 us
  transfers between devices with their start and end apart: 47, of which 14 were waited for; matrix products, arithmetic and copies ran while one was open for 34% of the time, Pallas kernels for 7%

profile of v1, /device:TPU:0, one launch (start us, length us, event | category | flops | bytes accessed | tf_op | source)
XLA Modules:
  0.0 531.8 jit_solution(15632760464713563803)
XLA Ops:
  42.5 22.4 %collective-permute-done = bf16[64,1024]{1,0:T(8,128)(2,1)S(1)} collective-permute-done((bf16[64,1024]{1,0:T(8,128)(2,1)S(1)}, bf16[64,1024]{1,0:T(8,128)(2,1)S(1)}, u32[]{:S(2)}, u32[]{:S(2)}) %collective-permute-start) | collective-permute-done | bytes 131104 | tf_op jit(solution)/shard_map/ppermute | solution.py:23
  82.0 10.4 %memory_forward.2 = (bf16[1024,256]{1,0:T(8,128)(2,1)}, f32[2,1024]{1,0:T(2,128)}, f32[2,64,1024]{2,1,0:T(8,128)}) custom-call(s32[1]{0:T(128)S(6)} %copy.147.flag_ref, bf16[1024,256]{1,0:T(8,128)(2,1)} %copy-done.20, bf16[64,1024]{1,0:T(8,128)(2,1)} %get-tuple-element.103.off_ref, bf16[2,4096,128]{2,1,0:T(8,128)(2,1)} %bitcast.245, ...), custom_call_target="tpu_custom_call" | custom-call | flops 8589934592 | bytes 4194304 | tf_op jit(solution)/shard_map/memory_forward/pallas_call | solution.py:141
  95.6 7.7 %collective-permute-start.8 = (f32[2,1024]{1,0:T(2,128)S(1)}, f32[2,1024]{1,0:T(2,128)S(1)}, u32[]{:S(2)}, u32[]{:S(2)}) collective-permute-start(f32[2,1024]{1,0:T(2,128)S(1)} %copy-done.59), channel_id=1, source_target_pairs={{0,4},{4,0},{8,12},{12,8},{16,20},{20,16},{24,28},{28,24},{1,5},{5... | collective-permute-start | bytes 24584 | tf_op jit(solution)/shard_map/ppermute | solution.py:23
  106.7 5.5 %local_forward.1 = (bf16[1024,256]{1,0:T(8,128)(2,1)}, f32[2,1024]{1,0:T(2,128)}) custom-call(bf16[1024,256]{1,0:T(8,128)(2,1)} %copy-done.20, bf16[1024,256]{1,0:T(8,128)(2,1)} %get-tuple-element.89.k_ref, bf16[1024,256]{1,0:T(8,128)(2,1)} %convolution_convert_fusion.1.v_ref), custom_call_target="tpu_custom_call" | custom-call | tf_op jit(solution)/shard_map/local_forward/pallas_call | solution.py:225
  116.0 12.2 %collective-permute-done.9 = bf16[1024,256]{1,0:T(8,128)(2,1)} collective-permute-done((bf16[1024,256]{1,0:T(8,128)(2,1)}, bf16[1024,256]{1,0:T(8,128)(2,1)}, u32[]{:S(2)}, u32[]{:S(2)}) %collective-permute-start.9) | collective-permute-done | bytes 524320 | tf_op jit(solution)/shard_map/ppermute | solution.py:23
  128.3 12.0 %mul.333 = f32[1024,2,128]{2,1,0:T(2,128)S(1)} broadcast(f32[1024,2]{1,0:T(8,128)S(1)} %copy.91), dimensions={0,1} | broadcast | bytes 1056768 | tf_op jit(solution)/shard_map/mul | solution.py:425
  148.4 10.0 %collective-permute-done.12 = bf16[1024,256]{1,0:T(8,128)(2,1)S(1)} collective-permute-done((bf16[1024,256]{1,0:T(8,128)(2,1)S(1)}, bf16[1024,256]{1,0:T(8,128)(2,1)S(1)}, u32[]{:S(2)}, u32[]{:S(2)}) %collective-permute-start.12) | collective-permute-done | bytes 524320 | tf_op jit(solution)/shard_map/ppermute | solution.py:23
  210.7 6.9 %collective-permute-done.21 = bf16[256,1024]{0,1:T(8,128)(2,1)S(1)} collective-permute-done((bf16[256,1024]{0,1:T(8,128)(2,1)}, bf16[256,1024]{0,1:T(8,128)(2,1)S(1)}, u32[]{:S(2)}, u32[]{:S(2)}) %collective-permute-start.21) | collective-permute-done | bytes 524320 | tf_op jit(solution)/shard_map/ppermute | solution.py:23
  217.6 10.9 %collective-permute-done.19 = bf16[256,1024]{0,1:T(8,128)(2,1)} collective-permute-done((bf16[256,1024]{0,1:T(8,128)(2,1)}, bf16[256,1024]{0,1:T(8,128)(2,1)}, u32[]{:S(2)}, u32[]{:S(2)}) %collective-permute-start.19) | collective-permute-done | bytes 524320 | tf_op jit(solution)/shard_map/ppermute | solution.py:23
  244.4 5.7 %collective-permute-done.22 = bf16[256,1024]{0,1:T(8,128)(2,1)} collective-permute-done((bf16[256,1024]{0,1:T(8,128)(2,1)}, bf16[256,1024]{0,1:T(8,128)(2,1)}, u32[]{:S(2)}, u32[]{:S(2)}) %collective-permute-start.22) | collective-permute-done | bytes 524320 | tf_op jit(solution)/shard_map/ppermute | solution.py:23
  267.2 7.5 %local_backward.1 = (f32[1024,256]{1,0:T(8,128)}, f32[1024,256]{1,0:T(8,128)}, f32[1024,256]{1,0:T(8,128)}) custom-call(bf16[1024,256]{1,0:T(8,128)(2,1)} %copy-done.20, bf16[1024,256]{1,0:T(8,128)(2,1)} %get-tuple-element.89.k_ref, bf16[1024,256]{1,0:T(8,128)(2,1)} %convolution_convert_fusion.1.v_ref, bf16[1024,256]{1,0:T(8,128)(2,1)} %get-tuple-element.111.g_ref, ...), custom_call_target="tpu_custom_call" | custom-call | tf_op jit(solution)/shard_map/local_backward/pallas_call | solution.py:264
  281.4 10.5 %memory_backward.2 = f32[1024,256]{1,0:T(8,128)} custom-call(s32[1]{0:T(128)S(6)} %copy.147.flag_ref, bf16[1024,256]{1,0:T(8,128)(2,1)} %get-tuple-element.111.g_ref, f32[4,1024]{1,0:T(4,128)} %pad_maximum_fusion.2.st_ref, f32[2,64,1024]{2,1,0:T(8,128)} %get-tuple-element.31.sel_ref, bf16[64,1024]{1,0:T(8,128)(2,1)} %get-tuple-element.103.off_ref, ...), custom_call_target="tpu_custom_call" | custom-call | flops 8589934592 | bytes 4194304 | tf_op jit(solution)/shard_map/memory_backward/pallas_call | solution.py:175
  291.9 6.5 %pad_maximum_fusion = f32[1024,2368]{0,1:T(8,128)} fusion(f32[1024,256]{0,1:T(8,128)S(1)} %copy-done.22, f32[1024,704]{0,1:T(8,128)} %convolution_bitcast_fusion, f32[1024,704]{0,1:T(8,128)} %fusion.54, f32[1024,704]{0,1:T(8,128)} %fusion.53), kind=kLoop, calls=%fused_computation | loop fusion | flops 7274496 | bytes 19398656 | tf_op jit(solution)/shard_map/concatenate | solution.py:477
  298.5 13.4 %reshape_reshape.19 = f32[2,2,2,128,2368]{3,2,1,0,4:T(2,128)} reshape(f32[1024,2368]{0,1:T(8,128)} %pad_maximum_fusion) | data formatting | bytes 19398656 | tf_op jit(solution)/shard_map/reshape;reshape | solution.py:340
  311.8 7.9 %constant_dynamic-slice_fusion.2 = bf16[2,2,1,128,2368]{3,2,1,0,4:T(2,128)(2,1)} fusion(f32[2,2,2,128,2368]{3,2,1,0,4:T(2,128)} %reshape_reshape.19, s32[]{:T(128)S(6)} %select_n.202), kind=kLoop, calls=%fused_computation.112 | loop fusion | bytes 4849668 | tf_op jit(solution)/shard_map/jit(dynamic_index_in_dim)/dynamic_slice | solution.py:346
  335.6 6.6 %collective-permute-start.32 = (bf16[1024,256]{1,0:T(8,128)(2,1)}, bf16[1024,256]{1,0:T(8,128)(2,1)S(1)}, u32[]{:S(2)}, u32[]{:S(2)}) collective-permute-start(bf16[1024,256]{1,0:T(8,128)(2,1)} %memory_backward.3), channel_id=1, source_target_pairs={{0,8},{4,12},{8,0},{12,4},{16,24},{20,28},{24,16},{28,20},{1,9},{5... | collective-permute-start | bytes 1572872 | tf_op jit(solution)/shard_map/ppermute | solution.py:23
  349.6 10.8 %collective-permute-done.31 = bf16[1024,256]{1,0:T(8,128)(2,1)S(1)} collective-permute-done((bf16[1024,256]{1,0:T(8,128)(2,1)}, bf16[1024,256]{1,0:T(8,128)(2,1)S(1)}, u32[]{:S(2)}, u32[]{:S(2)}) %collective-permute-start.31) | collective-permute-done | bytes 524320 | tf_op jit(solution)/shard_map/ppermute | solution.py:23
  360.4 32.2 %collective-permute-done.33 = bf16[1024,256]{1,0:T(8,128)(2,1)S(1)} collective-permute-done((bf16[1024,256]{1,0:T(8,128)(2,1)}, bf16[1024,256]{1,0:T(8,128)(2,1)S(1)}, u32[]{:S(2)}, u32[]{:S(2)}) %collective-permute-start.33) | collective-permute-done | bytes 524320 | tf_op jit(solution)/shard_map/ppermute | solution.py:23
  411.9 5.6 %reshape_reshape.18 = f32[2,2,2,128,768]{3,2,1,0,4:T(2,128)} reshape(f32[1024,768]{0,1:T(8,128)} %pad_maximum_fusion.1) | data formatting | bytes 6291456 | tf_op jit(solution)/shard_map/reshape;reshape | solution.py:340
  424.5 7.6 %constant_dynamic-slice_fusion.3 = f32[2,2,1,128,2368]{3,2,1,0,4:T(1,128)} fusion(f32[2,2,2,128,2368]{3,2,1,0,4:T(2,128)} %reshape_reshape.19, s32[]{:T(128)S(6)} %select_n.201), kind=kLoop, calls=%fused_computation.113 | loop fusion | bytes 9699332 | tf_op jit(solution)/shard_map/jit(dynamic_index_in_dim)/dynamic_slice | solution.py:345
  439.9 5.1 copy.102
  450.5 7.7 %collective-permute-done.37 = bf16[2,128,768]{2,1,0:T(8,128)(2,1)S(1)} collective-permute-done((bf16[2,128,768]{2,1,0:T(8,128)(2,1)S(1)}, bf16[2,128,768]{2,1,0:T(8,128)(2,1)S(1)}, u32[]{:S(2)}, u32[]{:S(2)}) %collective-permute-start.37) | collective-permute-done | bytes 393248 | tf_op jit(solution)/shard_map/ppermute | solution.py:23
  473.8 22.0 %collective-permute-done.45 = f32[8,2,128]{2,1,0:T(2,128)S(1)} collective-permute-done((f32[8,2,128]{2,1,0:T(2,128)S(1)}, f32[8,2,128]{2,1,0:T(2,128)S(1)}, u32[]{:S(2)}, u32[]{:S(2)}) %collective-permute-start.45) | collective-permute-done | bytes 8224 | tf_op jit(solution)/shard_map/ppermute | solution.py:23
  503.3 24.9 %collective-permute-done.41 = bf16[128,2368]{0,1:T(8,128)(2,1)S(1)} collective-permute-done((bf16[128,2368]{0,1:T(8,128)(2,1)}, bf16[128,2368]{0,1:T(8,128)(2,1)S(1)}, u32[]{:S(2)}, u32[]{:S(2)}) %collective-permute-start.41) | collective-permute-done | bytes 606240 | tf_op jit(solution)/shard_map/ppermute | solution.py:23
  (351 shorter events, 255.4 us)
Async XLA Ops:
  31.9 43.7 %collective-permute-start.3 = (bf16[1024,256]{1,0:T(8,128)(2,1)S(1)}, bf16[1024,256]{1,0:T(8,128)(2,1)}, u32[]{:S(2)}, u32[]{:S(2)}) collective-permute-start(bf16[1024,256]{1,0:T(8,128)(2,1)S(1)} %get-tuple-element.90.q_ref), channel_id=1, source_target_pairs={{0,16},{4,20},{8,24},{12,28},{16,0},{20,4},{24,8},{28,12},{1,17},{... | collective-permute-start | bytes 1572872 | tf_op jit(solution)/shard_map/ppermute | solution.py:23
  36.0 39.6 %collective-permute-start.4 = (bf16[1024,256]{1,0:T(8,128)(2,1)S(1)}, bf16[1024,256]{1,0:T(8,128)(2,1)}, u32[]{:S(2)}, u32[]{:S(2)}) collective-permute-start(bf16[1024,256]{1,0:T(8,128)(2,1)S(1)} %get-tuple-element.90.q_ref), channel_id=1, source_target_pairs={{0,8},{4,12},{8,0},{12,4},{16,24},{20,28},{24,16},{28,20},{1,9},{5... | collective-permute-start | bytes 1572872 | tf_op jit(solution)/shard_map/ppermute | solution.py:23
  37.6 38.1 %collective-permute-start.5 = (bf16[1024,256]{1,0:T(8,128)(2,1)S(1)}, bf16[1024,256]{1,0:T(8,128)(2,1)}, u32[]{:S(2)}, u32[]{:S(2)}) collective-permute-start(bf16[1024,256]{1,0:T(8,128)(2,1)S(1)} %get-tuple-element.90.q_ref), channel_id=1, source_target_pairs={{0,4},{4,0},{8,12},{12,8},{16,20},{20,16},{24,28},{28,24},{1,5},{5... | collective-permute-start | bytes 1572872 | tf_op jit(solution)/shard_map/ppermute | solution.py:23
  41.8 23.2 %collective-permute-start = (bf16[64,1024]{1,0:T(8,128)(2,1)S(1)}, bf16[64,1024]{1,0:T(8,128)(2,1)S(1)}, u32[]{:S(2)}, u32[]{:S(2)}) collective-permute-start(bf16[64,1024]{1,0:T(8,128)(2,1)S(1)} %get-tuple-element.102), channel_id=1, source_target_pairs={{0,16},{4,20},{8,24},{12,28},{16,0},{20,4},{24,8},{28,12},{1,17},{... | collective-permute-start | bytes 393224 | tf_op jit(solution)/shard_map/ppermute | solution.py:23
  42.1 32.3 %collective-permute-start.1 = (bf16[64,1024]{1,0:T(8,128)(2,1)S(1)}, bf16[64,1024]{1,0:T(8,128)(2,1)S(1)}, u32[]{:S(2)}, u32[]{:S(2)}) collective-permute-start(bf16[64,1024]{1,0:T(8,128)(2,1)S(1)} %get-tuple-element.102), channel_id=1, source_target_pairs={{0,8},{4,12},{8,0},{12,4},{16,24},{20,28},{24,16},{28,20},{1,9},{5... | collective-permute-start | bytes 393224 | tf_op jit(solution)/shard_map/ppermute | solution.py:23
  81.2 22.2 %collective-permute-start.6 = (f32[2,1024]{1,0:T(2,128)}, f32[2,1024]{1,0:T(2,128)S(1)}, u32[]{:S(2)}, u32[]{:S(2)}) collective-permute-start(f32[2,1024]{1,0:T(2,128)} %get-tuple-element.25), channel_id=1, source_target_pairs={{0,16},{4,20},{8,24},{12,28},{16,0},{20,4},{24,8},{28,12},{1,17},{... | collective-permute-start | bytes 24584 | tf_op jit(solution)/shard_map/ppermute | solution.py:23
  103.3 25.0 %collective-permute-start.9 = (bf16[1024,256]{1,0:T(8,128)(2,1)}, bf16[1024,256]{1,0:T(8,128)(2,1)}, u32[]{:S(2)}, u32[]{:S(2)}) collective-permute-start(bf16[1024,256]{1,0:T(8,128)(2,1)} %get-tuple-element.27), channel_id=1, source_target_pairs={{0,16},{4,20},{8,24},{12,28},{16,0},{20,4},{24,8},{28,12},{1,17},{... | collective-permute-start | bytes 1572872 | tf_op jit(solution)/shard_map/ppermute | solution.py:23
  103.3 25.0 %collective-permute-start.10 = (bf16[1024,256]{1,0:T(8,128)(2,1)}, bf16[1024,256]{1,0:T(8,128)(2,1)}, u32[]{:S(2)}, u32[]{:S(2)}) collective-permute-start(bf16[1024,256]{1,0:T(8,128)(2,1)} %get-tuple-element.27), channel_id=1, source_target_pairs={{0,8},{4,12},{8,0},{12,4},{16,24},{20,28},{24,16},{28,20},{1,9},{5... | collective-permute-start | bytes 1572872 | tf_op jit(solution)/shard_map/ppermute | solution.py:23
  103.4 24.9 %collective-permute-start.11 = (bf16[1024,256]{1,0:T(8,128)(2,1)}, bf16[1024,256]{1,0:T(8,128)(2,1)}, u32[]{:S(2)}, u32[]{:S(2)}) collective-permute-start(bf16[1024,256]{1,0:T(8,128)(2,1)} %get-tuple-element.27), channel_id=1, source_target_pairs={{0,4},{4,0},{8,12},{12,8},{16,20},{20,16},{24,28},{28,24},{1,5},{5... | collective-permute-start | bytes 1572872 | tf_op jit(solution)/shard_map/ppermute | solution.py:23
  112.2 33.8 %collective-permute-start.13 = (bf16[256,1024]{1,0:T(8,128)(2,1)}, bf16[256,1024]{1,0:T(8,128)(2,1)}, u32[]{:S(2)}, u32[]{:S(2)}) collective-permute-start(bf16[256,1024]{1,0:T(8,128)(2,1)} %param.22), channel_id=1, source_target_pairs={{0,2},{1,3},{2,0},{3,1},{4,6},{5,7},{6,4},{7,5},{8,10},{9,11},{10,... | collective-permute-start | bytes 1572872 | tf_op jit(solution)/shard_map/ppermute | solution.py:23
  260.6 69.4 %collective-permute-start.25 = (bf16[1024,256]{1,0:T(8,128)(2,1)}, bf16[1024,256]{1,0:T(8,128)(2,1)}, u32[]{:S(2)}, u32[]{:S(2)}) collective-permute-start(bf16[1024,256]{1,0:T(8,128)(2,1)} %get-tuple-element.111.g_ref), channel_id=1, source_target_pairs={{0,16},{4,20},{8,24},{12,28},{16,0},{20,4},{24,8},{28,12},{1,17},{... | collective-permute-start | bytes 1572872 | tf_op jit(solution)/shard_map/ppermute | solution.py:23
  260.6 69.4 %collective-permute-start.26 = (bf16[1024,256]{1,0:T(8,128)(2,1)}, bf16[1024,256]{1,0:T(8,128)(2,1)}, u32[]{:S(2)}, u32[]{:S(2)}) collective-permute-start(bf16[1024,256]{1,0:T(8,128)(2,1)} %get-tuple-element.111.g_ref), channel_id=1, source_target_pairs={{0,8},{4,12},{8,0},{12,4},{16,24},{20,28},{24,16},{28,20},{1,9},{5... | collective-permute-start | bytes 1572872 | tf_op jit(solution)/shard_map/ppermute | solution.py:23
  260.7 69.4 %collective-permute-start.27 = (bf16[1024,256]{1,0:T(8,128)(2,1)}, bf16[1024,256]{1,0:T(8,128)(2,1)}, u32[]{:S(2)}, u32[]{:S(2)}) collective-permute-start(bf16[1024,256]{1,0:T(8,128)(2,1)} %get-tuple-element.111.g_ref), channel_id=1, source_target_pairs={{0,4},{4,0},{8,12},{12,8},{16,20},{20,16},{24,28},{28,24},{1,5},{5... | collective-permute-start | bytes 1572872 | tf_op jit(solution)/shard_map/ppermute | solution.py:23
  274.7 45.0 %collective-permute-start.28 = (f32[4,1024]{1,0:T(4,128)}, f32[4,1024]{1,0:T(4,128)S(1)}, u32[]{:S(2)}, u32[]{:S(2)}) collective-permute-start(f32[4,1024]{1,0:T(4,128)} %pad_maximum_fusion.2.st_ref), channel_id=1, source_target_pairs={{0,16},{4,20},{8,24},{12,28},{16,0},{20,4},{24,8},{28,12},{1,17},{... | collective-permute-start | bytes 49160 | tf_op jit(solution)/shard_map/ppermute | solution.py:23
  277.6 49.8 %collective-permute-start.29 = (f32[4,1024]{1,0:T(4,128)}, f32[4,1024]{1,0:T(4,128)S(1)}, u32[]{:S(2)}, u32[]{:S(2)}) collective-permute-start(f32[4,1024]{1,0:T(4,128)} %pad_maximum_fusion.2.st_ref), channel_id=1, source_target_pairs={{0,8},{4,12},{8,0},{12,4},{16,24},{20,28},{24,16},{28,20},{1,9},{5... | collective-permute-start | bytes 49160 | tf_op jit(solution)/shard_map/ppermute | solution.py:23
  327.5 131.2 %collective-permute-start.39 = (bf16[2,2,128,2368]{2,3,0,1:T(8,128)(2,1)}, bf16[2,2,128,2368]{2,3,0,1:T(8,128)(2,1)}, u32[]{:S(2)}, u32[]{:S(2)}) collective-permute-start(bf16[2,2,128,2368]{2,3,0,1:T(8,128)(2,1)} %bitcast.221), channel_id=1, source_target_pairs={{0,4},{4,0},{8,12},{12,8},{16,20},{20,16},{24,28},{28,24},{1,5},{5... | collective-permute-start | bytes 7274504 | tf_op jit(solution)/shard_map/ppermute | solution.py:23
  335.5 24.8 %collective-permute-start.31 = (bf16[1024,256]{1,0:T(8,128)(2,1)}, bf16[1024,256]{1,0:T(8,128)(2,1)S(1)}, u32[]{:S(2)}, u32[]{:S(2)}) collective-permute-start(bf16[1024,256]{1,0:T(8,128)(2,1)} %memory_backward.3), channel_id=1, source_target_pairs={{0,16},{4,20},{8,24},{12,28},{16,0},{20,4},{24,8},{28,12},{1,17},{... | collective-permute-start | bytes 1572872 | tf_op jit(solution)/shard_map/ppermute | solution.py:23
  335.6 24.8 %collective-permute-start.32 = (bf16[1024,256]{1,0:T(8,128)(2,1)}, bf16[1024,256]{1,0:T(8,128)(2,1)S(1)}, u32[]{:S(2)}, u32[]{:S(2)}) collective-permute-start(bf16[1024,256]{1,0:T(8,128)(2,1)} %memory_backward.3), channel_id=1, source_target_pairs={{0,8},{4,12},{8,0},{12,4},{16,24},{20,28},{24,16},{28,20},{1,9},{5... | collective-permute-start | bytes 1572872 | tf_op jit(solution)/shard_map/ppermute | solution.py:23
  342.2 50.4 %collective-permute-start.33 = (bf16[1024,256]{1,0:T(8,128)(2,1)}, bf16[1024,256]{1,0:T(8,128)(2,1)S(1)}, u32[]{:S(2)}, u32[]{:S(2)}) collective-permute-start(bf16[1024,256]{1,0:T(8,128)(2,1)} %memory_backward.3), channel_id=1, source_target_pairs={{0,4},{4,0},{8,12},{12,8},{16,20},{20,16},{24,28},{28,24},{1,5},{5... | collective-permute-start | bytes 1572872 | tf_op jit(solution)/shard_map/ppermute | solution.py:23
  408.5 38.7 %collective-permute-start.34 = (bf16[2,256,1024]{1,2,0:T(8,128)(2,1)}, bf16[2,256,1024]{1,2,0:T(8,128)(2,1)}, u32[]{:S(2)}, u32[]{:S(2)}) collective-permute-start(bf16[2,256,1024]{1,2,0:T(8,128)(2,1)} %bitcast.254), channel_id=1, source_target_pairs={{0,1},{1,0},{2,3},{3,2},{4,5},{5,4},{6,7},{7,6},{8,9},{9,8},{10,11... | collective-permute-start | bytes 3145736 | tf_op jit(solution)/shard_map/ppermute | solution.py:23
  422.7 22.3 %collective-permute-start.36 = (bf16[2,2,128,768]{3,2,0,1:T(8,128)(2,1)S(1)}, bf16[2,2,128,768]{3,2,0,1:T(8,128)(2,1)}, u32[]{:S(2)}, u32[]{:S(2)}) collective-permute-start(bf16[2,2,128,768]{3,2,0,1:T(8,128)(2,1)S(1)} %bitcast.255), channel_id=1, source_target_pairs={{0,4},{4,0},{8,12},{12,8},{16,20},{20,16},{24,28},{28,24},{1,5},{5... | collective-permute-start | bytes 2359304 | tf_op jit(solution)/shard_map/ppermute | solution.py:23
  463.9 32.0 %collective-permute-start.40 = (bf16[2,128,2368]{1,2,0:T(8,128)(2,1)S(1)}, bf16[2,128,2368]{1,2,0:T(8,128)(2,1)S(1)}, u32[]{:S(2)}, u32[]{:S(2)}) collective-permute-start(bf16[2,128,2368]{1,2,0:T(8,128)(2,1)S(1)} %fusion.8), channel_id=1, source_target_pairs={{0,8},{4,12},{8,0},{12,4},{16,24},{20,28},{24,16},{28,20},{1,9},{5... | collective-permute-start | bytes 3637256 | tf_op jit(solution)/shard_map/ppermute | solution.py:23
  473.6 22.2 %collective-permute-start.45 = (f32[8,2,128]{2,1,0:T(2,128)S(1)}, f32[8,2,128]{2,1,0:T(2,128)S(1)}, u32[]{:S(2)}, u32[]{:S(2)}) collective-permute-start(f32[8,2,128]{2,1,0:T(2,128)S(1)} %fusion.104), channel_id=1, source_target_pairs={{0,8},{4,12},{8,0},{12,4},{16,24},{20,28},{24,16},{28,20},{1,9},{5... | collective-permute-start | bytes 24584 | tf_op jit(solution)/shard_map/ppermute | solution.py:23
  498.4 29.8 %collective-permute-start.41 = (bf16[128,2368]{0,1:T(8,128)(2,1)}, bf16[128,2368]{0,1:T(8,128)(2,1)S(1)}, u32[]{:S(2)}, u32[]{:S(2)}) collective-permute-start(bf16[128,2368]{0,1:T(8,128)(2,1)} %fusion.25), channel_id=1, source_target_pairs={{0,16},{4,20},{8,24},{12,28},{16,0},{20,4},{24,8},{28,12},{1,17},{... | collective-permute-start | bytes 1818632 | tf_op jit(solution)/shard_map/ppermute | solution.py:23
  (91 other events, 963.7 us)

commit v2 on v1

v2 whole, which is shorter than its diff:
```python
import functools

import jax
import jax.numpy as jnp
import numpy as np
from jax import lax
from jax.experimental import pallas as pl
from jax.experimental.pallas import tpu as pltpu
from jax.sharding import PartitionSpec as P

epsilon = 1e-05
negative_big = -1e30
F = jnp.float32
B = jnp.bfloat16
GROUP_BLOCK = 16


def dot(a, b, da, db):
    return lax.dot_general(a, b, (((da,), (db,)), ((), ())), preferred_element_type=F)


def swap(array, axis, bit):
    return lax.ppermute(array, axis, [(i, i ^ bit) for i in range(lax.axis_size(axis))])


def axis_bits(axis):
    return lax.axis_size(axis).bit_length() - 1


def call(body, out_shape, name, flops=0, **options):
    return pl.pallas_call(
        body,
        out_shape=out_shape,
        name=name,
        cost_estimate=pl.CostEstimate(flops=flops, transcendentals=0, bytes_accessed=flops // 400),
        **options,
    )


def shape(dims, dtype):
    return jax.ShapeDtypeStruct(dims, dtype)


def whole():
    return pl.BlockSpec(memory_space=pltpu.VMEM)


def scalars():
    return pl.BlockSpec(memory_space=pltpu.SMEM)


def slot_place(difference, order):
    place = 0
    for b in order:
        place = place * 2 + ((difference >> b) & 1)
    return place


def choose(refs, index, chosen):
    value = refs[0][index]
    for b in range(1, len(refs)):
        value = jnp.where(chosen == b, refs[b][index], value)
    return value


def split_terms(x):
    first = x.astype(B).astype(F)
    second = (x - first).astype(B).astype(F)
    third = (x - first - second).astype(B).astype(F)
    return [first, second, third]


def pack_rows(x, lanes, total):
    rows = []
    terms = split_terms(x)
    for b in range(x.shape[1] // lanes):
        rows += [t[:, b * lanes : (b + 1) * lanes] for t in terms]
    used = sum(r.shape[0] for r in rows)
    if total > used:
        rows.append(jnp.zeros((total - used, lanes), F))
    return jnp.concatenate(rows, axis=0).astype(B)


def unpack_rows(packed, n, blocks):
    packed = packed.astype(F)
    out = []
    for b in range(blocks):
        base = b * 3 * n
        out.append(
            packed[base : base + n]
            + packed[base + n : base + 2 * n]
            + packed[base + 2 * n : base + 3 * n]
        )
    return jnp.concatenate(out, axis=1)


def rope(x, table, direction):
    half = x.shape[1] // 2
    other = pltpu.roll(table, half, 1)
    front = lax.broadcasted_iota(jnp.int32, x.shape, 1) < half
    cos = jnp.where(front, table, other)
    sin = jnp.where(front, -other, table) * direction
    return x * cos + pltpu.roll(x, half, 1) * sin


def project_body(
    flag_ref, x_ref, knn_ref, gain_ref, wq_ref, wk_ref, wv_ref, table_ref,
    ship_ref, q_ref, k_ref, v_ref, normed_ref, off_ref, *, parts, heads, hd, spread,
):
    length = x_ref.shape[0]
    share = length // parts
    piece = share // 2
    chunk = length // 2
    columns = heads * hd
    groups = knn_ref.shape[1] // 2
    gain = gain_ref[...]
    for j in range(parts):
        r = slice(j * share, (j + 1) * share)
        x = x_ref[r, :].astype(F)
        factor = lax.rsqrt(jnp.mean(x * x, axis=1, keepdims=True) + epsilon)
        normed = (x * factor * gain).astype(B)
        table = table_ref[r, :]
        q = dot(normed, wq_ref[...], 1, 0)
        k = dot(normed, wk_ref[...], 1, 0)
        v_ref[r, :] = dot(normed, wv_ref[...], 1, 0).astype(B)
        q = jnp.concatenate(
            [rope(q[:, h * hd : (h + 1) * hd], table, 1.0) for h in range(heads)], axis=1
        ).astype(B)
        q_ref[r, :] = q
        k_ref[r, :] = jnp.concatenate(
            [rope(k[:, h * hd : (h + 1) * hd], table, 1.0) for h in range(heads)], axis=1
        ).astype(B)
        knn = knn_ref[r, :]
        start = lax.broadcasted_iota(jnp.int32, knn.shape, 1) * spread
        off = (knn - start).astype(F).T
        far = jnp.where(flag_ref[0] > 0, off[groups:], -1.0).astype(B)
        off = off[:groups].astype(B)
        for c in range(2):
            p = slice(c * piece, (c + 1) * piece)
            t = slice(j * piece, (j + 1) * piece)
            normed_ref[c, t, :] = normed[p]
            ship_ref[c, t, :] = q[p]
            off_ref[c, :, t] = off[:, p]
            lane = j * piece
            row = chunk + lane // columns * groups
            lane = lane % columns
            ship_ref[c, row : row + groups, lane : lane + piece] = far[:, p]


def project(flag, tokens, knn, gain, wq, wk, wv, table, parts, heads, spread):
    length, width = tokens.shape
    columns = wq.shape[1]
    groups = knn.shape[1] // 2
    chunk = length // 2
    body = functools.partial(
        project_body, parts=parts, heads=heads, hd=columns // heads, spread=spread
    )
    return call(
        body,
        [
            shape((2, chunk + chunk // columns * groups, columns), B),
            shape((length, columns), B),
            shape((length, columns), B),
            shape((length, columns), B),
            shape((2, chunk, width), B),
            shape((2, groups, chunk), B),
        ],
        "project",
        6 * length * width * columns,
        in_specs=[scalars()] + [whole()] * 7,
    )(flag, tokens, knn, gain, wq, wk, wv, table)


def pick(block_scores, offsets, heads, spread, gb):
    picked = [s[:gb] for s in block_scores]
    for t in range(1, spread):
        here = offsets == float(t)
        for h in range(heads):
            picked[h] = jnp.where(here, block_scores[h][t * gb : (t + 1) * gb], picked[h])
    return picked


def picked_scores(rows_ref, values, offs, heads, hd, spread, gb):
    rows = gb * spread
    wide = offs.astype(F)
    out = [[] for _ in range(heads)]
    for b in range(offs.shape[0] // gb):
        scores = [
            dot(
                rows_ref[h, b * rows : (b + 1) * rows, :], values[:, h * hd : (h + 1) * hd], 1, 1
            )
            for h in range(heads)
        ]
        picked = pick(scores, wide[b * gb : (b + 1) * gb], heads, spread, gb)
        for h in range(heads):
            out[h].append(picked[h])
    return [jnp.concatenate(o, axis=0) for o in out]


def spread_dot(rows_ref, h, picked, offs, spread, gb):
    rows = gb * spread
    total = None
    zero = jnp.zeros((gb, picked.shape[1]), B)
    for b in range(offs.shape[0] // gb):
        p = picked[b * gb : (b + 1) * gb]
        o = offs[b * gb : (b + 1) * gb]
        wide = jnp.concatenate(
            [jnp.where(o == jnp.asarray(t, B), p, zero) for t in range(spread)], axis=0
        )
        part = dot(rows_ref[h, b * rows : (b + 1) * rows, :], wide, 0, 0)
        total = part if total is None else total + part
    return total


def attend(q, offs, k_ref, v_ref, sel_ref, heads, hd, spread):
    outs, sums = [], []
    picked = picked_scores(k_ref, q, offs, heads, hd, spread, GROUP_BLOCK)
    for h in range(heads):
        x = picked[h] * hd**-0.5
        sel_ref[h] = x
        peak = jnp.max(x, axis=0, keepdims=True)
        p = jnp.exp(x - peak)
        total = jnp.sum(p, axis=0, keepdims=True)
        sums.append(peak + jnp.log(total))
        out = spread_dot(v_ref, h, p.astype(B), offs, spread, GROUP_BLOCK)
        outs.append((out / total).T.astype(B))
    return outs, sums


def own_attend_body(flag_ref, ship_ref, off_ref, k_ref, v_ref, o_ref, lse_ref, sel_ref, *, spread):
    heads, _, hd = k_ref.shape
    chunk = o_ref.shape[1]

    @pl.when(flag_ref[0] > 0)
    def _():
        outs, sums = attend(
            ship_ref[0, :chunk, :], off_ref[0], k_ref, v_ref, sel_ref.at[0], heads, hd, spread
        )
        for h in range(heads):
            o_ref[0, :, h * hd : (h + 1) * hd] = outs[h]
            lse_ref[0, h : h + 1, :] = sums[h]

    @pl.when(flag_ref[0] <= 0)
    def _():
        o_ref[...] = jnp.zeros_like(o_ref)
        lse_ref[...] = jnp.full_like(lse_ref, negative_big)


def resident(dims):
    return pl.BlockSpec(dims, lambda *i: (0,) * len(dims))


def own_attend(flag, ship, off, k, v, spread):
    heads, rows, hd = k.shape
    chunk = off.shape[2]
    groups = off.shape[1]
    columns = heads * hd
    by_chunk = lambda c: (c, 0, 0)
    return call(
        functools.partial(own_attend_body, spread=spread),
        [
            shape((2, chunk, columns), B),
            shape((2, heads, chunk), F),
            shape((2, heads, groups, chunk), F),
        ],
        "own_attend",
        16 * chunk * columns * rows,
        grid=(2,),
        in_specs=[
            scalars(),
            pl.BlockSpec((1,) + ship.shape[1:], by_chunk),
            pl.BlockSpec((1, groups, chunk), by_chunk),
            resident(k.shape),
            resident(v.shape),
        ],
        out_specs=[
            pl.BlockSpec((1, chunk, columns), by_chunk),
            pl.BlockSpec((1, heads, chunk), by_chunk),
            pl.BlockSpec((1, heads, groups, chunk), lambda c: (c, 0, 0, 0)),
        ],
    )(flag, ship, off, k, v)


def shipped_offsets(refs, chosen, chunk, groups, columns):
    blocks = chunk // columns
    index = (0, slice(chunk, chunk + blocks * groups), slice(None))
    packed = choose(refs, index, chosen)
    return jnp.concatenate([packed[b * groups : (b + 1) * groups] for b in range(blocks)], axis=1)


def their_attend_body(chosen_ref, *refs, count, spread, chunk, groups):
    ships = refs[:count]
    k_ref, v_ref, o_ref, sel_ref, off_ref, flag_ref = refs[count:]
    heads, _, hd = k_ref.shape
    columns = heads * hd
    chosen = chosen_ref[0]
    offs = shipped_offsets(ships, chosen, chunk, groups, columns)
    off_ref[...] = offs
    on = jnp.max(offs[:1, :128].astype(F)) >= 0
    flag_ref[0] = on.astype(jnp.int32)

    @pl.when(on)
    def _():
        q = choose(ships, (0, slice(0, chunk), slice(None)), chosen)
        outs, sums = attend(q, offs, k_ref, v_ref, sel_ref, heads, hd, spread)
        for h in range(heads):
            o_ref[:chunk, h * hd : (h + 1) * hd] = outs[h]
        o_ref[chunk:, :] = pack_rows(
            jnp.concatenate(sums, axis=0), columns, o_ref.shape[0] - chunk
        )

    @pl.when(jnp.logical_not(on))
    def _():
        o_ref[:chunk, :] = jnp.zeros((chunk, columns), B)
        o_ref[chunk:, :] = pack_rows(
            jnp.full((heads, chunk), negative_big, F), columns, o_ref.shape[0] - chunk
        )


def padded_rows(n):
    return -(-n // 16) * 16


def their_attend(c, chosen, ships, k, v, spread, groups):
    heads, rows, hd = k.shape
    columns = heads * hd
    chunk = ships[0].shape[1] * columns // (columns + groups)
    extra = padded_rows(3 * heads * chunk // columns)
    return call(
        functools.partial(
            their_attend_body, count=len(ships), spread=spread, chunk=chunk, groups=groups
        ),
        [
            shape((chunk + extra, columns), B),
            shape((heads, groups, chunk), F),
            shape((groups, chunk), B),
            shape((1,), jnp.int32),
        ],
        "their_attend",
        8 * chunk * columns * rows,
        grid=(1,),
        in_specs=[scalars()]
        + [pl.BlockSpec((1,) + s.shape[1:], lambda i: (c, 0, 0)) for s in ships]
        + [resident(k.shape), resident(v.shape)],
        out_specs=[
            resident((chunk + extra, columns)),
            resident((heads, groups, chunk)),
            resident((groups, chunk)),
            scalars(),
        ],
    )(chosen, *ships, k, v)


def score_gradients(g, offs, log_total, delta, sel_ref, v_ref, heads, hd, spread):
    picked = picked_scores(v_ref, g, offs, heads, hd, spread, GROUP_BLOCK)
    return [
        (jnp.exp(sel_ref[h] - log_total[h : h + 1]) * (picked[h] - delta[h : h + 1])).astype(B)
        for h in range(heads)
    ]


def own_backward_body(
    flag_ref, ship_ref, st_ref, sel_ref, off_ref, k_ref, v_ref, local_ref, dq_ref, *, spread
):
    heads, _, hd = k_ref.shape

    @pl.when(flag_ref[0] > 0)
    def _():
        offs = off_ref[0]
        stats = st_ref[0]
        ds = score_gradients(
            ship_ref[...], offs, stats[:heads], stats[heads:], sel_ref.at[0], v_ref, heads, hd,
            spread
        )
        for h in range(heads):
            c = slice(h * hd, (h + 1) * hd)
            out = spread_dot(k_ref, h, ds[h], offs, spread, GROUP_BLOCK)
            dq_ref[0, :, c] = local_ref[0, :, c] + (out * hd**-0.5).T

    @pl.when(flag_ref[0] <= 0)
    def _():
        dq_ref[...] = local_ref[...]


def own_backward(flag, ship, stats, sel, off, k, v, local, spread):
    heads, rows, hd = k.shape
    chunk = off.shape[2]
    groups = off.shape[1]
    columns = heads * hd
    by_chunk = lambda c: (c, 0, 0)
    return call(
        functools.partial(own_backward_body, spread=spread),
        shape((2, chunk, columns), F),
        "own_backward",
        16 * chunk * columns * rows,
        grid=(2,),
        in_specs=[
            scalars(),
            pl.BlockSpec((chunk, columns), lambda c: (c, 0)),
            pl.BlockSpec((1, 2 * heads, chunk), by_chunk),
            pl.BlockSpec((1, heads, groups, chunk), lambda c: (c, 0, 0, 0)),
            pl.BlockSpec((1, groups, chunk), by_chunk),
            resident(k.shape),
            resident(v.shape),
            pl.BlockSpec((1, chunk, columns), by_chunk),
        ],
        out_specs=pl.BlockSpec((1, chunk, columns), by_chunk),
    )(flag, ship, stats, sel, off, k, v, local)


def their_backward_body(chosen_ref, flag_ref, *refs, count, spread, chunk):
    ships = refs[:count]
    sel0, sel1, off0, off1, k_ref, v_ref, dq_ref = refs[count:]
    heads, _, hd = k_ref.shape
    columns = heads * hd
    blocks = chunk // columns
    extra = padded_rows(6 * heads * blocks)
    chosen = chosen_ref[0]
    on = flag_ref[0] > 0

    @pl.when(on)
    def _():
        for c, (sel_ref, off_ref) in enumerate(((sel0, off0), (sel1, off1))):
            offs = off_ref[...]
            g = choose(ships, (slice(c * chunk, (c + 1) * chunk), slice(None)), chosen)
            row = 2 * chunk + c * extra
            stats = unpack_rows(
                choose(ships, (slice(row, row + extra), slice(None)), chosen), 2 * heads, blocks
            )
            ds = score_gradients(
                g, offs, stats[:heads], stats[heads:], sel_ref, v_ref, heads, hd, spread
            )
            for h in range(heads):
                out = spread_dot(k_ref, h, ds[h], offs, spread, GROUP_BLOCK)
                dq_ref[c * chunk : (c + 1) * chunk, h * hd : (h + 1) * hd] = (
                    (out * hd**-0.5).T.astype(B)
                )

    @pl.when(jnp.logical_not(on))
    def _():
        dq_ref[...] = jnp.zeros_like(dq_ref)


def their_backward(chosen, flag, ships, sels, offs, k, v, spread):
    heads, rows, hd = k.shape
    columns = heads * hd
    chunk = offs[0].shape[1]
    return call(
        functools.partial(their_backward_body, count=len(ships), spread=spread, chunk=chunk),
        shape((2 * chunk, columns), B),
        "their_backward",
        16 * chunk * columns * rows,
        in_specs=[scalars(), scalars()] + [whole()] * (len(ships) + 6),
    )(chosen, flag, *ships, *sels, *offs, k, v)


def causal_scores(k, q, w, scale):
    s = dot(k, q, 1, 1) * scale
    n = k.shape[0]
    key = lax.broadcasted_iota(jnp.int32, (w, w), 0)
    query = lax.broadcasted_iota(jnp.int32, (w, w), 1)
    diagonal = jnp.where(key <= query, s[n - w :], negative_big)
    return diagonal if n == w else jnp.concatenate([s[: n - w], diagonal], axis=0)


def local_forward_body(q_ref, k_ref, v_ref, o_ref, lse_ref, *, heads, parts):
    length, columns = q_ref.shape
    hd = columns // heads
    w = length // parts
    piece = w // 2
    for h in range(heads):
        c = slice(h * hd, (h + 1) * hd)
        for i in range(parts):
            n = (i + 1) * w
            s = causal_scores(k_ref[:n, c], q_ref[i * w : n, c], w, hd**-0.5)
            peak = jnp.max(s, axis=0, keepdims=True)
            p = jnp.exp(s - peak)
            total = jnp.sum(p, axis=0, keepdims=True)
            lse = peak + jnp.log(total)
            out = (dot(v_ref[:n, c], p.astype(B), 0, 0) / total).T.astype(B)
            t = slice(i * piece, (i + 1) * piece)
            for a in range(2):
                o_ref[a, t, c] = out[a * piece : (a + 1) * piece]
                lse_ref[a, h : h + 1, t] = lse[:, a * piece : (a + 1) * piece]


def local_forward(q, k, v, heads, parts):
    length, columns = q.shape
    return call(
        functools.partial(local_forward_body, heads=heads, parts=parts),
        [shape((2, length // 2, columns), B), shape((2, heads, length // 2), F)],
        "local_forward",
        4 * length * length * columns,
        in_specs=[whole()] * 3,
    )(q, k, v)


def local_backward_body(
    q_ref, k_ref, v_ref, ship_ref, st_ref, table_ref, dq_ref, dkv_ref, dk_ref, dv_ref,
    *, heads, parts
):
    length, columns = q_ref.shape
    hd = columns // heads
    w = length // parts
    piece = w // 2
    chunk = length // 2
    scale = hd**-0.5
    for h in range(heads):
        c = slice(h * hd, (h + 1) * hd)
        for i in reversed(range(parts)):
            n = (i + 1) * w
            r = slice(i * w, n)
            t = slice(i * piece, (i + 1) * piece)
            g = jnp.concatenate(
                [ship_ref[a * chunk + i * piece : a * chunk + (i + 1) * piece, c] for a in range(2)],
                axis=0,
            )
            stats = jnp.concatenate([st_ref[a, :, t] for a in range(2)], axis=1)
            s = causal_scores(k_ref[:n, c], q_ref[r, c], w, scale)
            p = jnp.exp(s - stats[h : h + 1])
            dp = dot(v_ref[:n, c], g, 1, 1)
            ds = (p * (dp - stats[heads + h : heads + h + 1])).astype(B)
            dq = (dot(k_ref[:n, c], ds, 0, 0) * scale).T
            for a in range(2):
                dq_ref[a, t, c] = dq[a * piece : (a + 1) * piece]
            dk = dot(ds, q_ref[r, c], 1, 0) * scale
            dv = dot(p.astype(B), g, 1, 0)
            if i == parts - 1:
                dk_ref[:n, :] = dk
                dv_ref[:n, :] = dv
            else:
                dk_ref[:n, :] += dk
                dv_ref[:n, :] += dv
        dk = rope(dk_ref[...], table_ref[...], -1.0).astype(B)
        dv = dv_ref[...].astype(B)
        for i in range(parts):
            t = slice(i * piece, (i + 1) * piece)
            for a in range(2):
                r = slice(i * w + a * piece, i * w + (a + 1) * piece)
                dkv_ref[a, t, c] = dk[r]
                dkv_ref[a, t, columns + h * hd : columns + (h + 1) * hd] = dv[r]


def local_backward(q, k, v, ship, stats, table, heads, parts):
    length, columns = q.shape
    hd = columns // heads
    return call(
        functools.partial(local_backward_body, heads=heads, parts=parts),
        [shape((2, length // 2, columns), F), shape((2, length // 2, 2 * columns), B)],
        "local_backward",
        10 * length * length * columns,
        in_specs=[whole()] * 6,
        scratch_shapes=[pltpu.VMEM((length, hd), F)] * 2,
    )(q, k, v, ship, stats, table)


def merge_body(
    chosen_ref, lo_ref, ll_ref, oo_ref, ol_ref, *refs, count, heads
):
    ships = refs[:count]
    att_ref, total_ref = refs[count:]
    chunk, columns = att_ref.shape
    hd = columns // heads
    chosen = chosen_ref[0]
    far = choose(ships, (slice(0, chunk), slice(None)), chosen).astype(F)
    packed = choose(ships, (slice(chunk, ships[0].shape[0]), slice(None)), chosen)
    far_lse = unpack_rows(packed, heads, chunk // columns)
    local_lse = ll_ref[0]
    own_lse = ol_ref[0]
    peak = jnp.maximum(jnp.maximum(local_lse, own_lse), far_lse)
    weights = [jnp.exp(l - peak) for l in (local_lse, own_lse, far_lse)]
    total = weights[0] + weights[1] + weights[2]
    total_ref[...] = peak + jnp.log(total)
    weights = [x / total for x in weights]
    stacked = jnp.concatenate(weights + [jnp.zeros((8 - 3 * heads % 8, chunk), F)], axis=0).T
    for h in range(heads):
        c = slice(h * hd, (h + 1) * hd)
        att_ref[:, c] = (
            lo_ref[0, :, c].astype(F) * stacked[:, h : h + 1]
            + oo_ref[0, :, c].astype(F) * stacked[:, heads + h : heads + h + 1]
            + far[:, c] * stacked[:, 2 * heads + h : 2 * heads + h + 1]
        ).astype(B)


def merge(c, chosen, local, own, ships, heads):
    _, chunk, columns = local[0].shape
    part = pl.BlockSpec((1, chunk, columns), lambda i: (c, 0, 0))
    row = pl.BlockSpec((1, heads, chunk), lambda i: (c, 0, 0))
    return call(
        functools.partial(merge_body, count=len(ships), heads=heads),
        [shape((chunk, columns), B), shape((heads, chunk), F)],
        "merge",
        grid=(1,),
        in_specs=[scalars(), part, row, part, row] + [resident(s.shape) for s in ships],
        out_specs=[resident((chunk, columns)), resident((heads, chunk))],
    )(chosen, *local, *own, *ships)


def feed_body(me_ref, *refs, parts):
    pieces = refs[:parts]
    outs = refs[parts : 2 * parts]
    (x_ref, g_ref, gain_ref, wg_ref, wu_ref, wd_ref) = refs[2 * parts : 2 * parts + 6]
    (normed_ref, gu_ref, hidden_ref, gn_ref, down_ref, own_ref) = refs[2 * parts + 6 :]
    me = me_ref[0]
    piece = x_ref.shape[2]
    width = x_ref.shape[3]
    ff = wg_ref.shape[1]
    order = list(range(parts.bit_length() - 1))
    for half in range(2):
        js = range(half * parts // 2, (half + 1) * parts // 2)
        r = slice(half * parts // 2 * piece, (half + 1) * parts // 2 * piece)
        middle = x_ref[js[0] : js[-1] + 1, 0].reshape(-1, width).astype(F)
        for p, w in zip(pieces, outs):
            middle = middle + dot(p[r, :], w[...], 1, 0)
        for a, j in enumerate(js):
            @pl.when(me == j)
            def _(a=a):
                own_ref[...] = middle[a * piece : (a + 1) * piece]
        factor = lax.rsqrt(jnp.mean(middle * middle, axis=1, keepdims=True) + epsilon)
        normed = (middle * factor * gain_ref[...]).astype(B)
        normed_ref[r, :] = normed
        gate = dot(normed, wg_ref[...], 1, 0)
        upper = dot(normed, wu_ref[...], 1, 0)
        s = jax.nn.sigmoid(gate)
        silu = gate * s
        hidden = (silu * upper).astype(B)
        hidden_ref[r, :] = hidden
        grad_hidden = dot(g_ref[js[0] : js[-1] + 1, 0].reshape(-1, width), wd_ref[...], 1, 1)
        grad_gate = (grad_hidden * upper * s * (1.0 + gate * (1.0 - s))).astype(B)
        grad_upper = (grad_hidden * silu).astype(B)
        gu_ref[r, :ff] = grad_gate
        gu_ref[r, ff:] = grad_upper
        grad_normed = dot(grad_gate, wg_ref[...], 1, 1) + dot(grad_upper, wu_ref[...], 1, 1)
        down = dot(hidden, wd_ref[...], 1, 0)
        for a, j in enumerate(js):
            place = slot_place(jnp.bitwise_xor(me, j), order)
            gn_ref[place] = grad_normed[a * piece : (a + 1) * piece].astype(B)
            down_ref[place] = down[a * piece : (a + 1) * piece].astype(B)


def feed(c, me, pieces, outs, tokens, cotangent, gain, wg, wu, wd):
    parts, _, piece, width = tokens.shape
    chunk = parts * piece
    ff = wg.shape[1]
    part = pl.BlockSpec((parts, 1, piece, width), lambda i: (0, c, 0, 0))
    results = [
        shape((chunk, width), B),
        shape((chunk, 2 * ff), B),
        shape((chunk, ff), B),
        shape((parts, piece, width), B),
        shape((parts, piece, width), B),
        shape((piece, width), F),
    ]
    return call(
        functools.partial(feed_body, parts=parts),
        results,
        "feed",
        2 * chunk * width * (width + 6 * ff),
        grid=(1,),
        in_specs=[scalars()]
        + [resident(p.shape) for p in pieces]
        + [resident(w.shape) for w in outs]
        + [part, part]
        + [resident(a.shape) for a in (gain, wg, wu, wd)],
        out_specs=[resident(r.shape) for r in results],
    )(me, *pieces, *outs, tokens, cotangent, gain, wg, wu, wd)


def middle_back_body(me_ref, gn_ref, r1_ref, r2_ref, m_ref, g_ref, gain_ref, gm_ref, gb_ref, ga_ref):
    total = gn_ref[0].astype(F) + r1_ref[0].astype(F) + r2_ref[...].astype(F)
    middle = m_ref[...]
    factor = lax.rsqrt(jnp.mean(middle * middle, axis=1, keepdims=True) + epsilon)
    scaled = total * gain_ref[...]
    grad = (
        g_ref[0, 0].astype(F)
        + factor * scaled
        - middle * (factor * factor * factor) * jnp.mean(middle * scaled, axis=1, keepdims=True)
    )
    gm_ref[...] = grad
    gb_ref[...] = grad.astype(B)
    ga_ref[...] = jnp.sum(total * middle * factor, axis=0, keepdims=True)


def middle_back(c, me, gn, r1, r2, middle, cotangent, gain):
    piece, width = middle.shape
    fixed = lambda dims: pl.BlockSpec(dims, lambda i, m: (0,) * len(dims))
    results = [shape((piece, width), F), shape((piece, width), B), shape((1, width), F)]
    return call(
        middle_back_body,
        results,
        "middle_back",
        grid_spec=pltpu.PrefetchScalarGridSpec(
            num_scalar_prefetch=1,
            grid=(1,),
            in_specs=[
                fixed((1, piece, width)),
                fixed((1, piece, width)),
                fixed((piece, width)),
                fixed((piece, width)),
                pl.BlockSpec((1, 1, piece, width), lambda i, m: (m[0], c, 0, 0)),
                fixed((1, width)),
            ],
            out_specs=[fixed(r.shape) for r in results],
        ),
    )(me, gn, r1, r2, middle, cotangent, gain)


def branch_body(me_ref, *refs, parts, heads, distances):
    pieces = refs[: 2 * parts]
    w_ref, att0, att1, lse0, lse1, gb_ref, ship_ref, st_ref = refs[2 * parts :]
    me = me_ref[0]
    piece = pieces[0].shape[0]
    chunk = parts * piece
    columns = w_ref.shape[0]
    hd = columns // heads
    extra = padded_rows(6 * heads * (chunk // columns))
    for c, (att, lse) in enumerate(((att0, lse0), (att1, lse1))):
        for a, k in enumerate(distances):
            start = pl.multiple_of(jnp.bitwise_xor(me, k) * piece, piece)
            gb_ref[c, pl.ds(start, piece), :] = pieces[c * parts + a][...]
        grad = dot(gb_ref[c], w_ref[...], 1, 1).astype(B)
        ship_ref[c * chunk : (c + 1) * chunk, :] = grad
        product = grad.astype(F) * att[...].astype(F)
        rows = [lse[...]]
        for h in range(heads):
            rows.append(
                jnp.sum(product[:, h * hd : (h + 1) * hd].T, axis=0, keepdims=True)
            )
        stats = jnp.concatenate(rows, axis=0)
        st_ref[c] = stats
        row = 2 * chunk + c * extra
        ship_ref[row : row + extra, :] = pack_rows(stats, columns, extra)


def branch(me, pieces, distances, w_output, att, lse, heads):
    parts = len(distances)
    piece, width = pieces[0].shape
    chunk = parts * piece
    columns = w_output.shape[0]
    extra = padded_rows(6 * heads * (chunk // columns))
    return call(
        functools.partial(branch_body, parts=parts, heads=heads, distances=tuple(distances)),
        [
            shape((2, chunk, width), B),
            shape((2 * (chunk + extra), columns), B),
            shape((2, 2 * heads, chunk), F),
        ],
        "branch",
        4 * chunk * width * columns,
        in_specs=[scalars()] + [whole()] * (2 * parts + 5),
    )(me, *pieces, w_output, *att, *lse)


def store_slots(place_ref, out_ref, first, value, c):
    rows = out_ref.shape[1]
    for a in range(value.shape[0] // rows):
        out_ref[place_ref[first + a], :, c] = value[a * rows : (a + 1) * rows].astype(B)


def feed_grads_body(place_ref, n0, n1, gu0, gu1, h0, h1, g_ref, out_ref):
    block = n0.shape[1]
    per = block // out_ref.shape[1]
    first = pl.program_id(0) * per
    gu_width = gu0.shape[1]
    store_slots(
        place_ref, out_ref, first,
        dot(n0[...], gu0[...], 0, 0) + dot(n1[...], gu1[...], 0, 0), slice(0, gu_width),
    )
    g0 = g_ref[:, 0].reshape(-1, block)
    g1 = g_ref[:, 1].reshape(-1, block)
    store_slots(
        place_ref, out_ref, first,
        dot(g0, h0[...], 0, 0) + dot(g1, h1[...], 0, 0), slice(gu_width, out_ref.shape[2]),
    )


def feed_grads(place, normed, gu, hidden, cotangent, docs):
    chunk, width = normed[0].shape
    total = gu[0].shape[1] + hidden[0].shape[1]
    block = max(width // docs, 256)
    parts, _, piece, _ = cotangent.shape
    column = pl.BlockSpec((chunk, block), lambda i: (0, i))
    return call(
        feed_grads_body,
        shape((docs, width // docs, total), B),
        "feed_grads",
        4 * chunk * width * total,
        grid=(width // block,),
        in_specs=[scalars(), column, column]
        + [resident(a.shape) for a in (*gu, *hidden)]
        + [pl.BlockSpec((parts, 2, piece, block), lambda i: (0, 0, 0, i))],
        out_specs=resident((docs, width // docs, total)),
    )(place, *normed, *gu, *hidden, cotangent)


def key_grads_body(place_ref, n_ref, dkv_ref, gb_ref, att0, att1, wk_ref, wv_ref, out_ref, gn_ref):
    columns = wk_ref.shape[1]
    for c in range(2):
        gn_ref[c] = (
            dot(dkv_ref[c, :, :columns], wk_ref[...], 1, 1)
            + dot(dkv_ref[c, :, columns:], wv_ref[...], 1, 1)
        ).astype(B)
    store_slots(
        place_ref, out_ref, 0,
        dot(n_ref[0], dkv_ref[0], 0, 0) + dot(n_ref[1], dkv_ref[1], 0, 0), slice(0, 2 * columns),
    )
    store_slots(
        place_ref, out_ref, 0,
        dot(gb_ref[0], att0[...], 0, 0) + dot(gb_ref[1], att1[...], 0, 0),
        slice(2 * columns, 3 * columns),
    )


def key_grads(place, normed, dkv, gb, att, wk, wv, docs):
    _, chunk, width = normed.shape
    columns = wk.shape[1]
    return call(
        key_grads_body,
        [shape((docs, width // docs, 3 * columns), B), shape((2, chunk, width), B)],
        "key_grads",
        20 * chunk * width * columns,
        in_specs=[scalars()] + [whole()] * 7,
    )(place, normed, dkv, gb, *att, wk, wv)


def query_grads_body(
    chosen_ref, me_ref, place_ref, dq_ref, *refs, count, parts, heads
):
    ships = refs[:count]
    n_ref, part_ref, wq_ref, table_ref, x_ref = refs[count : count + 5]
    out_ref, gn_ref, gain_ref = refs[count + 5 :]
    chosen = chosen_ref[0]
    me = me_ref[0]
    _, chunk, columns = dq_ref.shape
    piece = chunk // parts
    hd = columns // heads
    width = wq_ref.shape[0]
    order = list(range(parts.bit_length() - 1))
    grads = None
    gain = None
    for c in range(2):
        far = choose(ships, (slice(c * chunk, (c + 1) * chunk), slice(None)), chosen)
        dq = dq_ref[c] + far.astype(F)
        table = table_ref[:, c].reshape(chunk, hd)
        low = jnp.concatenate(
            [rope(dq[:, h * hd : (h + 1) * hd], table, -1.0) for h in range(heads)], axis=1
        ).astype(B)
        gn = dot(low, wq_ref[...], 1, 1) + part_ref[c].astype(F)
        for j in range(parts):
            place = slot_place(jnp.bitwise_xor(me, j), order)
            gn_ref[place, c * piece : (c + 1) * piece, :] = gn[j * piece : (j + 1) * piece].astype(
                B
            )
        x = x_ref[:, c].reshape(chunk, width).astype(F)
        factor = lax.rsqrt(jnp.mean(x * x, axis=1, keepdims=True) + epsilon)
        part = jnp.sum(gn * x * factor, axis=0, keepdims=True)
        gain = part if gain is None else gain + part
        part = dot(n_ref[c], low, 0, 0)
        grads = part if grads is None else grads + part
    gain_ref[...] = gain
    store_slots(place_ref, out_ref, 0, grads, slice(0, columns))


def query_grads(chosen, me, place, dq, ships, normed, part, wq, table, tokens, docs, heads):
    _, chunk, width = normed.shape
    columns = wq.shape[1]
    parts = tokens.shape[0]
    return call(
        functools.partial(query_grads_body, count=len(ships), parts=parts, heads=heads),
        [
            shape((docs, width // docs, columns), B),
            shape((parts, 2 * chunk // parts, width), B),
            shape((1, width), F),
        ],
        "query_grads",
        8 * chunk * width * columns,
        in_specs=[scalars()] * 3 + [whole()] * (len(ships) + 6),
    )(chosen, me, place, dq, *ships, normed, part, wq, table, tokens)


def tokens_back_body(me_ref, gn_ref, r1_ref, r2_ref, x_ref, gm0, gm1, gain_ref, out_ref):
    total = gn_ref[0].astype(F) + r1_ref[0].astype(F) + r2_ref[...].astype(F)
    x = x_ref[...].astype(F)
    factor = lax.rsqrt(jnp.mean(x * x, axis=1, keepdims=True) + epsilon)
    scaled = total * gain_ref[...]
    grad = factor * scaled - x * (factor * factor * factor) * jnp.mean(
        x * scaled, axis=1, keepdims=True
    )
    piece = gm0.shape[0]
    out_ref[:piece, :] = (gm0[...] + grad[:piece]).astype(B)
    out_ref[piece:, :] = (gm1[...] + grad[piece:]).astype(B)


def tokens_back(me, gn, r1, r2, tokens, gm, gain):
    _, share, width = gn.shape
    fixed = lambda dims: pl.BlockSpec(dims, lambda i, m: (0,) * len(dims))
    return call(
        tokens_back_body,
        shape((share, width), B),
        "tokens_back",
        grid_spec=pltpu.PrefetchScalarGridSpec(
            num_scalar_prefetch=1,
            grid=(1,),
            in_specs=[
                fixed((1, share, width)),
                fixed((1, share, width)),
                fixed((share, width)),
                pl.BlockSpec((share, width), lambda i, m: (m[0], 0)),
                fixed(gm[0].shape),
                fixed(gm[1].shape),
                fixed((1, width)),
            ],
            out_specs=fixed((share, width)),
        ),
    )(me, gn, r1, r2, tokens, *gm, gain)


def rotate_table(length, hd):
    half = hd // 2
    position = np.arange(length, dtype=np.float32)
    inverse = np.exp(
        -np.log(np.float32(10000.0)) * np.arange(half, dtype=np.float32) * np.float32(2.0) / hd
    ).astype(np.float32)
    angles = position[:, None] * inverse[None, :]
    return jnp.asarray(np.concatenate([np.cos(angles), np.sin(angles)], axis=1).astype(np.float32))


def to_all(array):
    bits = axis_bits("dp")
    got = {b: swap(array, "dp", 1 << b) for b in reversed(range(bits))}
    return [got[b] for b in range(bits)]


def gather_tensor(value):
    pieces, distances = [value], [0]
    for b in reversed(range(axis_bits("tensor"))):
        pieces = pieces + [swap(p, "tensor", 1 << b) for p in pieces]
        distances = distances + [k ^ (1 << b) for k in distances]
    return pieces, distances


def halve(value, axis, bit):
    half = value.shape[0] // 2
    return swap(value[half:], axis, 1 << bit)


def add_low(a, b):
    return (a.astype(F) + b.astype(F)).astype(B)


def scatter_slots(value, axis, order):
    for b in order:
        half = value.shape[0] // 2
        got = halve(value, axis, b)
        if half == 1:
            return value[0].astype(F) + got[0].astype(F)
        value = add_low(value[:half], got)
    return value[0].astype(F)


def scatter_two(value):
    first = halve(value, "tensor", 0)
    second = swap(add_low(value[1], first[1]), "tensor", 2)
    return first, second


def per_device(
    tokens,
    w_query,
    w_key,
    w_value,
    w_output,
    w_gate,
    w_up,
    w_down,
    gain_attn,
    gain_mlp,
    cache_keys,
    cache_values,
    knn_index,
    memory_flag,
    pairing,
    cotangent,
):
    length, width = tokens.shape
    parts = lax.axis_size("tensor")
    docs = lax.axis_size("dp")
    piece = length // parts // 2
    me = lax.axis_index("tensor").astype(jnp.int32).reshape(1)
    heads = cache_keys.shape[1]
    rows = cache_keys.shape[2]
    hd = cache_keys.shape[3]
    columns = heads * hd
    groups = knn_index.shape[1] // 2
    spread = rows // groups
    ff = w_gate.shape[1]
    flag = memory_flag[:1].astype(jnp.int32)
    my_doc = lax.axis_index("dp").astype(jnp.int32)
    difference = jnp.bitwise_xor(pairing[0].astype(jnp.int32), my_doc)
    chosen = jnp.zeros((), jnp.int32)
    for b in range(1, axis_bits("dp")):
        chosen = jnp.where(difference == (1 << b), b, chosen)
    chosen = chosen.reshape(1)
    dp_order = list(range(axis_bits("dp")))
    place = slot_place(jnp.bitwise_xor(jnp.arange(docs, dtype=jnp.int32), my_doc), dp_order)
    place = place.astype(jnp.int32)
    table = rotate_table(length, hd)
    gain_a = gain_attn.reshape(1, width)
    gain_m = gain_mlp.reshape(1, width)
    tokens_view = tokens.reshape(parts, 2, piece, width)
    cotangent_view = cotangent.reshape(parts, 2, piece, width)
    table_view = table.reshape(parts, 2, piece, hd)

    def ordered_rows(cache):
        return (
            cache.reshape(heads, groups // GROUP_BLOCK, GROUP_BLOCK, spread, hd)
            .transpose(0, 1, 3, 2, 4)
            .reshape(heads, rows, hd)
        )

    ship, q, k, v, normed_low, own_off = project(
        flag, tokens, knn_index, gain_a, w_query, w_key, w_value, table, parts, heads, spread
    )
    ships = to_all(ship)
    out_weights, distances = gather_tensor(w_output)
    stored_keys = ordered_rows(cache_keys[0])
    stored_values = ordered_rows(cache_values[0])
    local = local_forward(q, k, v, heads, parts)
    own_out, own_lse, own_sel = own_attend(
        flag, ship, own_off, stored_keys, stored_values, spread
    )
    att, lse, their_sel, their_off, feeds = [], [], [], [], []
    gm, gb_pieces, gain_parts = [], [], []
    returned = []
    for c in range(2):
        packed, sel, off, their_flag = their_attend(
            c, chosen, ships, stored_keys, stored_values, spread, groups
        )
        their_sel.append(sel)
        their_off.append(off)
        returned.append(to_all(packed))
    for c in range(2):
        a, total = merge(c, chosen, local, (own_out, own_lse), returned[c], heads)
        att.append(a)
        lse.append(total)

        pieces, _ = gather_tensor(a)
        feeds.append(
            feed(
                c, me, pieces, out_weights, tokens_view, cotangent_view, gain_m, w_gate, w_up,
                w_down,
            )
        )
    for c in range(2):
        gn, middle = feeds[c][3], feeds[c][5]
        first, second = scatter_two(gn)
        grad_middle, low, gain_part = middle_back(
            c, me, gn, first, second, middle, cotangent_view, gain_m
        )
        gm.append(grad_middle)
        gain_parts.append(gain_part)
        gb_pieces += gather_tensor(low)[0]

    grad_branch, back_ship, stats = branch(me, gb_pieces, distances, w_output, att, lse, heads)
    back_ships = to_all(back_ship)
    local_dq, dkv = local_backward(q, k, v, back_ship, stats, table, heads, parts)
    dq = own_backward(
        flag, back_ship, stats, own_sel, own_off, stored_keys, stored_values, local_dq, spread
    )
    their_dq = their_backward(
        chosen, their_flag, back_ships, their_sel, their_off, stored_keys, stored_values, spread
    )
    dq_ships = to_all(their_dq)

    feed_sum = scatter_slots(
        feed_grads(
            place,
            [f[0] for f in feeds],
            [f[1] for f in feeds],
            [f[2] for f in feeds],
            cotangent_view,
            docs,
        ),
        "dp",
        dp_order,
    )
    output = []
    for c in range(2):
        down = feeds[c][4]
        first, second = scatter_two(down)
        output.append(
            feeds[c][5] + down[0].astype(F) + first[0].astype(F) + second.astype(F)
        )

    key_slots, gn_part = key_grads(
        place, normed_low, dkv, grad_branch, att, w_key, w_value, docs
    )
    key_sum = scatter_slots(key_slots, "dp", dp_order)
    query_slots, gn, gain_part = query_grads(
        chosen, me, place, dq, dq_ships, normed_low, gn_part, w_query, table_view, tokens_view,
        docs, heads
    )
    query_sum = scatter_slots(query_slots, "dp", dp_order)
    first, second = scatter_two(gn)
    grad_tokens = tokens_back(me, gn, first, second, tokens, gm, gain_a)
    gains = jnp.concatenate([gain_part, gain_parts[0] + gain_parts[1]], axis=0)
    gains = gains + sum(swap(gains, "tensor", t) for t in range(1, parts))
    for b in dp_order:
        gains = gains + swap(gains, "dp", 1 << b)
    gains = lax.dynamic_slice_in_dim(gains, my_doc * (width // docs), width // docs, 1)
    return (
        jnp.concatenate(output, axis=0).astype(B),
        grad_tokens,
        query_sum,
        key_sum[:, :columns],
        key_sum[:, columns : 2 * columns],
        key_sum[:, 2 * columns :].T,
        feed_sum[:, :ff],
        feed_sum[:, ff : 2 * ff],
        feed_sum[:, 2 * ff :].T,
        gains[0],
        gains[1],
    )


def solution(mesh):
    placed = (
        P("dp", None),
        P(None, "tensor"),
        P(None, "tensor"),
        P(None, "tensor"),
        P("tensor", None),
        P(None, "tensor"),
        P(None, "tensor"),
        P("tensor", None),
        P(),
        P(),
        P("dp", "tensor", None, None),
        P("dp", "tensor", None, None),
        P("dp", None),
        P("dp"),
        P("dp"),
        P("dp", None),
    )
    return jax.shard_map(
        per_device,
        mesh=mesh,
        in_specs=placed,
        out_specs=(
            P(("dp", "tensor"), None),
            P(("dp", "tensor"), None),
            P("dp", "tensor"),
            P("dp", "tensor"),
            P("dp", "tensor"),
            P("tensor", "dp"),
            P("dp", "tensor"),
            P("dp", "tensor"),
            P("tensor", "dp"),
            P("dp"),
            P("dp"),
        ),
        check_vma=False,
    )
```

time: 540 us -> 384 us (0.71)
  local copies, waits for them, and re-layouts: 158 us -> 39 us
  Pallas kernels: 41.2 us -> 130 us
  waiting for transfers between devices: 173 us -> 122 us
  matrix products: 48.6 us -> 0 us
  other arithmetic: 50.4 us -> 22.6 us
  starting transfers between devices: 56.9 us -> 65 us
    pallas_call x6 -> x19, Pallas kernels: 41.2 us -> 130 us  [the longest x2 34.8 us: feed(): call(functools.partial(feed_body, parts=parts), results, 'feed', 2 * chun...]
    ppermute x47 -> x55, waiting for transfers between devices: 173 us -> 122 us  [swap(): lax.ppermute(array, axis, [(i, i ^ bit) for i in range(lax.axis_size(axis...]
    dot_general x24 -> x0, matrix products: 48.6 us -> none  [dot(): lax.dot_general(a, b, (((da,), (db,)), ((), ())), preferred_element_type=F)]
    dynamic_slice x14 -> x0, local copies, waits for them, and re-layouts: 47.3 us -> none  [the longest x9 33 us: scatter_sum(): keep = lax.dynamic_index_in_dim(value, mine, where, keepdims=False)]
    unnamed x150 -> x66, local copies, waits for them, and re-layouts: 41.5 us -> 12.3 us
    another operation x4 -> x0, local copies, waits for them, and re-layouts: 19.1 us -> none  [the longest x2 19 us: scatter_sum(): value = value.reshape((2,) * bits + tail)]
    mul x4 -> x0, local copies, waits for them, and re-layouts: 14.9 us -> none  [the longest x3 14.5 us: weighted(): return out.reshape(length, heads, hd).astype(F) * weight[:, :, None]]
    convert_element_type x7 -> x11, other arithmetic: 4.7 us -> 14.8 us  [add_low(): return (a.astype(F) + b.astype(F)).astype(B)]
  transfers between devices with their start and end apart: 47 -> 55, of which waited for: 14 -> 16; matrix products, arithmetic and copies ran while one was open for 34% -> 14% of each run, Pallas kernels for 7% -> 32%
where the time goes in v2:
time: 384 us; the launch traced here: 380 us
  Pallas kernels  130 us (34%)
  waiting for transfers between devices  122 us (32%)
  starting transfers between devices  65 us (17%)
  local copies, waits for them, and re-layouts  39 us (10%)
  other arithmetic  22.6 us (6%)
    ppermute x55, waiting for transfers between devices, swap(): lax.ppermute(array, axis, [(i, i ^ bit) for i in range(lax.axis_size(axis...  122 us
    ppermute x55, starting transfers between devices, swap(): lax.ppermute(array, axis, [(i, i ^ bit) for i in range(lax.axis_size(axis...  65 us
    pallas_call x2, Pallas kernels, feed(): call(functools.partial(feed_body, parts=parts), results, 'feed', 2 * chun...  34.8 us
    slice x18, local copies, waits for them, and re-layouts, halve(): return swap(value[half:], axis, 1 << bit)  15.3 us
    convert_element_type x11, other arithmetic, add_low(): return (a.astype(F) + b.astype(F)).astype(B)  14.8 us
    unnamed x66, local copies, waits for them, and re-layouts  12.3 us
    pallas_call x1, Pallas kernels, feed_grads(): call(feed_grads_body, shape((docs, width // docs, total), B), 'feed_grads...  11.1 us
    pallas_call x1, Pallas kernels, own_backward(): call(functools.partial(own_backward_body, spread=spread), shape((2, chunk...  10.7 us
  transfers between devices with their start and end apart: 55, of which 16 were waited for; matrix products, arithmetic and copies ran while one was open for 14% of the time, Pallas kernels for 32%

profile of v2, /device:TPU:0, one launch (start us, length us, event | category | flops | bytes accessed | tf_op | source)
XLA Modules:
  0.0 380.4 jit_solution(16262088704799046594)
XLA Ops:
  1.3 6.6 %project.1 = (bf16[2,640,256]{2,1,0:T(8,128)(2,1)}, bf16[1024,256]{1,0:T(8,128)(2,1)}, bf16[1024,256]{1,0:T(8,128)(2,1)}, bf16[1024,256]{1,0:T(8,128)(2,1)}, bf1...) custom-call(s32[1]{0:T(128)S(6)} %copy.54.flag_ref, bf16[1024,1024]{1,0:T(8,128)(2,1)} %x_ref.3, ...), custom_call_target="tpu_custom_call" | custom-call | flops 1610612736 | bytes 4026531 | tf_op jit(solution)/shard_map/project/pallas_call | solution.py:158
  25.8 15.5 %collective-permute-done.1.refs_1_ = bf16[2,640,256]{2,1,0:T(8,128)(2,1)} collective-permute-done((bf16[2,640,256]{2,1,0:T(8,128)(2,1)}, bf16[2,640,256]{2,1,0:T(8,128)(2,1)}, u32[]{:S(2)}, u32[]{:S(2)}) %collective-permute-start.1) | collective-permute-done | bytes 655392 | tf_op jit(solution)/shard_map/ppermute | solution.py:23
  47.8 3.9 %collective-permute-start.4 = (bf16[528,256]{1,0:T(8,128)(2,1)}, bf16[528,256]{1,0:T(8,128)(2,1)S(1)}, u32[]{:S(2)}, u32[]{:S(2)}) collective-permute-start(bf16[528,256]{1,0:T(8,128)(2,1)} %get-tuple-element.70), channel_id=1, source_target_pairs={{0,8},{4,12},{8,0},{12,4},{16,24},{20,28},{24,16},{28,20},{1,9},{5... | collective-permute-start | bytes 811016 | tf_op jit(solution)/shard_map/ppermute | solution.py:23
  53.9 3.8 their_attend.3
  59.7 10.4 %own_attend.1 = (bf16[2,512,256]{2,1,0:T(8,128)(2,1)}, f32[2,2,512]{2,1,0:T(2,128)}, f32[2,2,64,512]{3,2,1,0:T(8,128)}) custom-call(s32[1]{0:T(128)S(6)} %copy.54.flag_ref, bf16[2,640,256]{2,1,0:T(8,128)(2,1)} %get-tuple-element.66.ship_ref, bf16[2,64,512]{2,1,0:T(8,128)(2,1)} %get-tuple-element.67.off_ref, bf16[2,4096,128]{2,1,0:T(8,128)(2,1)} %bitcast.68, ...), custom_call_target="tpu_custom_call" | custom-call | flops 8589934592 | bytes 21474836 | tf_op jit(solution)/shard_map/own_attend/pallas_call | solution.py:259
  70.1 3.9 %collective-permute-start.16 = (bf16[528,256]{1,0:T(8,128)(2,1)}, bf16[528,256]{1,0:T(8,128)(2,1)}, u32[]{:S(2)}, u32[]{:S(2)}) collective-permute-start(bf16[528,256]{1,0:T(8,128)(2,1)} %get-tuple-element.74), channel_id=1, source_target_pairs={{0,16},{4,20},{8,24},{12,28},{16,0},{20,4},{24,8},{28,12},{1,17},{... | collective-permute-start | bytes 811016 | tf_op jit(solution)/shard_map/ppermute | solution.py:23
  74.1 5.6 %local_forward.1 = (bf16[2,512,256]{2,1,0:T(8,128)(2,1)}, f32[2,2,512]{2,1,0:T(2,128)}) custom-call(bf16[1024,256]{1,0:T(8,128)(2,1)} %get-tuple-element.61.q_ref, bf16[1024,256]{1,0:T(8,128)(2,1)} %get-tuple-element.62.k_ref, bf16[1024,256]{1,0:T(8,128)(2,1)} %get-tuple-element.63.v_ref), custom_call_target="tpu_custom_call" | custom-call | flops 1073741824 | bytes 2684354 | tf_op jit(solution)/shard_map/local_forward/pallas_call | solution.py:489
  88.5 4.8 %collective-permute-done.6.refs_1_ = bf16[512,256]{1,0:T(8,128)(2,1)} collective-permute-done((bf16[512,256]{1,0:T(8,128)(2,1)}, bf16[512,256]{1,0:T(8,128)(2,1)}, u32[]{:S(2)}, u32[]{:S(2)}) %collective-permute-start.6) | collective-permute-done | bytes 262176 | tf_op jit(solution)/shard_map/ppermute | solution.py:23
  98.5 22.4 %feed.2 = (bf16[512,1024]{1,0:T(8,128)(2,1)}, bf16[512,1408]{1,0:T(8,128)(2,1)}, bf16[512,704]{1,0:T(8,128)(2,1)}, bf16[4,128,1024]{2,1,0:T(8,128)(2,1)}, bf16[4...) custom-call(s32[1]{0:T(128)} %bitcast.me_ref, bf16[512,256]{1,0:T(8,128)(2,1)} %get-tuple-element.71.refs_0_.refs_9_.att0, ...), custom_call_target="tpu_custom_call" | custom-call | flops 5502926848 | bytes 13757317 | tf_op jit(solution)/shard_map/feed/pallas_call | solution.py:654
  124.0 12.4 %feed.3 = (bf16[512,1024]{1,0:T(8,128)(2,1)}, bf16[512,1408]{1,0:T(8,128)(2,1)}, bf16[512,704]{1,0:T(8,128)(2,1)}, bf16[4,128,1024]{2,1,0:T(8,128)(2,1)}, bf16[4...) custom-call(s32[1]{0:T(128)} %bitcast.me_ref, bf16[512,256]{1,0:T(8,128)(2,1)} %get-tuple-element.75.refs_0_.refs_10_.att1, ...), custom_call_target="tpu_custom_call" | custom-call | flops 5502926848 | bytes 13757317 | tf_op jit(solution)/shard_map/feed/pallas_call | solution.py:654
  143.7 5.9 %collective-permute-done.23.r2_ref = bf16[128,1024]{1,0:T(8,128)(2,1)S(1)} collective-permute-done((bf16[128,1024]{1,0:T(8,128)(2,1)S(1)}, bf16[128,1024]{1,0:T(8,128)(2,1)S(1)}, u32[]{:S(2)}, u32[]{:S(2)}) %collective-permute-start.23) | collective-permute-done | bytes 262176 | tf_op jit(solution)/shard_map/ppermute | solution.py:23
  161.9 3.7 collective-permute-done.29.refs_5_
  165.6 11.1 %feed_grads.1 = bf16[8,128,2112]{2,1,0:T(8,128)(2,1)} custom-call(s32[8]{0:T(128)} %and_add_fusion.place_ref, bf16[512,1024]{1,0:T(8,128)(2,1)} %get-tuple-element.102.n0, bf16[512,1024]{1,0:T(8,128)(2,1)} %get-tuple-element.103.n1, bf16[512,1408]{1,0:T(8,128)(2,1)} %get-tuple-element.104.gu0, bf16[512,1408]{1,0:T(8,128)(2,1)} %get-tuple-element.105.gu1, ...), custom_call_target="tpu_custom_call" | custom-call | flops 4429185024 | bytes 11072962 | tf_op jit(solution)/shard_map/feed_grads/pallas_call | solution.py:783
  184.5 3.7 branch.1
  196.0 7.2 %local_backward.1 = (f32[2,512,256]{2,1,0:T(8,128)}, bf16[2,512,512]{2,1,0:T(8,128)(2,1)}) custom-call(bf16[1024,256]{1,0:T(8,128)(2,1)} %get-tuple-element.61.q_ref, bf16[1024,256]{1,0:T(8,128)(2,1)} %get-tuple-element.62.k_ref, bf16[1024,256]{1,0:T(8,128)(2,1)} %get-tuple-element.63.v_ref, bf16[1088,256]{1,0:T(8,128)(2,1)} %get-tuple-element.84.ship_ref, ...), custom_call_target="tpu_custom_call" | custom-call | flops 2684354560 | bytes 6710886 | tf_op jit(solution)/shard_map/local_backward/pallas_call | solution.py:547
  203.2 41.0 %collective-permute-done.32.refs_0_ = bf16[1088,256]{1,0:T(8,128)(2,1)} collective-permute-done((bf16[1088,256]{1,0:T(8,128)(2,1)}, bf16[1088,256]{1,0:T(8,128)(2,1)}, u32[]{:S(2)}, u32[]{:S(2)}) %collective-permute-start.32) | collective-permute-done | bytes 557088 | tf_op jit(solution)/shard_map/ppermute | solution.py:23
  244.2 4.6 %their_backward.1 = bf16[1024,256]{1,0:T(8,128)(2,1)} custom-call(s32[1]{0:T(128)} %bitcast.2.chosen_ref, s32[1]{0:T(128)} %get-tuple-element.88.flag_ref, bf16[1088,256]{1,0:T(8,128)(2,1)} %collective-permute-done.32.refs_0_, bf16[1088,256]{1,0:T(8,128)(2,1)} %collective-permute-done.33.refs_1_, bf16[1088,256]{1,0:T(8,128)(2,1)} %collective-permute-done.34.refs_2_, ...), custom_call_target="tpu_custom_call" | custom-call | flops 8589934592 | bytes 21474836 | tf_op jit(solution)/shard_map/their_backward/pallas_call | solution.py:448
  249.2 8.6 %collective-permute-start.36 = (bf16[1024,256]{1,0:T(8,128)(2,1)}, bf16[1024,256]{1,0:T(8,128)(2,1)}, u32[]{:S(2)}, u32[]{:S(2)}) collective-permute-start(bf16[1024,256]{1,0:T(8,128)(2,1)} %their_backward.1), channel_id=1, source_target_pairs={{0,8},{4,12},{8,0},{12,4},{16,24},{20,28},{24,16},{28,20},{1,9},{5... | collective-permute-start | bytes 1572872 | tf_op jit(solution)/shard_map/ppermute | solution.py:23
  257.8 10.7 %own_backward.1.dq_ref = f32[2,512,256]{2,1,0:T(8,128)} custom-call(s32[1]{0:T(128)S(6)} %copy.54.flag_ref, bf16[1088,256]{1,0:T(8,128)(2,1)} %get-tuple-element.84.ship_ref, f32[2,4,512]{2,1,0:T(4,128)} %get-tuple-element.85.st_ref, f32[2,2,64,512]{3,2,1,0:T(8,128)} %get-tuple-element.86.sel_ref, bf16[2,64,512]{2,1,0:T(8,128)(2,1)} %get-tuple-element.67.off_ref, ...), custom_call_target="tpu_custom_call" | custom-call | flops 8589934592 | bytes 21474836 | tf_op jit(solution)/shard_map/own_backward/pallas_call | solution.py:391
  268.5 7.0 %key_grads.1 = (bf16[8,128,768]{2,1,0:T(8,128)(2,1)}, bf16[2,512,1024]{2,1,0:T(8,128)(2,1)}) custom-call(s32[8]{0:T(128)} %and_add_fusion.place_ref, bf16[2,512,1024]{2,1,0:T(8,128)(2,1)} %get-tuple-element.93.n_ref.refs_3_, bf16[2,512,512]{2,1,0:T(8,128)(2,1)} %get-tuple-element.94.dkv_ref, bf16[2,512,1024]{2,1,0:T(8,128)(2,1)} %get-tuple-element.95.gb_ref, ...), custom_call_target="tpu_custom_call" | custom-call | flops 2684354560 | bytes 6710886 | tf_op jit(solution)/shard_map/key_grads/pallas_call | solution.py:817
  279.5 4.1 %collective-permute-done.37.refs_2_ = bf16[1024,256]{1,0:T(8,128)(2,1)} collective-permute-done((bf16[1024,256]{1,0:T(8,128)(2,1)}, bf16[1024,256]{1,0:T(8,128)(2,1)}, u32[]{:S(2)}, u32[]{:S(2)}) %collective-permute-start.37) | collective-permute-done | bytes 524320 | tf_op jit(solution)/shard_map/ppermute | solution.py:23
  283.5 7.1 %query_grads.1 = (bf16[8,128,256]{2,1,0:T(8,128)(2,1)}, bf16[4,256,1024]{2,1,0:T(8,128)(2,1)}, f32[1,1024]{1,0:T(1,128)}) custom-call(s32[1]{0:T(128)} %bitcast.2.chosen_ref, s32[1]{0:T(128)} %bitcast.me_ref, s32[8]{0:T(128)} %and_add_fusion.place_ref, f32[2,512,256]{2,1,0:T(8,128)} %own_backward.1.dq_ref, bf16[1024,256]{1,0:T(8,128)(2,1)} %copy-done.16, ...), custom_call_target="tpu_custom_call" | custom-call | flops 1073741824 | bytes 2684354 | tf_op jit(solution)/shard_map/query_grads/pallas_call | solution.py:868
  327.1 14.6 %collective-permute-done.45 = bf16[1,128,768]{2,1,0:T(8,128)(2,1)S(1)} collective-permute-done((bf16[1,128,768]{2,1,0:T(8,128)(2,1)S(1)}, bf16[1,128,768]{2,1,0:T(8,128)(2,1)S(1)}, u32[]{:S(2)}, u32[]{:S(2)}) %collective-permute-start.45) | collective-permute-done | bytes 196640 | tf_op jit(solution)/shard_map/ppermute | solution.py:23
  356.6 17.1 %collective-permute-done.48 = bf16[1,128,2112]{1,2,0:T(8,128)(2,1)S(1)} collective-permute-done((bf16[1,128,2112]{1,2,0:T(8,128)(2,1)S(1)}, bf16[1,128,2112]{1,2,0:T(8,128)(2,1)S(1)}, u32[]{:S(2)}, u32[]{:S(2)}) %collective-permute-start.48) | collective-permute-done | bytes 540704 | tf_op jit(solution)/shard_map/ppermute | solution.py:23
  (221 shorter events, 142.4 us)
Async XLA Ops:
  10.9 30.4 %collective-permute-start.1 = (bf16[2,640,256]{2,1,0:T(8,128)(2,1)}, bf16[2,640,256]{2,1,0:T(8,128)(2,1)}, u32[]{:S(2)}, u32[]{:S(2)}) collective-permute-start(bf16[2,640,256]{2,1,0:T(8,128)(2,1)} %get-tuple-element.66.ship_ref), channel_id=1, source_target_pairs={{0,8},{4,12},{8,0},{12,4},{16,24},{20,28},{24,16},{28,20},{1,9},{5... | collective-permute-start | bytes 1966088 | tf_op jit(solution)/shard_map/ppermute | solution.py:23
  12.4 31.2 %collective-permute-start.2 = (bf16[2,640,256]{2,1,0:T(8,128)(2,1)}, bf16[2,640,256]{2,1,0:T(8,128)(2,1)}, u32[]{:S(2)}, u32[]{:S(2)}) collective-permute-start(bf16[2,640,256]{2,1,0:T(8,128)(2,1)} %get-tuple-element.66.ship_ref), channel_id=1, source_target_pairs={{0,16},{4,20},{8,24},{12,28},{16,0},{20,4},{24,8},{28,12},{1,17},{... | collective-permute-start | bytes 1966088 | tf_op jit(solution)/shard_map/ppermute | solution.py:23
  15.0 55.0 %collective-permute-start.9 = (bf16[256,1024]{1,0:T(8,128)(2,1)S(1)}, bf16[256,1024]{1,0:T(8,128)(2,1)}, u32[]{:S(2)}, u32[]{:S(2)}) collective-permute-start(bf16[256,1024]{1,0:T(8,128)(2,1)S(1)} %copy-done.15), channel_id=1, source_target_pairs={{0,2},{1,3},{2,0},{3,1},{4,6},{5,7},{6,4},{7,5},{8,10},{9,11},{10,... | collective-permute-start | bytes 1572872 | tf_op jit(solution)/shard_map/ppermute | solution.py:23
  47.2 22.9 %collective-permute-start.3 = (bf16[528,256]{1,0:T(8,128)(2,1)}, bf16[528,256]{1,0:T(8,128)(2,1)S(1)}, u32[]{:S(2)}, u32[]{:S(2)}) collective-permute-start(bf16[528,256]{1,0:T(8,128)(2,1)} %get-tuple-element.70), channel_id=1, source_target_pairs={{0,4},{4,0},{8,12},{12,8},{16,20},{20,16},{24,28},{28,24},{1,5},{5... | collective-permute-start | bytes 811016 | tf_op jit(solution)/shard_map/ppermute | solution.py:23
  47.8 31.8 %collective-permute-start.4 = (bf16[528,256]{1,0:T(8,128)(2,1)}, bf16[528,256]{1,0:T(8,128)(2,1)S(1)}, u32[]{:S(2)}, u32[]{:S(2)}) collective-permute-start(bf16[528,256]{1,0:T(8,128)(2,1)} %get-tuple-element.70), channel_id=1, source_target_pairs={{0,8},{4,12},{8,0},{12,4},{16,24},{20,28},{24,16},{28,20},{1,9},{5... | collective-permute-start | bytes 811016 | tf_op jit(solution)/shard_map/ppermute | solution.py:23
  51.7 28.0 %collective-permute-start.5 = (bf16[528,256]{1,0:T(8,128)(2,1)}, bf16[528,256]{1,0:T(8,128)(2,1)S(1)}, u32[]{:S(2)}, u32[]{:S(2)}) collective-permute-start(bf16[528,256]{1,0:T(8,128)(2,1)} %get-tuple-element.70), channel_id=1, source_target_pairs={{0,16},{4,20},{8,24},{12,28},{16,0},{20,4},{24,8},{28,12},{1,17},{... | collective-permute-start | bytes 811016 | tf_op jit(solution)/shard_map/ppermute | solution.py:23
  57.7 25.4 %collective-permute-start.14 = (bf16[528,256]{1,0:T(8,128)(2,1)}, bf16[528,256]{1,0:T(8,128)(2,1)S(1)}, u32[]{:S(2)}, u32[]{:S(2)}) collective-permute-start(bf16[528,256]{1,0:T(8,128)(2,1)} %get-tuple-element.74), channel_id=1, source_target_pairs={{0,4},{4,0},{8,12},{12,8},{16,20},{20,16},{24,28},{28,24},{1,5},{5... | collective-permute-start | bytes 811016 | tf_op jit(solution)/shard_map/ppermute | solution.py:23
  96.5 26.1 %collective-permute-start.18 = (bf16[512,256]{1,0:T(8,128)(2,1)S(1)}, bf16[512,256]{1,0:T(8,128)(2,1)S(1)}, u32[]{:S(2)}, u32[]{:S(2)}) collective-permute-start(bf16[512,256]{1,0:T(8,128)(2,1)S(1)} %copy-done.22), channel_id=1, source_target_pairs={{0,1},{1,0},{2,3},{3,2},{4,5},{5,4},{6,7},{7,6},{8,9},{9,8},{10,11... | collective-permute-start | bytes 786440 | tf_op jit(solution)/shard_map/ppermute | solution.py:23
  98.4 24.1 %collective-permute-start.19 = (bf16[512,256]{1,0:T(8,128)(2,1)}, bf16[512,256]{1,0:T(8,128)(2,1)S(1)}, u32[]{:S(2)}, u32[]{:S(2)}) collective-permute-start(bf16[512,256]{1,0:T(8,128)(2,1)} %collective-permute-done.17.refs_1_), channel_id=1, source_target_pairs={{0,1},{1,0},{2,3},{3,2},{4,5},{5,4},{6,7},{7,6},{8,9},{9,8},{10,11... | collective-permute-start | bytes 786440 | tf_op jit(solution)/shard_map/ppermute | solution.py:23
  138.6 22.8 %collective-permute-start.20 = (bf16[2,128,1024]{2,1,0:T(8,128)(2,1)S(1)}, bf16[2,128,1024]{2,1,0:T(8,128)(2,1)S(1)}, u32[]{:S(2)}, u32[]{:S(2)}) collective-permute-start(bf16[2,128,1024]{2,1,0:T(8,128)(2,1)S(1)} %slice.141), channel_id=1, source_target_pairs={{0,1},{1,0},{2,3},{3,2},{4,5},{5,4},{6,7},{7,6},{8,9},{9,8},{10,11... | collective-permute-start | bytes 1572872 | tf_op jit(solution)/shard_map/ppermute | solution.py:23
  160.9 30.8 %collective-permute-start.12 = (bf16[2,128,1024]{2,1,0:T(8,128)(2,1)}, bf16[2,128,1024]{2,1,0:T(8,128)(2,1)S(1)}, u32[]{:S(2)}, u32[]{:S(2)}) collective-permute-start(bf16[2,128,1024]{2,1,0:T(8,128)(2,1)} %slice.136), channel_id=1, source_target_pairs={{0,1},{1,0},{2,3},{3,2},{4,5},{5,4},{6,7},{7,6},{8,9},{9,8},{10,11... | collective-permute-start | bytes 1572872 | tf_op jit(solution)/shard_map/ppermute | solution.py:23
  161.5 23.0 %collective-permute-start.26 = (bf16[128,1024]{1,0:T(8,128)(2,1)}, bf16[128,1024]{1,0:T(8,128)(2,1)}, u32[]{:S(2)}, u32[]{:S(2)}) collective-permute-start(bf16[128,1024]{1,0:T(8,128)(2,1)} %collective-permute-done.24.refs_1_), channel_id=1, source_target_pairs={{0,1},{1,0},{2,3},{3,2},{4,5},{5,4},{6,7},{7,6},{8,9},{9,8},{10,11... | collective-permute-start | bytes 786440 | tf_op jit(solution)/shard_map/ppermute | solution.py:23
  182.4 123.7 %collective-permute-start.46 = (bf16[4,128,2112]{1,2,0:T(8,128)(2,1)}, bf16[4,128,2112]{1,2,0:T(8,128)(2,1)S(1)}, u32[]{:S(2)}, u32[]{:S(2)}) collective-permute-start(bf16[4,128,2112]{1,2,0:T(8,128)(2,1)} %copy.44), channel_id=1, source_target_pairs={{0,4},{4,0},{8,12},{12,8},{16,20},{20,16},{24,28},{28,24},{1,5},{5... | collective-permute-start | bytes 6488072 | tf_op jit(solution)/shard_map/ppermute | solution.py:23
  188.2 56.0 %collective-permute-start.32 = (bf16[1088,256]{1,0:T(8,128)(2,1)}, bf16[1088,256]{1,0:T(8,128)(2,1)}, u32[]{:S(2)}, u32[]{:S(2)}) collective-permute-start(bf16[1088,256]{1,0:T(8,128)(2,1)} %get-tuple-element.84.ship_ref), channel_id=1, source_target_pairs={{0,4},{4,0},{8,12},{12,8},{16,20},{20,16},{24,28},{28,24},{1,5},{5... | collective-permute-start | bytes 1671176 | tf_op jit(solution)/shard_map/ppermute | solution.py:23
  189.8 54.4 %collective-permute-start.33 = (bf16[1088,256]{1,0:T(8,128)(2,1)}, bf16[1088,256]{1,0:T(8,128)(2,1)}, u32[]{:S(2)}, u32[]{:S(2)}) collective-permute-start(bf16[1088,256]{1,0:T(8,128)(2,1)} %get-tuple-element.84.ship_ref), channel_id=1, source_target_pairs={{0,8},{4,12},{8,0},{12,4},{16,24},{20,28},{24,16},{28,20},{1,9},{5... | collective-permute-start | bytes 1671176 | tf_op jit(solution)/shard_map/ppermute | solution.py:23
  191.7 52.5 %collective-permute-start.34 = (bf16[1088,256]{1,0:T(8,128)(2,1)}, bf16[1088,256]{1,0:T(8,128)(2,1)}, u32[]{:S(2)}, u32[]{:S(2)}) collective-permute-start(bf16[1088,256]{1,0:T(8,128)(2,1)} %get-tuple-element.84.ship_ref), channel_id=1, source_target_pairs={{0,16},{4,20},{8,24},{12,28},{16,0},{20,4},{24,8},{28,12},{1,17},{... | collective-permute-start | bytes 1671176 | tf_op jit(solution)/shard_map/ppermute | solution.py:23
  194.3 98.8 %collective-permute-start.13 = (bf16[128,1024]{1,0:T(8,128)(2,1)}, bf16[128,1024]{1,0:T(8,128)(2,1)}, u32[]{:S(2)}, u32[]{:S(2)}) collective-permute-start(bf16[128,1024]{1,0:T(8,128)(2,1)} %fusion.5), channel_id=1, source_target_pairs={{0,2},{1,3},{2,0},{3,1},{4,6},{5,7},{6,4},{7,5},{8,10},{9,11},{10,... | collective-permute-start | bytes 786440 | tf_op jit(solution)/shard_map/ppermute | solution.py:23
  248.8 28.8 %collective-permute-start.35 = (bf16[1024,256]{1,0:T(8,128)(2,1)}, bf16[1024,256]{1,0:T(8,128)(2,1)S(1)}, u32[]{:S(2)}, u32[]{:S(2)}) collective-permute-start(bf16[1024,256]{1,0:T(8,128)(2,1)} %their_backward.1), channel_id=1, source_target_pairs={{0,4},{4,0},{8,12},{12,8},{16,20},{20,16},{24,28},{28,24},{1,5},{5... | collective-permute-start | bytes 1572872 | tf_op jit(solution)/shard_map/ppermute | solution.py:23
  249.2 30.2 %collective-permute-start.36 = (bf16[1024,256]{1,0:T(8,128)(2,1)}, bf16[1024,256]{1,0:T(8,128)(2,1)}, u32[]{:S(2)}, u32[]{:S(2)}) collective-permute-start(bf16[1024,256]{1,0:T(8,128)(2,1)} %their_backward.1), channel_id=1, source_target_pairs={{0,8},{4,12},{8,0},{12,4},{16,24},{20,28},{24,16},{28,20},{1,9},{5... | collective-permute-start | bytes 1572872 | tf_op jit(solution)/shard_map/ppermute | solution.py:23
  257.8 25.7 %collective-permute-start.37 = (bf16[1024,256]{1,0:T(8,128)(2,1)}, bf16[1024,256]{1,0:T(8,128)(2,1)}, u32[]{:S(2)}, u32[]{:S(2)}) collective-permute-start(bf16[1024,256]{1,0:T(8,128)(2,1)} %their_backward.1), channel_id=1, source_target_pairs={{0,16},{4,20},{8,24},{12,28},{16,0},{20,4},{24,8},{28,12},{1,17},{... | collective-permute-start | bytes 1572872 | tf_op jit(solution)/shard_map/ppermute | solution.py:23
  277.6 23.5 %collective-permute-start.43 = (bf16[4,128,768]{2,1,0:T(8,128)(2,1)}, bf16[4,128,768]{2,1,0:T(8,128)(2,1)}, u32[]{:S(2)}, u32[]{:S(2)}) collective-permute-start(bf16[4,128,768]{2,1,0:T(8,128)(2,1)} %slice.161), channel_id=1, source_target_pairs={{0,4},{4,0},{8,12},{12,8},{16,20},{20,16},{24,28},{28,24},{1,5},{5... | collective-permute-start | bytes 2359304 | tf_op jit(solution)/shard_map/ppermute | solution.py:23
  313.7 33.1 %collective-permute-start.47 = (bf16[2,128,2112]{1,2,0:T(8,128)(2,1)}, bf16[2,128,2112]{1,2,0:T(8,128)(2,1)S(1)}, u32[]{:S(2)}, u32[]{:S(2)}) collective-permute-start(bf16[2,128,2112]{1,2,0:T(8,128)(2,1)} %copy.46), channel_id=1, source_target_pairs={{0,8},{4,12},{8,0},{12,4},{16,24},{20,28},{24,16},{28,20},{1,9},{5... | collective-permute-start | bytes 3244040 | tf_op jit(solution)/shard_map/ppermute | solution.py:23
  316.2 37.6 %collective-permute-start.38 = (bf16[2,256,1024]{2,1,0:T(8,128)(2,1)}, bf16[2,256,1024]{2,1,0:T(8,128)(2,1)}, u32[]{:S(2)}, u32[]{:S(2)}) collective-permute-start(bf16[2,256,1024]{2,1,0:T(8,128)(2,1)} %slice.151), channel_id=1, source_target_pairs={{0,1},{1,0},{2,3},{3,2},{4,5},{5,4},{6,7},{7,6},{8,9},{9,8},{10,11... | collective-permute-start | bytes 3145736 | tf_op jit(solution)/shard_map/ppermute | solution.py:23
  350.1 23.6 %collective-permute-start.48 = (bf16[1,128,2112]{1,2,0:T(8,128)(2,1)S(1)}, bf16[1,128,2112]{1,2,0:T(8,128)(2,1)S(1)}, u32[]{:S(2)}, u32[]{:S(2)}) collective-permute-start(bf16[1,128,2112]{1,2,0:T(8,128)(2,1)S(1)} %copy.48), channel_id=1, source_target_pairs={{0,16},{4,20},{8,24},{12,28},{16,0},{20,4},{24,8},{28,12},{1,17},{... | collective-permute-start | bytes 1622024 | tf_op jit(solution)/shard_map/ppermute | solution.py:23
  (62 other events, 583.7 us)

commit v3 on v2

--- a/solution.py
+++ b/solution.py
@@ -27,14 +27,28 @@
     return lax.axis_size(axis).bit_length() - 1
 
 
-def call(body, out_shape, name, flops=0, **options):
-    return pl.pallas_call(
+def call(body, out_shape, name, flops=0, limit=28, **options):
+    kernel = pl.pallas_call(
         body,
         out_shape=out_shape,
         name=name,
-        cost_estimate=pl.CostEstimate(flops=flops, transcendentals=0, bytes_accessed=flops // 400),
+        cost_estimate=pl.CostEstimate(flops=0, transcendentals=0, bytes_accessed=0),
+        compiler_params=pltpu.CompilerParams(vmem_limit_bytes=limit << 20),
         **options,
     )
+    specs = options.get("in_specs")
+
+    def run(*args):
+        if specs is not None:
+            args = [
+                pltpu.with_memory_space_constraint(a, pltpu.VMEM)
+                if s.block_shape is None and s.memory_space is pltpu.VMEM
+                else a
+                for a, s in zip(args, specs)
+            ]
+        return kernel(*args)
+
+    return run
 
 
 def shape(dims, dtype):
@@ -54,6 +68,19 @@
     for b in order:
         place = place * 2 + ((difference >> b) & 1)
     return place
+
+
+def store_half(refs, place, c, value, rows=slice(None)):
+    half = refs[0].shape[0]
+    value = value.astype(B)
+
+    @pl.when(place < half)
+    def _():
+        refs[0][place, rows, c] = value
+
+    @pl.when(place >= half)
+    def _():
+        refs[1][place - half, rows, c] = value
 
 
 def choose(refs, index, chosen):
@@ -600,11 +627,14 @@
     pieces = refs[:parts]
     outs = refs[parts : 2 * parts]
     (x_ref, g_ref, gain_ref, wg_ref, wu_ref, wd_ref) = refs[2 * parts : 2 * parts + 6]
-    (normed_ref, gu_ref, hidden_ref, gn_ref, down_ref, own_ref) = refs[2 * parts + 6 :]
+    normed_ref, gu_ref, hidden_ref = refs[2 * parts + 6 : 2 * parts + 9]
+    gn_refs = refs[2 * parts + 9 : 2 * parts + 11]
+    down_refs = refs[2 * parts + 11 : 2 * parts + 13]
+    own_ref = refs[2 * parts + 13]
     me = me_ref[0]
     piece = x_ref.shape[2]
     width = x_ref.shape[3]
-    ff = wg_ref.shape[1]
+    ff = wg_ref.shape[0]
     order = list(range(parts.bit_length() - 1))
     for half in range(2):
         js = range(half * parts // 2, (half + 1) * parts // 2)
@@ -619,8 +649,8 @@
         factor = lax.rsqrt(jnp.mean(middle * middle, axis=1, keepdims=True) + epsilon)
         normed = (middle * factor * gain_ref[...]).astype(B)
         normed_ref[r, :] = normed
-        gate = dot(normed, wg_ref[...], 1, 0)
-        upper = dot(normed, wu_ref[...], 1, 0)
+        gate = dot(normed, wg_ref[...], 1, 1)
+        upper = dot(normed, wu_ref[...], 1, 1)
         s = jax.nn.sigmoid(gate)
         silu = gate * s
         hidden = (silu * upper).astype(B)
@@ -630,25 +660,27 @@
         grad_upper = (grad_hidden * silu).astype(B)
         gu_ref[r, :ff] = grad_gate
         gu_ref[r, ff:] = grad_upper
-        grad_normed = dot(grad_gate, wg_ref[...], 1, 1) + dot(grad_upper, wu_ref[...], 1, 1)
+        grad_normed = dot(grad_gate, wg_ref[...], 1, 0) + dot(grad_upper, wu_ref[...], 1, 0)
         down = dot(hidden, wd_ref[...], 1, 0)
         for a, j in enumerate(js):
             place = slot_place(jnp.bitwise_xor(me, j), order)
-            gn_ref[place] = grad_normed[a * piece : (a + 1) * piece].astype(B)
-            down_ref[place] = down[a * piece : (a + 1) * piece].astype(B)
+            store_half(gn_refs, place, slice(None), grad_normed[a * piece : (a + 1) * piece])
+            store_half(down_refs, place, slice(None), down[a * piece : (a + 1) * piece])
 
 
 def feed(c, me, pieces, outs, tokens, cotangent, gain, wg, wu, wd):
     parts, _, piece, width = tokens.shape
     chunk = parts * piece
-    ff = wg.shape[1]
+    ff = wg.shape[0]
     part = pl.BlockSpec((parts, 1, piece, width), lambda i: (0, c, 0, 0))
     results = [
         shape((chunk, width), B),
         shape((chunk, 2 * ff), B),
         shape((chunk, ff), B),
-        shape((parts, piece, width), B),
-        shape((parts, piece, width), B),
+        shape((parts // 2, piece, width), B),
+        shape((parts // 2, piece, width), B),
+        shape((parts // 2, piece, width), B),
+        shape((parts // 2, piece, width), B),
         shape((piece, width), F),
     ]
     return call(
@@ -751,49 +783,81 @@
     )(me, *pieces, w_output, *att, *lse)
 
 
-def store_slots(place_ref, out_ref, first, value, c):
-    rows = out_ref.shape[1]
+def store_slots(place_ref, outs, first, value, c):
+    rows = outs[0].shape[1]
     for a in range(value.shape[0] // rows):
-        out_ref[place_ref[first + a], :, c] = value[a * rows : (a + 1) * rows].astype(B)
-
-
-def feed_grads_body(place_ref, n0, n1, gu0, gu1, h0, h1, g_ref, out_ref):
-    block = n0.shape[1]
-    per = block // out_ref.shape[1]
+        store_half(outs, place_ref[first + a], c, value[a * rows : (a + 1) * rows])
+
+
+def columns_body(place_ref, a0, a1, r_ref, keep_ref, send_ref, *, view):
+    if view:
+        r0 = r_ref[:, 0].reshape(a0.shape[0], -1)
+        r1 = r_ref[:, 1].reshape(a0.shape[0], -1)
+    else:
+        r0 = r_ref[0]
+        r1 = r_ref[1]
+    value = dot(a0[...], r0, 0, 0) + dot(a1[...], r1, 0, 0)
+    lanes = keep_ref.shape[2]
+    per = value.shape[1] // lanes
     first = pl.program_id(0) * per
-    gu_width = gu0.shape[1]
-    store_slots(
-        place_ref, out_ref, first,
-        dot(n0[...], gu0[...], 0, 0) + dot(n1[...], gu1[...], 0, 0), slice(0, gu_width),
-    )
-    g0 = g_ref[:, 0].reshape(-1, block)
-    g1 = g_ref[:, 1].reshape(-1, block)
-    store_slots(
-        place_ref, out_ref, first,
-        dot(g0, h0[...], 0, 0) + dot(g1, h1[...], 0, 0), slice(gu_width, out_ref.shape[2]),
-    )
-
-
-def feed_grads(place, normed, gu, hidden, cotangent, docs):
-    chunk, width = normed[0].shape
-    total = gu[0].shape[1] + hidden[0].shape[1]
+    for a in range(per):
+        store_half(
+            (keep_ref, send_ref), place_ref[first + a], slice(None),
+            value[:, a * lanes : (a + 1) * lanes],
+        )
+
+
+def column_grads(place, left, right, docs, name):
+    chunk, features = left[0].shape
+    width = right.shape[-1]
     block = max(width // docs, 256)
-    parts, _, piece, _ = cotangent.shape
+    view = right.ndim == 4
+    rows = right.shape[:-1]
+    out = shape((docs // 2, features, width // docs), B)
+    return call(
+        functools.partial(columns_body, view=view),
+        [out, out],
+        name,
+        grid=(width // block,),
+        in_specs=[scalars()]
+        + [resident(a.shape) for a in left]
+        + [pl.BlockSpec(rows + (block,), lambda i: (0,) * len(rows) + (i,))],
+        out_specs=[resident(out.shape)] * 2,
+    )(place, *left, right)
+
+
+def two_columns_body(place_ref, a0, a1, r0, r1, keep_ref, send_ref):
+    value = dot(a0[...], r0[...], 0, 0) + dot(a1[...], r1[...], 0, 0)
+    lanes = keep_ref.shape[2]
+    per = value.shape[1] // lanes
+    first = pl.program_id(0) * per
+    for a in range(per):
+        store_half(
+            (keep_ref, send_ref), place_ref[first + a], slice(None),
+            value[:, a * lanes : (a + 1) * lanes],
+        )
+
+
+def two_column_grads(place, left, right, docs, name):
+    chunk, features = left[0].shape
+    width = right[0].shape[1]
+    block = max(width // docs, 256)
+    out = shape((docs // 2, features, width // docs), B)
     column = pl.BlockSpec((chunk, block), lambda i: (0, i))
     return call(
-        feed_grads_body,
-        shape((docs, width // docs, total), B),
-        "feed_grads",
-        4 * chunk * width * total,
+        two_columns_body,
+        [out, out],
+        name,
         grid=(width // block,),
-        in_specs=[scalars(), column, column]
-        + [resident(a.shape) for a in (*gu, *hidden)]
-        + [pl.BlockSpec((parts, 2, piece, block), lambda i: (0, 0, 0, i))],
-        out_specs=resident((docs, width // docs, total)),
-    )(place, *normed, *gu, *hidden, cotangent)
-
-
-def key_grads_body(place_ref, n_ref, dkv_ref, gb_ref, att0, att1, wk_ref, wv_ref, out_ref, gn_ref):
+        in_specs=[scalars()] + [resident(a.shape) for a in left] + [column, column],
+        out_specs=[resident(out.shape)] * 2,
+    )(place, *left, *right)
+
+
+def key_grads_body(
+    place_ref, n_ref, dkv_ref, gb_ref, att0, att1, wk_ref, wv_ref, keep_ref, send_ref, gn_ref
+):
+    out_ref = (keep_ref, send_ref)
     columns = wk_ref.shape[1]
     for c in range(2):
         gn_ref[c] = (
@@ -816,7 +880,7 @@
     columns = wk.shape[1]
     return call(
         key_grads_body,
-        [shape((docs, width // docs, 3 * columns), B), shape((2, chunk, width), B)],
+        [shape((docs // 2, width // docs, 3 * columns), B)] * 2 + [shape((2, chunk, width), B)],
         "key_grads",
         20 * chunk * width * columns,
         in_specs=[scalars()] + [whole()] * 7,
@@ -828,7 +892,9 @@
 ):
     ships = refs[:count]
     n_ref, part_ref, wq_ref, table_ref, x_ref = refs[count : count + 5]
-    out_ref, gn_ref, gain_ref = refs[count + 5 :]
+    out_ref = refs[count + 5 : count + 7]
+    gn_refs = refs[count + 7 : count + 9]
+    gain_ref = refs[count + 9]
     chosen = chosen_ref[0]
     me = me_ref[0]
     _, chunk, columns = dq_ref.shape
@@ -848,8 +914,9 @@
         gn = dot(low, wq_ref[...], 1, 1) + part_ref[c].astype(F)
         for j in range(parts):
             place = slot_place(jnp.bitwise_xor(me, j), order)
-            gn_ref[place, c * piece : (c + 1) * piece, :] = gn[j * piece : (j + 1) * piece].astype(
-                B
+            store_half(
+                gn_refs, place, slice(None), gn[j * piece : (j + 1) * piece],
+                slice(c * piece, (c + 1) * piece),
             )
         x = x_ref[:, c].reshape(chunk, width).astype(F)
         factor = lax.rsqrt(jnp.mean(x * x, axis=1, keepdims=True) + epsilon)
@@ -867,11 +934,9 @@
     parts = tokens.shape[0]
     return call(
         functools.partial(query_grads_body, count=len(ships), parts=parts, heads=heads),
-        [
-            shape((docs, width // docs, columns), B),
-            shape((parts, 2 * chunk // parts, width), B),
-            shape((1, width), F),
-        ],
+        [shape((docs // 2, width // docs, columns), B)] * 2
+        + [shape((parts // 2, 2 * chunk // parts, width), B)] * 2
+        + [shape((1, width), F)],
         "query_grads",
         8 * chunk * width * columns,
         in_specs=[scalars()] * 3 + [whole()] * (len(ships) + 6),
@@ -939,29 +1004,24 @@
     return pieces, distances
 
 
-def halve(value, axis, bit):
-    half = value.shape[0] // 2
-    return swap(value[half:], axis, 1 << bit)
+def after(value, *others):
+    return lax.optimization_barrier((value,) + others)[0]
 
 
 def add_low(a, b):
     return (a.astype(F) + b.astype(F)).astype(B)
 
 
-def scatter_slots(value, axis, order):
-    for b in order:
-        half = value.shape[0] // 2
-        got = halve(value, axis, b)
-        if half == 1:
-            return value[0].astype(F) + got[0].astype(F)
-        value = add_low(value[:half], got)
-    return value[0].astype(F)
-
-
-def scatter_two(value):
-    first = halve(value, "tensor", 0)
-    second = swap(add_low(value[1], first[1]), "tensor", 2)
-    return first, second
+def fold(keep, send, bit, *others):
+    got = swap(after(send, *others) if others else send, "dp", 1 << bit)
+    half = keep.shape[0] // 2
+    if half == 0:
+        return keep[0], got[0]
+    return add_low(keep[:half], got[:half]), add_low(keep[half:], got[half:])
+
+
+def total(pair, c=slice(None)):
+    return pair[0][:, c].astype(F) + pair[1][:, c].astype(F)
 
 
 def per_device(
@@ -1029,9 +1089,8 @@
     own_out, own_lse, own_sel = own_attend(
         flag, ship, own_off, stored_keys, stored_values, spread
     )
-    att, lse, their_sel, their_off, feeds = [], [], [], [], []
-    gm, gb_pieces, gain_parts = [], [], []
-    returned = []
+    ships = list(after(tuple(ships), own_out, local[0]))
+    att, lse, their_sel, their_off, returned, pieces = [], [], [], [], [], []
     for c in range(2):
         packed, sel, off, their_flag = their_attend(
             c, chosen, ships, stored_keys, stored_values, spread, groups
@@ -1040,84 +1099,107 @@
         their_off.append(off)
         returned.append(to_all(packed))
     for c in range(2):
-        a, total = merge(c, chosen, local, (own_out, own_lse), returned[c], heads)
+        a, log_total = merge(c, chosen, local, (own_out, own_lse), returned[c], heads)
         att.append(a)
-        lse.append(total)
-
-        pieces, _ = gather_tensor(a)
+        lse.append(log_total)
+        pieces.append(gather_tensor(a)[0])
+
+    feeds, back = [], []
+    for c in range(2):
+        if c:
+            pieces[c] = list(after(tuple(pieces[c]), back[0][1]))
         feeds.append(
             feed(
-                c, me, pieces, out_weights, tokens_view, cotangent_view, gain_m, w_gate, w_up,
-                w_down,
+                c, me, pieces[c], out_weights, tokens_view, cotangent_view, gain_m, w_gate.T,
+                w_up.T, w_down,
             )
         )
+        keep, send = feeds[c][3], feeds[c][4]
+        first = swap(send, "tensor", 1)
+        back.append((first, add_low(keep[1], first[1])))
+    gm, gb_pieces, gain_parts = [], [], []
     for c in range(2):
-        gn, middle = feeds[c][3], feeds[c][5]
-        first, second = scatter_two(gn)
+        first, second = back[c]
         grad_middle, low, gain_part = middle_back(
-            c, me, gn, first, second, middle, cotangent_view, gain_m
+            c, me, feeds[c][3], first, swap(second, "tensor", 2), feeds[c][7], cotangent_view,
+            gain_m
         )
         gm.append(grad_middle)
         gain_parts.append(gain_part)
         gb_pieces += gather_tensor(low)[0]
-
-    grad_branch, back_ship, stats = branch(me, gb_pieces, distances, w_output, att, lse, heads)
+    down_slots = column_grads(
+        place, after((feeds[0][2], feeds[1][2]), back[1][1]), cotangent_view, docs, "down_grads"
+    )
+    down_half = fold(*down_slots, dp_order[0])
+    gate_slots = two_column_grads(
+        place,
+        after((feeds[0][1], feeds[1][1]), gm[1], down_slots[1]),
+        (feeds[0][0], feeds[1][0]),
+        docs,
+        "gate_grads",
+    )
+
+    grad_branch, back_ship, stats = branch(
+        me, after(tuple(gb_pieces), gate_slots[0]), distances, w_output, att, lse, heads
+    )
     back_ships = to_all(back_ship)
     local_dq, dkv = local_backward(q, k, v, back_ship, stats, table, heads, parts)
+    gate_half = fold(*gate_slots, dp_order[0], local_dq)
     dq = own_backward(
         flag, back_ship, stats, own_sel, own_off, stored_keys, stored_values, local_dq, spread
     )
+    down_half = fold(*down_half, dp_order[1], dq)
     their_dq = their_backward(
-        chosen, their_flag, back_ships, their_sel, their_off, stored_keys, stored_values, spread
+        chosen, their_flag, list(after(tuple(back_ships), dq)), their_sel, their_off, stored_keys,
+        stored_values, spread
     )
     dq_ships = to_all(their_dq)
 
-    feed_sum = scatter_slots(
-        feed_grads(
-            place,
-            [f[0] for f in feeds],
-            [f[1] for f in feeds],
-            [f[2] for f in feeds],
-            cotangent_view,
-            docs,
-        ),
-        "dp",
-        dp_order,
-    )
+    keep, send, gn_part = key_grads(
+        place, normed_low, after(dkv, their_dq), grad_branch, att, w_key, w_value, docs
+    )
+    down_half = fold(*down_half, dp_order[2], their_dq) if len(dp_order) > 2 else down_half
+    key_half = fold(keep, send, dp_order[0])
+    gate_half = fold(*gate_half, dp_order[1], their_dq)
     output = []
     for c in range(2):
-        down = feeds[c][4]
-        first, second = scatter_two(down)
+        keep, send = feeds[c][5], after(feeds[c][6], their_dq)
+        first = swap(send, "tensor", 1)
+        second = swap(add_low(keep[1], first[1]), "tensor", 2)
         output.append(
-            feeds[c][5] + down[0].astype(F) + first[0].astype(F) + second.astype(F)
+            feeds[c][7] + keep[0].astype(F) + first[0].astype(F) + second.astype(F)
         )
-
-    key_slots, gn_part = key_grads(
-        place, normed_low, dkv, grad_branch, att, w_key, w_value, docs
-    )
-    key_sum = scatter_slots(key_slots, "dp", dp_order)
-    query_slots, gn, gain_part = query_grads(
+    keep, send, gn_keep, gn_send, gain_part = query_grads(
         chosen, me, place, dq, dq_ships, normed_low, gn_part, w_query, table_view, tokens_view,
         docs, heads
     )
-    query_sum = scatter_slots(query_slots, "dp", dp_order)
-    first, second = scatter_two(gn)
-    grad_tokens = tokens_back(me, gn, first, second, tokens, gm, gain_a)
+    query_half = fold(keep, send, dp_order[0])
+    first = swap(gn_send, "tensor", 1)
+    second = swap(add_low(gn_keep[1], first[1]), "tensor", 2)
+    grad_tokens = tokens_back(me, gn_keep, first, second, tokens, gm, gain_a)
+    for b in dp_order[1:]:
+        query_half = fold(*query_half, b)
+        key_half = fold(*key_half, b)
+    for b in dp_order[2:]:
+        gate_half = fold(*gate_half, b)
+    for b in dp_order[3:]:
+        down_half = fold(*down_half, b)
     gains = jnp.concatenate([gain_part, gain_parts[0] + gain_parts[1]], axis=0)
     gains = gains + sum(swap(gains, "tensor", t) for t in range(1, parts))
     for b in dp_order:
         gains = gains + swap(gains, "dp", 1 << b)
     gains = lax.dynamic_slice_in_dim(gains, my_doc * (width // docs), width // docs, 1)
+    gate_pair = gate_half
     return (
         jnp.concatenate(output, axis=0).astype(B),
         grad_tokens,
-        query_sum,
-        key_sum[:, :columns],
-        key_sum[:, columns : 2 * columns],
-        key_sum[:, 2 * columns :].T,
-        feed_sum[:, :ff],
-        feed_sum[:, ff : 2 * ff],
-        feed_sum[:, 2 * ff :].T,
+        total(query_half),
+        total(key_half, slice(0, columns)),
+        total(key_half, slice(columns, 2 * columns)),
+        total(key_half, slice(2 * columns, None)).T,
+        (gate_pair[0][:ff].astype(F) + gate_pair[1][:ff].astype(F)).T,
+        (gate_pair[0][ff:].astype(F) + gate_pair[1][ff:].astype(F)).T,
+        total(down_half),
         gains[0],
         gains[1],
     )

time: 384 us -> 342 us (0.89)
  Pallas kernels: 130 us -> 95.5 us
  other arithmetic: 22.6 us -> 11.4 us
  starting transfers between devices: 65 us -> 56.6 us
  waiting for transfers between devices: 122 us -> 129 us
    pallas_call x19 -> x20, Pallas kernels: 130 us -> 95.5 us  [run(): return kernel(*args)]
    unnamed x66 -> x195, local copies, waits for them, and re-layouts: 12.3 us -> 36.6 us
    slice x18 -> x0, local copies, waits for them, and re-layouts: 15.3 us -> none  [halve(): return swap(value[half:], axis, 1 << bit)]
    convert_element_type x11 -> x12, other arithmetic: 14.8 us -> 4.99 us  [add_low(): return (a.astype(F) + b.astype(F)).astype(B)]
    ppermute x55 -> x58, starting transfers between devices: 65 us -> 56.6 us  [swap(): lax.ppermute(array, axis, [(i, i ^ bit) for i in range(lax.axis_size(axis...]
    ppermute x55 -> x58, waiting for transfers between devices: 122 us -> 129 us  [swap(): lax.ppermute(array, axis, [(i, i ^ bit) for i in range(lax.axis_size(axis...]
    ppermute x3 -> x0, local copies, waits for them, and re-layouts: 4.45 us -> none  [swap(): lax.ppermute(array, axis, [(i, i ^ bit) for i in range(lax.axis_size(axis...]
  transfers between devices with their start and end apart: 55 -> 58, of which waited for: 16 -> 25; matrix products, arithmetic and copies ran while one was open for 14% -> 5% of each run, Pallas kernels for 32% -> 24%
where the time goes in v3:
time: 342 us; the launch traced here: 336 us
  waiting for transfers between devices  129 us (38%)
  Pallas kernels  95.5 us (28%)
  starting transfers between devices  56.6 us (17%)
  local copies, waits for them, and re-layouts  41.2 us (12%)
  other arithmetic  11.4 us (3%)
    ppermute x58, waiting for transfers between devices, swap(): lax.ppermute(array, axis, [(i, i ^ bit) for i in range(lax.axis_size(axis...  129 us
    pallas_call x20, Pallas kernels, run(): return kernel(*args)  95.5 us
    ppermute x58, starting transfers between devices, swap(): lax.ppermute(array, axis, [(i, i ^ bit) for i in range(lax.axis_size(axis...  56.6 us
    unnamed x195, local copies, waits for them, and re-layouts  36.6 us
  transfers between devices with their start and end apart: 58, of which 25 were waited for; matrix products, arithmetic and copies ran while one was open for 5% of the time, Pallas kernels for 24%

profile of v3, /device:TPU:0, one launch (start us, length us, event | category | flops | bytes accessed | tf_op | source)
XLA Modules:
  0.0 336.5 jit_solution(292419142860546628)
XLA Ops:
  27.5 8.9 %own_attend.1 = (bf16[2,512,256]{2,1,0:T(8,128)(2,1)S(1)}, f32[2,2,512]{2,1,0:T(2,128)S(1)}, f32[2,2,64,512]{3,2,1,0:T(8,128)S(1)}) custom-call(s32[1]{0:T(128)S(6)} %copy.31.flag_ref, bf16[2,640,256]{2,1,0:T(8,128)(2,1)} %get-tuple-element.106.ship_ref, bf16[2,64,512]{2,1,0:T(8,128)(2,1)S(1)} %get-tuple-element.107.off_ref, ...), custom_call_target="tpu_custom_call" | custom-call | tf_op jit(solution)/shard_map/own_attend/pallas_call | solution.py:49
  40.0 5.5 %collective-permute-done.1.refs_1_ = bf16[2,640,256]{2,1,0:T(8,128)(2,1)S(1)} collective-permute-done((bf16[2,640,256]{2,1,0:T(8,128)(2,1)}, bf16[2,640,256]{2,1,0:T(8,128)(2,1)S(1)}, u32[]{:S(2)}, u32[]{:S(2)}) %collective-permute-start.1) | collective-permute-done | bytes 655392 | tf_op jit(solution)/shard_map/ppermute | solution.py:23
  48.0 5.2 %their_attend.2 = (bf16[528,256]{1,0:T(8,128)(2,1)S(1)}, f32[2,64,512]{2,1,0:T(8,128)S(1)}, bf16[64,512]{1,0:T(8,128)(2,1)S(1)}, s32[1]{0:T(128)}) custom-call(s32[1]{0:T(128)} %bitcast.2.chosen_ref, bf16[2,640,256]{2,1,0:T(8,128)(2,1)S(1)} %collective-permute-done.refs_0_, bf16[2,640,256]{2,1,0:T(8,128)(2,1)S(1)} %collective-permute-done.1.refs_1_, ...), custom_call_target="tpu_custom_call" | custom-call | tf_op jit(solution)/shard_map/their_attend/pallas_call | solution.py:49
  54.8 5.0 %collective-permute-done.3.refs_0_ = bf16[528,256]{1,0:T(8,128)(2,1)S(1)} collective-permute-done((bf16[528,256]{1,0:T(8,128)(2,1)S(1)}, bf16[528,256]{1,0:T(8,128)(2,1)S(1)}, u32[]{:S(2)}, u32[]{:S(2)}) %collective-permute-start.3) | collective-permute-done | bytes 270368 | tf_op jit(solution)/shard_map/ppermute | solution.py:23
  70.4 5.2 %collective-permute-done.6.refs_1_ = bf16[512,256]{1,0:T(8,128)(2,1)} collective-permute-done((bf16[512,256]{1,0:T(8,128)(2,1)}, bf16[512,256]{1,0:T(8,128)(2,1)}, u32[]{:S(2)}, u32[]{:S(2)}) %collective-permute-start.6) | collective-permute-done | bytes 262176 | tf_op jit(solution)/shard_map/ppermute | solution.py:23
  75.6 5.6 %their_attend.3 = (bf16[528,256]{1,0:T(8,128)(2,1)}, f32[2,64,512]{2,1,0:T(8,128)S(1)}, bf16[64,512]{1,0:T(8,128)(2,1)S(1)}, s32[1]{0:T(128)}) custom-call(s32[1]{0:T(128)} %bitcast.2.chosen_ref, bf16[2,640,256]{2,1,0:T(8,128)(2,1)S(1)} %copy-done.17, bf16[2,640,256]{2,1,0:T(8,128)(2,1)S(1)} %copy-done.19, ...), custom_call_target="tpu_custom_call" | custom-call | tf_op jit(solution)/shard_map/their_attend/pallas_call | solution.py:49
  93.0 9.9 %feed.2 = (bf16[512,1024]{1,0:T(8,128)(2,1)S(1)}, bf16[512,1408]{1,0:T(8,128)(2,1)S(1)}, bf16[512,704]{1,0:T(8,128)(2,1)S(1)}, bf16[2,128,1024]{2,1,0:T(8,128)(2...) custom-call(s32[1]{0:T(128)} %bitcast.me_ref, ...), custom_call_target="tpu_custom_call" | custom-call | tf_op jit(solution)/shard_map/feed/pallas_call | solution.py:49
  107.3 7.0 %collective-permute-done.20.refs_1_ = bf16[512,256]{1,0:T(8,128)(2,1)S(1)} collective-permute-done((bf16[512,256]{1,0:T(8,128)(2,1)S(1)}, bf16[512,256]{1,0:T(8,128)(2,1)S(1)}, u32[]{:S(2)}, u32[]{:S(2)}) %collective-permute-start.20) | collective-permute-done | bytes 262176 | tf_op jit(solution)/shard_map/ppermute | solution.py:23
  115.9 9.7 %feed.3 = (bf16[512,1024]{1,0:T(8,128)(2,1)S(1)}, bf16[512,1408]{1,0:T(8,128)(2,1)S(1)}, bf16[512,704]{1,0:T(8,128)(2,1)S(1)}, bf16[2,128,1024]{2,1,0:T(8,128)(2...) custom-call(s32[1]{0:T(128)} %bitcast.me_ref, ...), custom_call_target="tpu_custom_call" | custom-call | tf_op jit(solution)/shard_map/feed/pallas_call | solution.py:49
  129.9 5.8 %collective-permute-done.13.r2_ref = bf16[128,1024]{1,0:T(8,128)(2,1)S(1)} collective-permute-done((bf16[128,1024]{1,0:T(8,128)(2,1)S(1)}, bf16[128,1024]{1,0:T(8,128)(2,1)S(1)}, u32[]{:S(2)}, u32[]{:S(2)}) %collective-permute-start.13) | collective-permute-done | bytes 262176 | tf_op jit(solution)/shard_map/ppermute | solution.py:23
  147.4 4.5 %collective-permute-done.25.refs_5_ = bf16[128,1024]{1,0:T(8,128)(2,1)S(1)} collective-permute-done((bf16[128,1024]{1,0:T(8,128)(2,1)S(1)}, bf16[128,1024]{1,0:T(8,128)(2,1)S(1)}, u32[]{:S(2)}, u32[]{:S(2)}) %collective-permute-start.25) | collective-permute-done | bytes 262176 | tf_op jit(solution)/shard_map/ppermute | solution.py:23
  157.6 6.2 %gate_grads.1 = (bf16[4,1408,128]{2,1,0:T(8,128)(2,1)S(1)}, bf16[4,1408,128]{2,1,0:T(8,128)(2,1)}) custom-call(s32[8]{0:T(128)S(1)} %and_add_fusion.place_ref, bf16[512,1408]{1,0:T(8,128)(2,1)S(1)} %get-tuple-element.140.a0, bf16[512,1408]{1,0:T(8,128)(2,1)S(1)} %get-tuple-element.141.a1, bf16[512,1024]{1,0:T(8,128)(2,1)S(1)} %get-tuple-element.142.r0, ...), custom_call_target="tpu_custom_call" | custom-call | tf_op jit(solution)/shard_map/gate_grads/pallas_call | solution.py:49
  173.4 4.3 %local_backward.1 = (f32[2,512,256]{2,1,0:T(8,128)S(1)}, bf16[2,512,512]{2,1,0:T(8,128)(2,1)S(1)}) custom-call(bf16[1024,256]{1,0:T(8,128)(2,1)S(1)} %copy-done.40, bf16[1024,256]{1,0:T(8,128)(2,1)S(1)} %copy-done.43, bf16[1024,256]{1,0:T(8,128)(2,1)S(1)} %copy-done.46, bf16[1088,256]{1,0:T(8,128)(2,1)S(1)} %get-tuple-element.155.ship_ref, ...), custom_call_target="tpu_custom_call" | custom-call | tf_op jit(solution)/shard_map/local_backward/pallas_call | solution.py:49
  178.7 7.2 %own_backward.1.dq_ref = f32[2,512,256]{2,1,0:T(8,128)S(1)} custom-call(s32[1]{0:T(128)S(6)} %copy.31.flag_ref, bf16[1088,256]{1,0:T(8,128)(2,1)S(1)} %get-tuple-element.155.ship_ref, f32[2,4,512]{2,1,0:T(4,128)S(1)} %get-tuple-element.156.st_ref, f32[2,2,64,512]{3,2,1,0:T(8,128)S(1)} %copy-done.70, bf16[2,64,512]{2,1,0:T(8,128)(2,1)S(1)} %copy-done.64, ...), custom_call_target="tpu_custom_call" | custom-call | tf_op jit(solution)/shard_map/own_backward/pallas_call | solution.py:49
  186.5 9.0 %collective-permute-done.29.refs_1_ = bf16[1088,256]{1,0:T(8,128)(2,1)S(1)} collective-permute-done((bf16[1088,256]{1,0:T(8,128)(2,1)S(1)}, bf16[1088,256]{1,0:T(8,128)(2,1)S(1)}, u32[]{:S(2)}, u32[]{:S(2)}) %collective-permute-start.29) | collective-permute-done | bytes 557088 | tf_op jit(solution)/shard_map/ppermute | solution.py:23
  197.9 8.5 %their_backward.1 = bf16[1024,256]{1,0:T(8,128)(2,1)} custom-call(s32[1]{0:T(128)} %bitcast.2.chosen_ref, s32[1]{0:T(128)} %get-tuple-element.118.flag_ref, bf16[1088,256]{1,0:T(8,128)(2,1)S(1)} %collective-permute-done.28.refs_0_, bf16[1088,256]{1,0:T(8,128)(2,1)S(1)} %collective-permute-done.29.refs_1_, ...), custom_call_target="tpu_custom_call" | custom-call | tf_op jit(solution)/shard_map/their_backward/pallas_call | solution.py:49
  218.3 5.6 %key_grads.1 = (bf16[4,128,768]{2,1,0:T(8,128)(2,1)S(1)}, bf16[4,128,768]{2,1,0:T(8,128)(2,1)S(1)}, bf16[2,512,1024]{2,1,0:T(8,128)(2,1)S(1)}) custom-call(s32[8]{0:T(128)S(1)} %and_add_fusion.place_ref, bf16[2,512,1024]{2,1,0:T(8,128)(2,1)S(1)} %copy-done.10, bf16[2,512,512]{2,1,0:T(8,128)(2,1)S(1)} %copy-done.62, bf16[2,512,1024]{2,1,0:T(8,128)(2,1)S(1)} %copy-done.37, ...), custom_call_target="tpu_custom_call" | custom-call | tf_op jit(solution)/shard_map/key_grads/pallas_call | solution.py:49
  224.0 8.7 %collective-permute-done.36.refs_1_ = bf16[1024,256]{1,0:T(8,128)(2,1)} collective-permute-done((bf16[1024,256]{1,0:T(8,128)(2,1)}, bf16[1024,256]{1,0:T(8,128)(2,1)}, u32[]{:S(2)}, u32[]{:S(2)}) %collective-permute-start.36) | collective-permute-done | bytes 524320 | tf_op jit(solution)/shard_map/ppermute | solution.py:23
  232.8 4.4 %query_grads.1 = (bf16[4,128,256]{2,1,0:T(8,128)(2,1)S(1)}, bf16[4,128,256]{2,1,0:T(8,128)(2,1)S(1)}, bf16[2,256,1024]{2,1,0:T(8,128)(2,1)S(1)}, bf16[2,256,1024]{2,1,0:T(8,128)(2,1)S(1)}, f32[1,1024]{1,0:T(1,128)S(1)}) custom-call(s32[1]{0:T(128)} %bitcast.2.chosen_ref, s32[1]{0:T(128)} %bitcast.me_ref, s32[8]{0:T(128)S(1)} %and_add_fusion.place_ref, ...), custom_call_target="tpu_custom_call" | custom-call | tf_op jit(solution)/shard_map/query_grads/pallas_call | solution.py:49
  243.3 9.1 %collective-permute-done.51 = bf16[1,704,128]{2,1,0:T(8,128)(2,1)S(1)} collective-permute-done((bf16[1,704,128]{2,1,0:T(8,128)(2,1)S(1)}, bf16[1,704,128]{2,1,0:T(8,128)(2,1)S(1)}, u32[]{:S(2)}, u32[]{:S(2)}) %collective-permute-start.51) | collective-permute-done | bytes 180256 | tf_op jit(solution)/shard_map/ppermute | solution.py:23
  254.4 10.6 %collective-permute-done.55 = f32[2,1024]{1,0:T(2,128)S(1)} collective-permute-done((f32[2,1024]{1,0:T(2,128)S(1)}, f32[2,1024]{1,0:T(2,128)S(1)}, u32[]{:S(2)}, u32[]{:S(2)}) %collective-permute-start.55) | collective-permute-done | bytes 8224 | tf_op jit(solution)/shard_map/ppermute | solution.py:23
  280.6 4.3 %collective-permute-done.32 = bf16[128,1024]{1,0:T(8,128)(2,1)S(1)} collective-permute-done((bf16[128,1024]{1,0:T(8,128)(2,1)S(1)}, bf16[128,1024]{1,0:T(8,128)(2,1)S(1)}, u32[]{:S(2)}, u32[]{:S(2)}) %collective-permute-start.32) | collective-permute-done | bytes 262176 | tf_op jit(solution)/shard_map/ppermute | solution.py:23
  298.2 14.5 %collective-permute-done.47 = bf16[2,1408,128]{2,1,0:T(8,128)(2,1)S(1)} collective-permute-done((bf16[2,1408,128]{2,1,0:T(8,128)(2,1)S(1)}, bf16[2,1408,128]{2,1,0:T(8,128)(2,1)S(1)}, u32[]{:S(2)}, u32[]{:S(2)}) %collective-permute-start.47) | collective-permute-done | bytes 720928 | tf_op jit(solution)/shard_map/ppermute | solution.py:23
  316.8 13.0 %collective-permute-done.48 = bf16[1,1408,128]{2,1,0:T(8,128)(2,1)} collective-permute-done((bf16[1,1408,128]{2,1,0:T(8,128)(2,1)}, bf16[1,1408,128]{2,1,0:T(8,128)(2,1)}, u32[]{:S(2)}, u32[]{:S(2)}) %collective-permute-start.48) | collective-permute-done | bytes 360480 | tf_op jit(solution)/shard_map/ppermute | solution.py:23
  (337 shorter events, 155.8 us)
Async XLA Ops:
  12.1 27.8 %collective-permute-start = (bf16[2,640,256]{2,1,0:T(8,128)(2,1)}, bf16[2,640,256]{2,1,0:T(8,128)(2,1)S(1)}, u32[]{:S(2)}, u32[]{:S(2)}) collective-permute-start(bf16[2,640,256]{2,1,0:T(8,128)(2,1)} %get-tuple-element.106.ship_ref), channel_id=1, source_target_pairs={{0,4},{4,0},{8,12},{12,8},{16,20},{20,16},{24,28},{28,24},{1,5},{5... | collective-permute-start | bytes 1966088 | tf_op jit(solution)/shard_map/ppermute | solution.py:23
  15.2 30.3 %collective-permute-start.1 = (bf16[2,640,256]{2,1,0:T(8,128)(2,1)}, bf16[2,640,256]{2,1,0:T(8,128)(2,1)S(1)}, u32[]{:S(2)}, u32[]{:S(2)}) collective-permute-start(bf16[2,640,256]{2,1,0:T(8,128)(2,1)} %get-tuple-element.106.ship_ref), channel_id=1, source_target_pairs={{0,8},{4,12},{8,0},{12,4},{16,24},{20,28},{24,16},{28,20},{1,9},{5... | collective-permute-start | bytes 1966088 | tf_op jit(solution)/shard_map/ppermute | solution.py:23
  16.8 31.2 %collective-permute-start.2 = (bf16[2,640,256]{2,1,0:T(8,128)(2,1)}, bf16[2,640,256]{2,1,0:T(8,128)(2,1)}, u32[]{:S(2)}, u32[]{:S(2)}) collective-permute-start(bf16[2,640,256]{2,1,0:T(8,128)(2,1)} %get-tuple-element.106.ship_ref), channel_id=1, source_target_pairs={{0,16},{4,20},{8,24},{12,28},{16,0},{20,4},{24,8},{28,12},{1,17},{... | collective-permute-start | bytes 1966088 | tf_op jit(solution)/shard_map/ppermute | solution.py:23
  19.3 34.9 %collective-permute-start.9 = (bf16[256,1024]{1,0:T(8,128)(2,1)}, bf16[256,1024]{1,0:T(8,128)(2,1)}, u32[]{:S(2)}, u32[]{:S(2)}) collective-permute-start(bf16[256,1024]{1,0:T(8,128)(2,1)} %refs_8_.1), channel_id=1, source_target_pairs={{0,2},{1,3},{2,0},{3,1},{4,6},{5,7},{6,4},{7,5},{8,10},{9,11},{10,... | collective-permute-start | bytes 1572872 | tf_op jit(solution)/shard_map/ppermute | solution.py:23
  54.3 28.3 %collective-permute-start.10 = (bf16[256,1024]{1,0:T(8,128)(2,1)}, bf16[256,1024]{1,0:T(8,128)(2,1)S(1)}, u32[]{:S(2)}, u32[]{:S(2)}) collective-permute-start(bf16[256,1024]{1,0:T(8,128)(2,1)} %refs_8_.1), channel_id=1, source_target_pairs={{0,1},{1,0},{2,3},{3,2},{4,5},{5,4},{6,7},{7,6},{8,9},{9,8},{10,11... | collective-permute-start | bytes 1572872 | tf_op jit(solution)/shard_map/ppermute | solution.py:23
  54.3 29.9 %collective-permute-start.11 = (bf16[256,1024]{1,0:T(8,128)(2,1)}, bf16[256,1024]{1,0:T(8,128)(2,1)S(1)}, u32[]{:S(2)}, u32[]{:S(2)}) collective-permute-start(bf16[256,1024]{1,0:T(8,128)(2,1)} %collective-permute-done.9.refs_5_), channel_id=1, source_target_pairs={{0,1},{1,0},{2,3},{3,2},{4,5},{5,4},{6,7},{7,6},{8,9},{9,8},{10,11... | collective-permute-start | bytes 1572872 | tf_op jit(solution)/shard_map/ppermute | solution.py:23
  82.5 20.5 %collective-permute-start.17 = (bf16[528,256]{1,0:T(8,128)(2,1)}, bf16[528,256]{1,0:T(8,128)(2,1)}, u32[]{:S(2)}, u32[]{:S(2)}) collective-permute-start(bf16[528,256]{1,0:T(8,128)(2,1)} %get-tuple-element.122), channel_id=1, source_target_pairs={{0,4},{4,0},{8,12},{12,8},{16,20},{20,16},{24,28},{28,24},{1,5},{5... | collective-permute-start | bytes 811016 | tf_op jit(solution)/shard_map/ppermute | solution.py:23
  83.3 19.7 %collective-permute-start.18 = (bf16[528,256]{1,0:T(8,128)(2,1)}, bf16[528,256]{1,0:T(8,128)(2,1)}, u32[]{:S(2)}, u32[]{:S(2)}) collective-permute-start(bf16[528,256]{1,0:T(8,128)(2,1)} %get-tuple-element.122), channel_id=1, source_target_pairs={{0,8},{4,12},{8,0},{12,4},{16,24},{20,28},{24,16},{28,20},{1,9},{5... | collective-permute-start | bytes 811016 | tf_op jit(solution)/shard_map/ppermute | solution.py:23
  144.0 20.9 %collective-permute-start.15 = (bf16[128,1024]{1,0:T(8,128)(2,1)S(1)}, bf16[128,1024]{1,0:T(8,128)(2,1)S(1)}, u32[]{:S(2)}, u32[]{:S(2)}) collective-permute-start(bf16[128,1024]{1,0:T(8,128)(2,1)S(1)} %get-tuple-element.145.refs_0_), channel_id=1, source_target_pairs={{0,1},{1,0},{2,3},{3,2},{4,5},{5,4},{6,7},{7,6},{8,9},{9,8},{10,11... | collective-permute-start | bytes 786440 | tf_op jit(solution)/shard_map/ppermute | solution.py:23
  156.0 52.5 %collective-permute-start.49 = (bf16[4,704,128]{2,1,0:T(8,128)(2,1)S(1)}, bf16[4,704,128]{2,1,0:T(8,128)(2,1)S(1)}, u32[]{:S(2)}, u32[]{:S(2)}) collective-permute-start(bf16[4,704,128]{2,1,0:T(8,128)(2,1)S(1)} %get-tuple-element.139), channel_id=1, source_target_pairs={{0,4},{4,0},{8,12},{12,8},{16,20},{20,16},{24,28},{28,24},{1,5},{5... | collective-permute-start | bytes 2162696 | tf_op jit(solution)/shard_map/ppermute | solution.py:23
  169.2 26.3 %collective-permute-start.29 = (bf16[1088,256]{1,0:T(8,128)(2,1)S(1)}, bf16[1088,256]{1,0:T(8,128)(2,1)S(1)}, u32[]{:S(2)}, u32[]{:S(2)}) collective-permute-start(bf16[1088,256]{1,0:T(8,128)(2,1)S(1)} %get-tuple-element.155.ship_ref), channel_id=1, source_target_pairs={{0,8},{4,12},{8,0},{12,4},{16,24},{20,28},{24,16},{28,20},{1,9},{5... | collective-permute-start | bytes 1671176 | tf_op jit(solution)/shard_map/ppermute | solution.py:23
  170.8 27.1 %collective-permute-start.30 = (bf16[1088,256]{1,0:T(8,128)(2,1)S(1)}, bf16[1088,256]{1,0:T(8,128)(2,1)S(1)}, u32[]{:S(2)}, u32[]{:S(2)}) collective-permute-start(bf16[1088,256]{1,0:T(8,128)(2,1)S(1)} %get-tuple-element.155.ship_ref), channel_id=1, source_target_pairs={{0,16},{4,20},{8,24},{12,28},{16,0},{20,4},{24,8},{28,12},{1,17},{... | collective-permute-start | bytes 1671176 | tf_op jit(solution)/shard_map/ppermute | solution.py:23
  206.4 26.4 %collective-permute-start.36 = (bf16[1024,256]{1,0:T(8,128)(2,1)}, bf16[1024,256]{1,0:T(8,128)(2,1)}, u32[]{:S(2)}, u32[]{:S(2)}) collective-permute-start(bf16[1024,256]{1,0:T(8,128)(2,1)} %their_backward.1), channel_id=1, source_target_pairs={{0,8},{4,12},{8,0},{12,4},{16,24},{20,28},{24,16},{28,20},{1,9},{5... | collective-permute-start | bytes 1572872 | tf_op jit(solution)/shard_map/ppermute | solution.py:23
  208.4 24.4 %collective-permute-start.37 = (bf16[1024,256]{1,0:T(8,128)(2,1)}, bf16[1024,256]{1,0:T(8,128)(2,1)}, u32[]{:S(2)}, u32[]{:S(2)}) collective-permute-start(bf16[1024,256]{1,0:T(8,128)(2,1)} %their_backward.1), channel_id=1, source_target_pairs={{0,16},{4,20},{8,24},{12,28},{16,0},{20,4},{24,8},{28,12},{1,17},{... | collective-permute-start | bytes 1572872 | tf_op jit(solution)/shard_map/ppermute | solution.py:23
  209.5 29.4 %collective-permute-start.50 = (bf16[2,704,128]{2,1,0:T(8,128)(2,1)}, bf16[2,704,128]{2,1,0:T(8,128)(2,1)}, u32[]{:S(2)}, u32[]{:S(2)}) collective-permute-start(bf16[2,704,128]{2,1,0:T(8,128)(2,1)} %get-tuple-element.186), channel_id=1, source_target_pairs={{0,8},{4,12},{8,0},{12,4},{16,24},{20,28},{24,16},{28,20},{1,9},{5... | collective-permute-start | bytes 1081352 | tf_op jit(solution)/shard_map/ppermute | solution.py:23
  211.5 78.3 %collective-permute-start.46 = (bf16[4,1408,128]{2,1,0:T(8,128)(2,1)}, bf16[4,1408,128]{2,1,0:T(8,128)(2,1)S(1)}, u32[]{:S(2)}, u32[]{:S(2)}) collective-permute-start(bf16[4,1408,128]{2,1,0:T(8,128)(2,1)} %get-tuple-element.183), channel_id=1, source_target_pairs={{0,4},{4,0},{8,12},{12,8},{16,20},{20,16},{24,28},{28,24},{1,5},{5... | collective-permute-start | bytes 4325384 | tf_op jit(solution)/shard_map/ppermute | solution.py:23
  224.0 41.4 %collective-permute-start.31 = (bf16[2,128,1024]{2,1,0:T(8,128)(2,1)S(1)}, bf16[2,128,1024]{2,1,0:T(8,128)(2,1)S(1)}, u32[]{:S(2)}, u32[]{:S(2)}) collective-permute-start(bf16[2,128,1024]{2,1,0:T(8,128)(2,1)S(1)} %copy-done.91), channel_id=1, source_target_pairs={{0,1},{1,0},{2,3},{3,2},{4,5},{5,4},{6,7},{7,6},{8,9},{9,8},{10,11... | collective-permute-start | bytes 1572872 | tf_op jit(solution)/shard_map/ppermute | solution.py:23
  243.1 34.6 %collective-permute-start.43 = (bf16[4,128,768]{2,1,0:T(8,128)(2,1)S(1)}, bf16[4,128,768]{2,1,0:T(8,128)(2,1)S(1)}, u32[]{:S(2)}, u32[]{:S(2)}) collective-permute-start(bf16[4,128,768]{2,1,0:T(8,128)(2,1)S(1)} %get-tuple-element.181), channel_id=1, source_target_pairs={{0,4},{4,0},{8,12},{12,8},{16,20},{20,16},{24,28},{28,24},{1,5},{5... | collective-permute-start | bytes 2359304 | tf_op jit(solution)/shard_map/ppermute | solution.py:23
  243.2 27.8 %collective-permute-start.33 = (bf16[2,128,1024]{2,1,0:T(8,128)(2,1)S(1)}, bf16[2,128,1024]{2,1,0:T(8,128)(2,1)S(1)}, u32[]{:S(2)}, u32[]{:S(2)}) collective-permute-start(bf16[2,128,1024]{2,1,0:T(8,128)(2,1)S(1)} %copy-done.93), channel_id=1, source_target_pairs={{0,1},{1,0},{2,3},{3,2},{4,5},{5,4},{6,7},{7,6},{8,9},{9,8},{10,11... | collective-permute-start | bytes 1572872 | tf_op jit(solution)/shard_map/ppermute | solution.py:23
  271.0 24.5 %collective-permute-start.38 = (bf16[2,256,1024]{2,1,0:T(8,128)(2,1)S(1)}, bf16[2,256,1024]{2,1,0:T(8,128)(2,1)S(1)}, u32[]{:S(2)}, u32[]{:S(2)}) collective-permute-start(bf16[2,256,1024]{2,1,0:T(8,128)(2,1)S(1)} %get-tuple-element.176), channel_id=1, source_target_pairs={{0,1},{1,0},{2,3},{3,2},{4,5},{5,4},{6,7},{7,6},{8,9},{9,8},{10,11... | collective-permute-start | bytes 3145736 | tf_op jit(solution)/shard_map/ppermute | solution.py:23
  290.2 22.5 %collective-permute-start.47 = (bf16[2,1408,128]{2,1,0:T(8,128)(2,1)S(1)}, bf16[2,1408,128]{2,1,0:T(8,128)(2,1)S(1)}, u32[]{:S(2)}, u32[]{:S(2)}) collective-permute-start(bf16[2,1408,128]{2,1,0:T(8,128)(2,1)S(1)} %get-tuple-element.184), channel_id=1, source_target_pairs={{0,8},{4,12},{8,0},{12,4},{16,24},{20,28},{24,16},{28,20},{1,9},{5... | collective-permute-start | bytes 2162696 | tf_op jit(solution)/shard_map/ppermute | solution.py:23
  292.3 21.3 %collective-permute-start.42 = (bf16[1,128,256]{2,1,0:T(8,128)(2,1)S(1)}, bf16[1,128,256]{2,1,0:T(8,128)(2,1)S(1)}, u32[]{:S(2)}, u32[]{:S(2)}) collective-permute-start(bf16[1,128,256]{2,1,0:T(8,128)(2,1)S(1)} %add_convert_fusion.19), channel_id=1, source_target_pairs={{0,16},{4,20},{8,24},{12,28},{16,0},{20,4},{24,8},{28,12},{1,17},{... | collective-permute-start | bytes 196616 | tf_op jit(solution)/shard_map/ppermute | solution.py:23
  293.4 20.9 %collective-permute-start.45 = (bf16[1,128,768]{2,1,0:T(8,128)(2,1)S(1)}, bf16[1,128,768]{2,1,0:T(8,128)(2,1)S(1)}, u32[]{:S(2)}, u32[]{:S(2)}) collective-permute-start(bf16[1,128,768]{2,1,0:T(8,128)(2,1)S(1)} %get-tuple-element.211), channel_id=1, source_target_pairs={{0,16},{4,20},{8,24},{12,28},{16,0},{20,4},{24,8},{28,12},{1,17},{... | collective-permute-start | bytes 589832 | tf_op jit(solution)/shard_map/ppermute | solution.py:23
  296.7 35.1 %collective-permute-start.39 = (bf16[256,1024]{1,0:T(8,128)(2,1)}, bf16[256,1024]{1,0:T(8,128)(2,1)}, u32[]{:S(2)}, u32[]{:S(2)}) collective-permute-start(bf16[256,1024]{1,0:T(8,128)(2,1)} %fusion), channel_id=1, source_target_pairs={{0,2},{1,3},{2,0},{3,1},{4,6},{5,7},{6,4},{7,5},{8,10},{9,11},{10,... | collective-permute-start | bytes 1572872 | tf_op jit(solution)/shard_map/ppermute | solution.py:23
  (131 other events, 1448.8 us)

commit v4 on v3

--- a/solution.py
+++ b/solution.py
@@ -13,6 +13,12 @@
 F = jnp.float32
 B = jnp.bfloat16
 GROUP_BLOCK = 16
+extra_rows = 16
+kernel_us = dict(
+    project=3.4, own_attend=9.0, their_attend=5.3, own_backward=7.2, their_backward=8.5,
+    local_forward=3.4, local_backward=4.2, merge=1.9, feed=9.8, middle_back=0.4, branch=2.3,
+    down_grads=4.0, gate_grads=6.2, key_grads=5.6, query_grads=4.3, tokens_back=2.4,
+)
 
 
 def dot(a, b, da, db):
@@ -32,7 +38,9 @@
         body,
         out_shape=out_shape,
         name=name,
-        cost_estimate=pl.CostEstimate(flops=0, transcendentals=0, bytes_accessed=0),
+        cost_estimate=pl.CostEstimate(
+            flops=int(kernel_us[name] * 1e9 * 1.15), transcendentals=0, bytes_accessed=0
+        ),
         compiler_params=pltpu.CompilerParams(vmem_limit_bytes=limit << 20),
         **options,
     )
@@ -182,20 +190,24 @@
     body = functools.partial(
         project_body, parts=parts, heads=heads, hd=columns // heads, spread=spread
     )
+    arrays = (tokens, knn, gain, wq, wk, wv, table)
+    results = [
+        shape((2, chunk + chunk // columns * groups, columns), B),
+        shape((length, columns), B),
+        shape((length, columns), B),
+        shape((length, columns), B),
+        shape((2, chunk, width), B),
+        shape((2, groups, chunk), B),
+    ]
     return call(
         body,
-        [
-            shape((2, chunk + chunk // columns * groups, columns), B),
-            shape((length, columns), B),
-            shape((length, columns), B),
-            shape((length, columns), B),
-            shape((2, chunk, width), B),
-            shape((2, groups, chunk), B),
-        ],
+        results,
         "project",
         6 * length * width * columns,
-        in_specs=[scalars()] + [whole()] * 7,
-    )(flag, tokens, knn, gain, wq, wk, wv, table)
+        grid=(1,),
+        in_specs=[scalars()] + [resident(a.shape) for a in arrays],
+        out_specs=[resident(r.shape) for r in results],
+    )(flag, *[pltpu.with_memory_space_constraint(a, pltpu.HBM) for a in arrays])
 
 
 def pick(block_scores, offsets, heads, spread, gb):
@@ -698,25 +710,41 @@
     )(me, *pieces, *outs, tokens, cotangent, gain, wg, wu, wd)
 
 
-def middle_back_body(me_ref, gn_ref, r1_ref, r2_ref, m_ref, g_ref, gain_ref, gm_ref, gb_ref, ga_ref):
-    total = gn_ref[0].astype(F) + r1_ref[0].astype(F) + r2_ref[...].astype(F)
-    middle = m_ref[...]
-    factor = lax.rsqrt(jnp.mean(middle * middle, axis=1, keepdims=True) + epsilon)
-    scaled = total * gain_ref[...]
-    grad = (
-        g_ref[0, 0].astype(F)
-        + factor * scaled
-        - middle * (factor * factor * factor) * jnp.mean(middle * scaled, axis=1, keepdims=True)
-    )
-    gm_ref[...] = grad
-    gb_ref[...] = grad.astype(B)
-    ga_ref[...] = jnp.sum(total * middle * factor, axis=0, keepdims=True)
-
-
-def middle_back(c, me, gn, r1, r2, middle, cotangent, gain):
-    piece, width = middle.shape
+def middle_back_body(me_ref, *refs):
+    g_ref, gain_ref, gm_ref, gb_ref, ga_ref = refs[8:]
+    gain = None
+    for c in range(2):
+        gn_ref, r1_ref, r2_ref, m_ref = refs[4 * c : 4 * c + 4]
+        total = gn_ref[0].astype(F) + r1_ref[0].astype(F) + r2_ref[...].astype(F)
+        middle = m_ref[...]
+        piece = middle.shape[0]
+        rows = slice(c * piece, (c + 1) * piece)
+        factor = lax.rsqrt(jnp.mean(middle * middle, axis=1, keepdims=True) + epsilon)
+        scaled = total * gain_ref[...]
+        grad = (
+            g_ref[0, c].astype(F)
+            + factor * scaled
+            - middle
+            * (factor * factor * factor)
+            * jnp.mean(middle * scaled, axis=1, keepdims=True)
+        )
+        gm_ref[rows, :] = grad
+        gb_ref[rows, :] = grad.astype(B)
+        part = jnp.sum(total * middle * factor, axis=0, keepdims=True)
+        gain = part if gain is None else gain + part
+    ga_ref[...] = gain
+
+
+def middle_back(me, chunks, cotangent, gain):
+    piece, width = chunks[0][3].shape
     fixed = lambda dims: pl.BlockSpec(dims, lambda i, m: (0,) * len(dims))
-    results = [shape((piece, width), F), shape((piece, width), B), shape((1, width), F)]
+    results = [shape((2 * piece, width), F), shape((2 * piece, width), B), shape((1, width), F)]
+    per_chunk = [
+        fixed((1, piece, width)),
+        fixed((1, piece, width)),
+        fixed((piece, width)),
+        fixed((piece, width)),
+    ]
     return call(
         middle_back_body,
         results,
@@ -724,24 +752,21 @@
         grid_spec=pltpu.PrefetchScalarGridSpec(
             num_scalar_prefetch=1,
             grid=(1,),
-            in_specs=[
-                fixed((1, piece, width)),
-                fixed((1, piece, width)),
-                fixed((piece, width)),
-                fixed((piece, width)),
-                pl.BlockSpec((1, 1, piece, width), lambda i, m: (m[0], c, 0, 0)),
+            in_specs=per_chunk * 2
+            + [
+                pl.BlockSpec((1, 2, piece, width), lambda i, m: (m[0], 0, 0, 0)),
                 fixed((1, width)),
             ],
             out_specs=[fixed(r.shape) for r in results],
         ),
-    )(me, gn, r1, r2, middle, cotangent, gain)
+    )(me, *chunks[0], *chunks[1], cotangent, gain)
 
 
 def branch_body(me_ref, *refs, parts, heads, distances):
-    pieces = refs[: 2 * parts]
-    w_ref, att0, att1, lse0, lse1, gb_ref, ship_ref, st_ref = refs[2 * parts :]
+    pieces = refs[:parts]
+    w_ref, att0, att1, lse0, lse1, gb_ref, ship_ref, st_ref = refs[parts:]
     me = me_ref[0]
-    piece = pieces[0].shape[0]
+    piece = pieces[0].shape[0] // 2
     chunk = parts * piece
     columns = w_ref.shape[0]
     hd = columns // heads
@@ -749,7 +774,7 @@
     for c, (att, lse) in enumerate(((att0, lse0), (att1, lse1))):
         for a, k in enumerate(distances):
             start = pl.multiple_of(jnp.bitwise_xor(me, k) * piece, piece)
-            gb_ref[c, pl.ds(start, piece), :] = pieces[c * parts + a][...]
+            gb_ref[c, pl.ds(start, piece), :] = pieces[a][c * piece : (c + 1) * piece, :]
         grad = dot(gb_ref[c], w_ref[...], 1, 1).astype(B)
         ship_ref[c * chunk : (c + 1) * chunk, :] = grad
         product = grad.astype(F) * att[...].astype(F)
@@ -767,6 +792,7 @@
 def branch(me, pieces, distances, w_output, att, lse, heads):
     parts = len(distances)
     piece, width = pieces[0].shape
+    piece = piece // 2
     chunk = parts * piece
     columns = w_output.shape[0]
     extra = padded_rows(6 * heads * (chunk // columns))
@@ -779,7 +805,7 @@
         ],
         "branch",
         4 * chunk * width * columns,
-        in_specs=[scalars()] + [whole()] * (2 * parts + 5),
+        in_specs=[scalars()] + [whole()] * (parts + 5),
     )(me, *pieces, w_output, *att, *lse)
 
 
@@ -826,32 +852,31 @@
     )(place, *left, right)
 
 
-def two_columns_body(place_ref, a0, a1, r0, r1, keep_ref, send_ref):
+def two_columns_body(first_ref, second_ref, a0, a1, r0, r1, keep0, send0, keep1, send1):
     value = dot(a0[...], r0[...], 0, 0) + dot(a1[...], r1[...], 0, 0)
-    lanes = keep_ref.shape[2]
+    _, half, lanes = keep0.shape
     per = value.shape[1] // lanes
     first = pl.program_id(0) * per
     for a in range(per):
-        store_half(
-            (keep_ref, send_ref), place_ref[first + a], slice(None),
-            value[:, a * lanes : (a + 1) * lanes],
-        )
-
-
-def two_column_grads(place, left, right, docs, name):
+        c = slice(a * lanes, (a + 1) * lanes)
+        store_half((keep0, send0), first_ref[first + a], slice(None), value[:half, c])
+        store_half((keep1, send1), second_ref[first + a], slice(None), value[half:, c])
+
+
+def two_column_grads(places, left, right, docs, name):
     chunk, features = left[0].shape
     width = right[0].shape[1]
     block = max(width // docs, 256)
-    out = shape((docs // 2, features, width // docs), B)
+    out = shape((docs // 2, features // 2, width // docs), B)
     column = pl.BlockSpec((chunk, block), lambda i: (0, i))
     return call(
         two_columns_body,
-        [out, out],
+        [out] * 4,
         name,
         grid=(width // block,),
-        in_specs=[scalars()] + [resident(a.shape) for a in left] + [column, column],
-        out_specs=[resident(out.shape)] * 2,
-    )(place, *left, *right)
+        in_specs=[scalars()] * 2 + [resident(a.shape) for a in left] + [column, column],
+        out_specs=[resident(out.shape)] * 4,
+    )(*places, *left, *right)
 
 
 def key_grads_body(
@@ -891,10 +916,9 @@
     chosen_ref, me_ref, place_ref, dq_ref, *refs, count, parts, heads
 ):
     ships = refs[:count]
-    n_ref, part_ref, wq_ref, table_ref, x_ref = refs[count : count + 5]
-    out_ref = refs[count + 5 : count + 7]
-    gn_refs = refs[count + 7 : count + 9]
-    gain_ref = refs[count + 9]
+    n_ref, part_ref, wq_ref, table_ref, x_ref, mlp_ref = refs[count : count + 6]
+    out_ref = refs[count + 6 : count + 8]
+    gn_refs = refs[count + 8 : count + 10]
     chosen = chosen_ref[0]
     me = me_ref[0]
     _, chunk, columns = dq_ref.shape
@@ -924,26 +948,34 @@
         gain = part if gain is None else gain + part
         part = dot(n_ref[c], low, 0, 0)
         grads = part if grads is None else grads + part
-    gain_ref[...] = gain
-    store_slots(place_ref, out_ref, 0, grads, slice(0, columns))
-
-
-def query_grads(chosen, me, place, dq, ships, normed, part, wq, table, tokens, docs, heads):
+    gains = jnp.concatenate([gain, mlp_ref[...]], axis=0)
+    lanes = out_ref[0].shape[1] - extra_rows
+    for d in range(width // lanes):
+        rows = slice(d * lanes, (d + 1) * lanes)
+        own = jnp.concatenate([gains[:, rows], jnp.zeros((2, columns - lanes), F)], axis=1)
+        own = jnp.concatenate([own, jnp.zeros((extra_rows - 2, columns), F)], axis=0)
+        store_half(
+            out_ref, place_ref[d], slice(None), jnp.concatenate([grads[rows], own], axis=0)
+        )
+
+
+def query_grads(
+    chosen, me, place, dq, ships, normed, part, wq, table, tokens, mlp_gain, docs, heads
+):
     _, chunk, width = normed.shape
     columns = wq.shape[1]
     parts = tokens.shape[0]
     return call(
         functools.partial(query_grads_body, count=len(ships), parts=parts, heads=heads),
-        [shape((docs // 2, width // docs, columns), B)] * 2
-        + [shape((parts // 2, 2 * chunk // parts, width), B)] * 2
-        + [shape((1, width), F)],
+        [shape((docs // 2, width // docs + extra_rows, columns), B)] * 2
+        + [shape((parts // 2, 2 * chunk // parts, width), B)] * 2,
         "query_grads",
         8 * chunk * width * columns,
-        in_specs=[scalars()] * 3 + [whole()] * (len(ships) + 6),
-    )(chosen, me, place, dq, *ships, normed, part, wq, table, tokens)
-
-
-def tokens_back_body(me_ref, gn_ref, r1_ref, r2_ref, x_ref, gm0, gm1, gain_ref, out_ref):
+        in_specs=[scalars()] * 3 + [whole()] * (len(ships) + 7),
+    )(chosen, me, place, dq, *ships, normed, part, wq, table, tokens, mlp_gain)
+
+
+def tokens_back_body(me_ref, gn_ref, r1_ref, r2_ref, x_ref, gm_ref, gain_ref, out_ref):
     total = gn_ref[0].astype(F) + r1_ref[0].astype(F) + r2_ref[...].astype(F)
     x = x_ref[...].astype(F)
     factor = lax.rsqrt(jnp.mean(x * x, axis=1, keepdims=True) + epsilon)
@@ -951,9 +983,7 @@
     grad = factor * scaled - x * (factor * factor * factor) * jnp.mean(
         x * scaled, axis=1, keepdims=True
     )
-    piece = gm0.shape[0]
-    out_ref[:piece, :] = (gm0[...] + grad[:piece]).astype(B)
-    out_ref[piece:, :] = (gm1[...] + grad[piece:]).astype(B)
+    out_ref[...] = (gm_ref[...] + grad).astype(B)
 
 
 def tokens_back(me, gn, r1, r2, tokens, gm, gain):
@@ -971,13 +1001,12 @@
                 fixed((1, share, width)),
                 fixed((share, width)),
                 pl.BlockSpec((share, width), lambda i, m: (m[0], 0)),
-                fixed(gm[0].shape),
-                fixed(gm[1].shape),
+                fixed(gm.shape),
                 fixed((1, width)),
             ],
             out_specs=fixed((share, width)),
         ),
-    )(me, gn, r1, r2, tokens, *gm, gain)
+    )(me, gn, r1, r2, tokens, gm, gain)
 
 
 def rotate_table(length, hd):
@@ -1012,8 +1041,10 @@
     return (a.astype(F) + b.astype(F)).astype(B)
 
 
-def fold(keep, send, bit, *others):
+def fold(keep, send, bit, *others, hold=None):
     got = swap(after(send, *others) if others else send, "dp", 1 << bit)
+    if hold is not None:
+        got = after(got, hold)
     half = keep.shape[0] // 2
     if half == 0:
         return keep[0], got[0]
@@ -1053,7 +1084,6 @@
     columns = heads * hd
     groups = knn_index.shape[1] // 2
     spread = rows // groups
-    ff = w_gate.shape[1]
     flag = memory_flag[:1].astype(jnp.int32)
     my_doc = lax.axis_index("dp").astype(jnp.int32)
     difference = jnp.bitwise_xor(pairing[0].astype(jnp.int32), my_doc)
@@ -1062,8 +1092,11 @@
         chosen = jnp.where(difference == (1 << b), b, chosen)
     chosen = chosen.reshape(1)
     dp_order = list(range(axis_bits("dp")))
-    place = slot_place(jnp.bitwise_xor(jnp.arange(docs, dtype=jnp.int32), my_doc), dp_order)
-    place = place.astype(jnp.int32)
+    other_order = [dp_order[1], dp_order[0]] + dp_order[2:]
+    place, other_place = [
+        slot_place(jnp.bitwise_xor(jnp.arange(docs, dtype=jnp.int32), my_doc), o).astype(jnp.int32)
+        for o in (dp_order, other_order)
+    ]
     table = rotate_table(length, hd)
     gain_a = gain_attn.reshape(1, width)
     gain_m = gain_mlp.reshape(1, width)
@@ -1089,15 +1122,18 @@
     own_out, own_lse, own_sel = own_attend(
         flag, ship, own_off, stored_keys, stored_values, spread
     )
-    ships = list(after(tuple(ships), own_out, local[0]))
+    ships = list(after(tuple(ships), own_out, local[0], *out_weights))
     att, lse, their_sel, their_off, returned, pieces = [], [], [], [], [], []
+    packs = []
     for c in range(2):
         packed, sel, off, their_flag = their_attend(
             c, chosen, ships, stored_keys, stored_values, spread, groups
         )
         their_sel.append(sel)
         their_off.append(off)
+        packs.append(packed)
         returned.append(to_all(packed))
+    returned[0] = list(after(tuple(returned[0]), packs[1]))
     for c in range(2):
         a, log_total = merge(c, chosen, local, (own_out, own_lse), returned[c], heads)
         att.append(a)
@@ -1106,8 +1142,7 @@
 
     feeds, back = [], []
     for c in range(2):
-        if c:
-            pieces[c] = list(after(tuple(pieces[c]), back[0][1]))
+        pieces[c] = list(after(tuple(pieces[c]), feeds[0][0] if c else att[1]))
         feeds.append(
             feed(
                 c, me, pieces[c], out_weights, tokens_view, cotangent_view, gain_m, w_gate.T,
@@ -1117,88 +1152,101 @@
         keep, send = feeds[c][3], feeds[c][4]
         first = swap(send, "tensor", 1)
         back.append((first, add_low(keep[1], first[1])))
-    gm, gb_pieces, gain_parts = [], [], []
-    for c in range(2):
-        first, second = back[c]
-        grad_middle, low, gain_part = middle_back(
-            c, me, feeds[c][3], first, swap(second, "tensor", 2), feeds[c][7], cotangent_view,
-            gain_m
-        )
-        gm.append(grad_middle)
-        gain_parts.append(gain_part)
-        gb_pieces += gather_tensor(low)[0]
-    down_slots = column_grads(
-        place, after((feeds[0][2], feeds[1][2]), back[1][1]), cotangent_view, docs, "down_grads"
-    )
-    down_half = fold(*down_slots, dp_order[0])
+    rows_back = (back[0][1], back[1][1])
     gate_slots = two_column_grads(
-        place,
-        after((feeds[0][1], feeds[1][1]), gm[1], down_slots[1]),
+        (place, other_place),
+        after((feeds[0][1], feeds[1][1]), *rows_back),
         (feeds[0][0], feeds[1][0]),
         docs,
         "gate_grads",
     )
+    partial, seconds = [], []
+    for c in range(2):
+        keep, send = feeds[c][5], after(feeds[c][6], *rows_back)
+        first = swap(send, "tensor", 1)
+        seconds.append(add_low(keep[1], first[1]))
+        partial.append(feeds[c][7] + keep[0].astype(F) + first[0].astype(F))
+    seconds = jnp.concatenate(seconds, axis=0)
+    partial = jnp.concatenate(partial, axis=0)
+    arrived = [swap(second, "tensor", 2) for _, second in back]
+    arrived = after(tuple(arrived), gate_slots[1], seconds, partial)
+    gm, low, gain_part = middle_back(
+        me,
+        [(feeds[c][3], back[c][0], arrived[c], feeds[c][7]) for c in range(2)],
+        cotangent_view,
+        gain_m,
+    )
+    gb_pieces, _ = gather_tensor(low)
+    gate_half = fold(*gate_slots[:2], dp_order[0], hold=low)
+    up_half = fold(*gate_slots[2:], other_order[0], hold=low)
+    down_slots = column_grads(
+        place,
+        after((feeds[0][2], feeds[1][2]), low, gate_half[1], up_half[1]),
+        cotangent_view,
+        docs,
+        "down_grads",
+    )
 
     grad_branch, back_ship, stats = branch(
-        me, after(tuple(gb_pieces), gate_slots[0]), distances, w_output, att, lse, heads
-    )
+        me, after(tuple(gb_pieces), down_slots[1]), distances, w_output, att, lse, heads
+    )
+    gate_half = fold(*gate_half, dp_order[1], hold=back_ship)
+    up_half = fold(*up_half, other_order[1], hold=back_ship)
     back_ships = to_all(back_ship)
+    down_half = fold(*down_slots, dp_order[0], gate_half[1], up_half[1])
     local_dq, dkv = local_backward(q, k, v, back_ship, stats, table, heads, parts)
-    gate_half = fold(*gate_slots, dp_order[0], local_dq)
     dq = own_backward(
         flag, back_ship, stats, own_sel, own_off, stored_keys, stored_values, local_dq, spread
     )
-    down_half = fold(*down_half, dp_order[1], dq)
+    second = swap(after(seconds, back_ship), "tensor", 2)
+    output = (partial + second.astype(F)).astype(B)
+    back_ships = list(after(tuple(back_ships), dq, gate_half[1], up_half[1], output, down_half[1]))
     their_dq = their_backward(
-        chosen, their_flag, list(after(tuple(back_ships), dq)), their_sel, their_off, stored_keys,
-        stored_values, spread
-    )
+        chosen, their_flag, back_ships, their_sel, their_off, stored_keys, stored_values, spread
+    )
+    down_half = fold(*down_half, dp_order[1], back_ships[0], hold=their_dq)
+    if len(dp_order) > 2:
+        gate_half = fold(*gate_half, dp_order[2], back_ships[0], hold=their_dq)
     dq_ships = to_all(their_dq)
 
     keep, send, gn_part = key_grads(
         place, normed_low, after(dkv, their_dq), grad_branch, att, w_key, w_value, docs
     )
-    down_half = fold(*down_half, dp_order[2], their_dq) if len(dp_order) > 2 else down_half
     key_half = fold(keep, send, dp_order[0])
-    gate_half = fold(*gate_half, dp_order[1], their_dq)
-    output = []
-    for c in range(2):
-        keep, send = feeds[c][5], after(feeds[c][6], their_dq)
-        first = swap(send, "tensor", 1)
-        second = swap(add_low(keep[1], first[1]), "tensor", 2)
-        output.append(
-            feeds[c][7] + keep[0].astype(F) + first[0].astype(F) + second.astype(F)
-        )
-    keep, send, gn_keep, gn_send, gain_part = query_grads(
+    keep, send, gn_keep, gn_send = query_grads(
         chosen, me, place, dq, dq_ships, normed_low, gn_part, w_query, table_view, tokens_view,
-        docs, heads
-    )
+        gain_part, docs, heads
+    )
+    first = swap(gn_send, "tensor", 1)
     query_half = fold(keep, send, dp_order[0])
-    first = swap(gn_send, "tensor", 1)
-    second = swap(add_low(gn_keep[1], first[1]), "tensor", 2)
-    grad_tokens = tokens_back(me, gn_keep, first, second, tokens, gm, gain_a)
-    for b in dp_order[1:]:
-        query_half = fold(*query_half, b)
+    second = add_low(gn_keep[1], first[1])
+    last = swap(second, "tensor", 2)
+    query_half = fold(*query_half, dp_order[1], second)
+    key_half = fold(*key_half, dp_order[1], gn_send)
+    for b in dp_order[2:]:
         key_half = fold(*key_half, b)
+        query_half = fold(*query_half, b, key_half[1])
+    if len(dp_order) > 2:
+        up_half = fold(*up_half, other_order[2], their_dq, hold=second)
     for b in dp_order[2:]:
+        down_half = fold(*down_half, b, gn_send, hold=key_half[1])
+    for b in dp_order[3:]:
         gate_half = fold(*gate_half, b)
-    for b in dp_order[3:]:
-        down_half = fold(*down_half, b)
-    gains = jnp.concatenate([gain_part, gain_parts[0] + gain_parts[1]], axis=0)
+        up_half = fold(*up_half, b)
+    grad_tokens = tokens_back(me, gn_keep, first, last, tokens, gm, gain_a)
+    query_total = total(query_half)
+    lanes = width // docs
+    gains = query_total[lanes : lanes + 8, :lanes]
     gains = gains + sum(swap(gains, "tensor", t) for t in range(1, parts))
-    for b in dp_order:
-        gains = gains + swap(gains, "dp", 1 << b)
-    gains = lax.dynamic_slice_in_dim(gains, my_doc * (width // docs), width // docs, 1)
-    gate_pair = gate_half
     return (
-        jnp.concatenate(output, axis=0).astype(B),
+        output,
         grad_tokens,
-        total(query_half),
+        query_total[:lanes],
         total(key_half, slice(0, columns)),
         total(key_half, slice(columns, 2 * columns)),
         total(key_half, slice(2 * columns, None)).T,
-        (gate_pair[0][:ff].astype(F) + gate_pair[1][:ff].astype(F)).T,
-        (gate_pair[0][ff:].astype(F) + gate_pair[1][ff:].astype(F)).T,
+        total(gate_half).T,
+        total(up_half).T,
         total(down_half),
         gains[0],
         gains[1],

time: 342 us -> 283 us (0.83)
  local copies, waits for them, and re-layouts: 41.2 us -> 17.3 us
  waiting for transfers between devices: 129 us -> 112 us
  starting transfers between devices: 56.6 us -> 41.4 us
    unnamed x195 -> x109, local copies, waits for them, and re-layouts: 36.6 us -> 13.3 us
    ppermute x58 -> x54, waiting for transfers between devices: 129 us -> 112 us  [swap(): lax.ppermute(array, axis, [(i, i ^ bit) for i in range(lax.axis_size(axis...]
    ppermute x58 -> x54, starting transfers between devices: 56.6 us -> 41.4 us  [swap(): lax.ppermute(array, axis, [(i, i ^ bit) for i in range(lax.axis_size(axis...]
    pallas_call x20 -> x19, Pallas kernels: 95.5 us -> 94.4 us  [run(): return kernel(*args)]
  transfers between devices with their start and end apart: 58 -> 54, of which waited for: 25 -> 23; matrix products, arithmetic and copies ran while one was open for 5% -> 5% of each run, Pallas kernels for 24% -> 25%
where the time goes in v4:
time: 283 us; the launch traced here: 278 us
  waiting for transfers between devices  112 us (40%)
  Pallas kernels  94.4 us (33%)
  starting transfers between devices  41.4 us (15%)
  local copies, waits for them, and re-layouts  17.3 us (6%)
  other arithmetic  9.47 us (3%)
  between operations  3.27 us (1%)
    ppermute x54, waiting for transfers between devices, swap(): lax.ppermute(array, axis, [(i, i ^ bit) for i in range(lax.axis_size(axis...  112 us
    pallas_call x19, Pallas kernels, run(): return kernel(*args)  94.4 us
    ppermute x54, starting transfers between devices, swap(): lax.ppermute(array, axis, [(i, i ^ bit) for i in range(lax.axis_size(axis...  41.4 us
    unnamed x109, local copies, waits for them, and re-layouts  13.3 us
  transfers between devices with their start and end apart: 54, of which 23 were waited for; matrix products, arithmetic and copies ran while one was open for 5% of the time, Pallas kernels for 25%

profile of v4, /device:TPU:0, one launch (start us, length us, event | category | flops | bytes accessed | tf_op | source)
XLA Modules:
  0.0 277.8 jit_solution(9921418408618488620)
XLA Ops:
  4.4 5.6 %project.1 = (bf16[2,640,256]{2,1,0:T(8,128)(2,1)}, bf16[1024,256]{1,0:T(8,128)(2,1)S(1)}, bf16[1024,256]{1,0:T(8,128)(2,1)S(1)}, bf16[1024,256]{1,0:T(8,128)(2,...) custom-call(s32[1]{0:T(128)S(6)} %copy.31.flag_ref, bf16[1024,1024]{1,0:T(8,128)(2,1)} %x_ref.3, ...), custom_call_target="tpu_custom_call" | custom-call | flops 3909999872 | tf_op jit(solution)/shard_map/project/pallas_call | solution.py:57
  19.3 8.3 %own_attend.1 = (bf16[2,512,256]{2,1,0:T(8,128)(2,1)S(1)}, f32[2,2,512]{2,1,0:T(2,128)S(1)}, f32[2,2,64,512]{3,2,1,0:T(8,128)S(1)}) custom-call(s32[1]{0:T(128)S(6)} %copy.31.flag_ref, bf16[2,640,256]{2,1,0:T(8,128)(2,1)} %get-tuple-element.122.ship_ref, bf16[2,64,512]{2,1,0:T(8,128)(2,1)S(1)} %get-tuple-element.123.off_ref, ...), custom_call_target="tpu_custom_call" | custom-call | flops 10350000128 | tf_op jit(solution)/shard_map/own_attend/pallas_call | solution.py:57
  36.5 5.0 %collective-permute-done.1.refs_1_ = bf16[2,640,256]{2,1,0:T(8,128)(2,1)S(1)} collective-permute-done((bf16[2,640,256]{2,1,0:T(8,128)(2,1)}, bf16[2,640,256]{2,1,0:T(8,128)(2,1)S(1)}, u32[]{:S(2)}, u32[]{:S(2)}) %collective-permute-start.1) | collective-permute-done | bytes 655392 | tf_op jit(solution)/shard_map/ppermute | solution.py:29
  44.1 5.2 %their_attend.2 = (bf16[528,256]{1,0:T(8,128)(2,1)S(1)}, f32[2,64,512]{2,1,0:T(8,128)S(1)}, bf16[64,512]{1,0:T(8,128)(2,1)S(1)}, s32[1]{0:T(128)}) custom-call(s32[1]{0:T(128)} %bitcast.2.chosen_ref, bf16[2,640,256]{2,1,0:T(8,128)(2,1)S(1)} %collective-permute-done.refs_0_, bf16[2,640,256]{2,1,0:T(8,128)(2,1)S(1)} %collective-permute-done.1.refs_1_, ...), custom_call_target="tpu_custom_call" | custom-call | flops 6095000064 | tf_op jit(solution)/shard_map/their_attend/pallas_call | solution.py:57
  52.5 5.4 %their_attend.3 = (bf16[528,256]{1,0:T(8,128)(2,1)S(1)}, f32[2,64,512]{2,1,0:T(8,128)S(1)}, bf16[64,512]{1,0:T(8,128)(2,1)S(1)}, s32[1]{0:T(128)}) custom-call(s32[1]{0:T(128)} %bitcast.2.chosen_ref, bf16[2,640,256]{2,1,0:T(8,128)(2,1)S(1)} %collective-permute-done.refs_0_, bf16[2,640,256]{2,1,0:T(8,128)(2,1)S(1)} %collective-permute-done.1.refs_1_, ...), custom_call_target="tpu_custom_call" | custom-call | flops 6095000064 | tf_op jit(solution)/shard_map/their_attend/pallas_call | solution.py:57
  62.0 4.4 %collective-permute-done.8.refs_2_ = bf16[528,256]{1,0:T(8,128)(2,1)S(1)} collective-permute-done((bf16[528,256]{1,0:T(8,128)(2,1)S(1)}, bf16[528,256]{1,0:T(8,128)(2,1)S(1)}, u32[]{:S(2)}, u32[]{:S(2)}) %collective-permute-start.8) | collective-permute-done | bytes 270368 | tf_op jit(solution)/shard_map/ppermute | solution.py:29
  70.4 4.5 %collective-permute-done.14.refs_2_ = bf16[528,256]{1,0:T(8,128)(2,1)S(1)} collective-permute-done((bf16[528,256]{1,0:T(8,128)(2,1)S(1)}, bf16[528,256]{1,0:T(8,128)(2,1)S(1)}, u32[]{:S(2)}, u32[]{:S(2)}) %collective-permute-start.14) | collective-permute-done | bytes 270368 | tf_op jit(solution)/shard_map/ppermute | solution.py:29
  77.9 6.3 %collective-permute-done.16.refs_1_ = bf16[512,256]{1,0:T(8,128)(2,1)} collective-permute-done((bf16[512,256]{1,0:T(8,128)(2,1)}, bf16[512,256]{1,0:T(8,128)(2,1)}, u32[]{:S(2)}, u32[]{:S(2)}) %collective-permute-start.16) | collective-permute-done | bytes 262176 | tf_op jit(solution)/shard_map/ppermute | solution.py:29
  90.1 10.2 %feed.2 = (bf16[512,1024]{1,0:T(8,128)(2,1)S(1)}, bf16[512,1408]{1,0:T(8,128)(2,1)S(1)}, bf16[512,704]{1,0:T(8,128)(2,1)S(1)}, bf16[2,128,1024]{2,1,0:T(8,128)(2...) custom-call(s32[1]{0:T(128)} %bitcast.me_ref, ...), custom_call_target="tpu_custom_call" | custom-call | flops 11269999616 | tf_op jit(solution)/shard_map/feed/pallas_call | solution.py:57
  100.4 10.5 %feed.3 = (bf16[512,1024]{1,0:T(8,128)(2,1)S(1)}, bf16[512,1408]{1,0:T(8,128)(2,1)S(1)}, bf16[512,704]{1,0:T(8,128)(2,1)S(1)}, bf16[2,128,1024]{2,1,0:T(8,128)(2...) custom-call(s32[1]{0:T(128)} %bitcast.me_ref, ...), custom_call_target="tpu_custom_call" | custom-call | flops 11269999616 | tf_op jit(solution)/shard_map/feed/pallas_call | solution.py:57
  115.8 5.2 %gate_grads.1 = (bf16[4,704,128]{2,1,0:T(8,128)(2,1)S(1)}, bf16[4,704,128]{2,1,0:T(8,128)(2,1)S(1)}, bf16[4,704,128]{2,1,0:T(8,128)(2,1)S(1)}, bf16[4,704,128]{2,1,0:T(8,128)(2,1)S(1)}) custom-call(s32[8]{0:T(128)S(1)} %multiply_add_fusion.1.first_ref.place_ref, s32[8]{0:T(128)S(1)} %multiply_add_fusion.second_ref, ...), custom_call_target="tpu_custom_call" | custom-call | flops 7129999872 | tf_op jit(solution)/shard_map/gate_grads/pallas_call | solution.py:57
  122.9 4.4 %collective-permute-done.22.refs_2_ = bf16[128,1024]{1,0:T(8,128)(2,1)S(1)} collective-permute-done((bf16[128,1024]{1,0:T(8,128)(2,1)S(1)}, bf16[128,1024]{1,0:T(8,128)(2,1)S(1)}, u32[]{:S(2)}, u32[]{:S(2)}) %collective-permute-start.22) | collective-permute-done | bytes 262176 | tf_op jit(solution)/shard_map/ppermute | solution.py:29
  128.9 10.3 %collective-permute-done.28 = bf16[4,704,128]{2,1,0:T(8,128)(2,1)S(1)} collective-permute-done((bf16[4,704,128]{2,1,0:T(8,128)(2,1)S(1)}, bf16[4,704,128]{2,1,0:T(8,128)(2,1)S(1)}, u32[]{:S(2)}, u32[]{:S(2)}) %collective-permute-start.28) | collective-permute-done | bytes 720928 | tf_op jit(solution)/shard_map/ppermute | solution.py:29
  155.5 4.3 %local_backward.1 = (f32[2,512,256]{2,1,0:T(8,128)S(1)}, bf16[2,512,512]{2,1,0:T(8,128)(2,1)S(1)}) custom-call(bf16[1024,256]{1,0:T(8,128)(2,1)S(1)} %copy-done.24, bf16[1024,256]{1,0:T(8,128)(2,1)S(1)} %copy-done.27, bf16[1024,256]{1,0:T(8,128)(2,1)S(1)} %copy-done.30, bf16[1088,256]{1,0:T(8,128)(2,1)S(1)} %get-tuple-element.182.ship_ref, ...), custom_call_target="tpu_custom_call" | custom-call | flops 4830000128 | tf_op jit(solution)/shard_map/local_backward/pallas_call | solution.py:57
  160.4 7.4 %own_backward.1.dq_ref = f32[2,512,256]{2,1,0:T(8,128)S(1)} custom-call(s32[1]{0:T(128)S(6)} %copy.31.flag_ref, bf16[1088,256]{1,0:T(8,128)(2,1)S(1)} %get-tuple-element.182.ship_ref, f32[2,4,512]{2,1,0:T(4,128)S(1)} %get-tuple-element.184.st_ref, f32[2,2,64,512]{3,2,1,0:T(8,128)S(1)} %copy-done.34, bf16[2,64,512]{2,1,0:T(8,128)(2,1)S(1)} %copy-done.32, ...), custom_call_target="tpu_custom_call" | custom-call | flops 8280000000 | tf_op jit(solution)/shard_map/own_backward/pallas_call | solution.py:57
  167.8 4.8 %collective-permute-done.29 = bf16[256,1024]{1,0:T(8,128)(2,1)S(1)} collective-permute-done((bf16[256,1024]{1,0:T(8,128)(2,1)S(1)}, bf16[256,1024]{1,0:T(8,128)(2,1)S(1)}, u32[]{:S(2)}, u32[]{:S(2)}) %collective-permute-start.29) | collective-permute-done | bytes 524320 | tf_op jit(solution)/shard_map/ppermute | solution.py:29
  173.6 6.4 %collective-permute-done.35 = bf16[4,704,128]{2,1,0:T(8,128)(2,1)S(1)} collective-permute-done((bf16[4,704,128]{2,1,0:T(8,128)(2,1)S(1)}, bf16[4,704,128]{2,1,0:T(8,128)(2,1)S(1)}, u32[]{:S(2)}, u32[]{:S(2)}) %collective-permute-start.35) | collective-permute-done | bytes 720928 | tf_op jit(solution)/shard_map/ppermute | solution.py:29
  180.3 7.9 %their_backward.1 = bf16[1024,256]{1,0:T(8,128)(2,1)S(1)} custom-call(s32[1]{0:T(128)} %bitcast.2.chosen_ref, s32[1]{0:T(128)} %get-tuple-element.187.flag_ref, bf16[1088,256]{1,0:T(8,128)(2,1)S(1)} %collective-permute-done.30.refs_0_, bf16[1088,256]{1,0:T(8,128)(2,1)S(1)} %collective-permute-done.31.refs_1_, ...), custom_call_target="tpu_custom_call" | custom-call | flops 9774999552 | tf_op jit(solution)/shard_map/their_backward/pallas_call | solution.py:57
  189.9 5.7 %key_grads.1 = (bf16[4,128,768]{2,1,0:T(8,128)(2,1)S(1)}, bf16[4,128,768]{2,1,0:T(8,128)(2,1)S(1)}, bf16[2,512,1024]{2,1,0:T(8,128)(2,1)S(1)}) custom-call(s32[8]{0:T(128)S(1)} %multiply_add_fusion.1.first_ref.place_ref, bf16[2,512,1024]{2,1,0:T(8,128)(2,1)S(1)} %copy-done.19, bf16[2,512,512]{2,1,0:T(8,128)(2,1)S(1)} %get-tuple-element.201.dkv_ref, ...), custom_call_target="tpu_custom_call" | custom-call | flops 6440000000 | tf_op jit(solution)/shard_map/key_grads/pallas_call | solution.py:57
  199.0 23.6 %collective-permute-done.47 = bf16[1,704,128]{2,1,0:T(8,128)(2,1)S(1)} collective-permute-done((bf16[1,704,128]{2,1,0:T(8,128)(2,1)S(1)}, bf16[1,704,128]{2,1,0:T(8,128)(2,1)S(1)}, u32[]{:S(2)}, u32[]{:S(2)}) %collective-permute-start.47) | collective-permute-done | bytes 180256 | tf_op jit(solution)/shard_map/ppermute | solution.py:29
  223.8 4.5 %query_grads.1 = (bf16[4,144,256]{2,1,0:T(8,128)(2,1)S(1)}, bf16[4,144,256]{2,1,0:T(8,128)(2,1)S(1)}, bf16[2,256,1024]{2,1,0:T(8,128)(2,1)S(1)}, bf16[2,256,1024]{2,1,0:T(8,128)(2,1)}) custom-call(s32[1]{0:T(128)} %bitcast.2.chosen_ref, s32[1]{0:T(128)} %bitcast.me_ref, s32[8]{0:T(128)S(1)} %multiply_add_fusion.1.first_ref.place_ref, ...), custom_call_target="tpu_custom_call" | custom-call | flops 4944999936 | tf_op jit(solution)/shard_map/query_grads/pallas_call | solution.py:57
  230.2 6.1 %collective-permute-done.49 = bf16[2,704,128]{2,1,0:T(8,128)(2,1)S(1)} collective-permute-done((bf16[2,704,128]{2,1,0:T(8,128)(2,1)S(1)}, bf16[2,704,128]{2,1,0:T(8,128)(2,1)S(1)}, u32[]{:S(2)}, u32[]{:S(2)}) %collective-permute-start.49) | collective-permute-done | bytes 360480 | tf_op jit(solution)/shard_map/ppermute | solution.py:29
  237.6 9.2 %collective-permute-done.44 = bf16[2,128,768]{2,1,0:T(8,128)(2,1)S(1)} collective-permute-done((bf16[2,128,768]{2,1,0:T(8,128)(2,1)S(1)}, bf16[2,128,768]{2,1,0:T(8,128)(2,1)S(1)}, u32[]{:S(2)}, u32[]{:S(2)}) %collective-permute-start.44) | collective-permute-done | bytes 393248 | tf_op jit(solution)/shard_map/ppermute | solution.py:29
  247.7 9.0 %collective-permute-done.45 = bf16[1,128,768]{2,1,0:T(8,128)(2,1)S(1)} collective-permute-done((bf16[1,128,768]{2,1,0:T(8,128)(2,1)S(1)}, bf16[1,128,768]{2,1,0:T(8,128)(2,1)S(1)}, u32[]{:S(2)}, u32[]{:S(2)}) %collective-permute-start.45) | collective-permute-done | bytes 196640 | tf_op jit(solution)/shard_map/ppermute | solution.py:29
  (243 shorter events, 100.5 us)
Async XLA Ops:
  0.6 18.1 %collective-permute-start.3 = (bf16[256,1024]{1,0:T(8,128)(2,1)}, bf16[256,1024]{1,0:T(8,128)(2,1)}, u32[]{:S(2)}, u32[]{:S(2)}) collective-permute-start(bf16[256,1024]{1,0:T(8,128)(2,1)} %refs_4_.5), channel_id=1, source_target_pairs={{0,2},{1,3},{2,0},{3,1},{4,6},{5,7},{6,4},{7,5},{8,10},{9,11},{10,... | collective-permute-start | bytes 1572872 | tf_op jit(solution)/shard_map/ppermute | solution.py:29
  10.0 26.5 %collective-permute-start = (bf16[2,640,256]{2,1,0:T(8,128)(2,1)}, bf16[2,640,256]{2,1,0:T(8,128)(2,1)S(1)}, u32[]{:S(2)}, u32[]{:S(2)}) collective-permute-start(bf16[2,640,256]{2,1,0:T(8,128)(2,1)} %get-tuple-element.122.ship_ref), channel_id=1, source_target_pairs={{0,4},{4,0},{8,12},{12,8},{16,20},{20,16},{24,28},{28,24},{1,5},{5... | collective-permute-start | bytes 1966088 | tf_op jit(solution)/shard_map/ppermute | solution.py:29
  11.6 30.0 %collective-permute-start.1 = (bf16[2,640,256]{2,1,0:T(8,128)(2,1)}, bf16[2,640,256]{2,1,0:T(8,128)(2,1)S(1)}, u32[]{:S(2)}, u32[]{:S(2)}) collective-permute-start(bf16[2,640,256]{2,1,0:T(8,128)(2,1)} %get-tuple-element.122.ship_ref), channel_id=1, source_target_pairs={{0,8},{4,12},{8,0},{12,4},{16,24},{20,28},{24,16},{28,20},{1,9},{5... | collective-permute-start | bytes 1966088 | tf_op jit(solution)/shard_map/ppermute | solution.py:29
  13.1 31.0 %collective-permute-start.2 = (bf16[2,640,256]{2,1,0:T(8,128)(2,1)}, bf16[2,640,256]{2,1,0:T(8,128)(2,1)}, u32[]{:S(2)}, u32[]{:S(2)}) collective-permute-start(bf16[2,640,256]{2,1,0:T(8,128)(2,1)} %get-tuple-element.122.ship_ref), channel_id=1, source_target_pairs={{0,16},{4,20},{8,24},{12,28},{16,0},{20,4},{24,8},{28,12},{1,17},{... | collective-permute-start | bytes 1966088 | tf_op jit(solution)/shard_map/ppermute | solution.py:29
  15.7 20.8 %collective-permute-start.4 = (bf16[256,1024]{1,0:T(8,128)(2,1)}, bf16[256,1024]{1,0:T(8,128)(2,1)}, u32[]{:S(2)}, u32[]{:S(2)}) collective-permute-start(bf16[256,1024]{1,0:T(8,128)(2,1)} %refs_4_.5), channel_id=1, source_target_pairs={{0,1},{1,0},{2,3},{3,2},{4,5},{5,4},{6,7},{7,6},{8,9},{9,8},{10,11... | collective-permute-start | bytes 1572872 | tf_op jit(solution)/shard_map/ppermute | solution.py:29
  18.7 25.4 %collective-permute-start.5 = (bf16[256,1024]{1,0:T(8,128)(2,1)}, bf16[256,1024]{1,0:T(8,128)(2,1)}, u32[]{:S(2)}, u32[]{:S(2)}) collective-permute-start(bf16[256,1024]{1,0:T(8,128)(2,1)} %collective-permute-done.3.refs_5_), channel_id=1, source_target_pairs={{0,1},{1,0},{2,3},{3,2},{4,5},{5,4},{6,7},{7,6},{8,9},{9,8},{10,11... | collective-permute-start | bytes 1572872 | tf_op jit(solution)/shard_map/ppermute | solution.py:29
  50.3 16.1 %collective-permute-start.8 = (bf16[528,256]{1,0:T(8,128)(2,1)S(1)}, bf16[528,256]{1,0:T(8,128)(2,1)S(1)}, u32[]{:S(2)}, u32[]{:S(2)}) collective-permute-start(bf16[528,256]{1,0:T(8,128)(2,1)S(1)} %get-tuple-element.129), channel_id=1, source_target_pairs={{0,16},{4,20},{8,24},{12,28},{16,0},{20,4},{24,8},{28,12},{1,17},{... | collective-permute-start | bytes 811016 | tf_op jit(solution)/shard_map/ppermute | solution.py:29
  77.9 22.5 %collective-permute-start.17 = (bf16[512,256]{1,0:T(8,128)(2,1)}, bf16[512,256]{1,0:T(8,128)(2,1)S(1)}, u32[]{:S(2)}, u32[]{:S(2)}) collective-permute-start(bf16[512,256]{1,0:T(8,128)(2,1)} %get-tuple-element.146.refs_0_.refs_6_.att1), channel_id=1, source_target_pairs={{0,1},{1,0},{2,3},{3,2},{4,5},{5,4},{6,7},{7,6},{8,9},{9,8},{10,11... | collective-permute-start | bytes 786440 | tf_op jit(solution)/shard_map/ppermute | solution.py:29
  84.2 16.2 %collective-permute-start.18 = (bf16[512,256]{1,0:T(8,128)(2,1)}, bf16[512,256]{1,0:T(8,128)(2,1)S(1)}, u32[]{:S(2)}, u32[]{:S(2)}) collective-permute-start(bf16[512,256]{1,0:T(8,128)(2,1)} %collective-permute-done.16.refs_1_), channel_id=1, source_target_pairs={{0,1},{1,0},{2,3},{3,2},{4,5},{5,4},{6,7},{7,6},{8,9},{9,8},{10,11... | collective-permute-start | bytes 786440 | tf_op jit(solution)/shard_map/ppermute | solution.py:29
  121.0 18.1 %collective-permute-start.28 = (bf16[4,704,128]{2,1,0:T(8,128)(2,1)S(1)}, bf16[4,704,128]{2,1,0:T(8,128)(2,1)S(1)}, u32[]{:S(2)}, u32[]{:S(2)}) collective-permute-start(bf16[4,704,128]{2,1,0:T(8,128)(2,1)S(1)} %get-tuple-element.171), channel_id=1, source_target_pairs={{0,8},{4,12},{8,0},{12,4},{16,24},{20,28},{24,16},{28,20},{1,9},{5... | collective-permute-start | bytes 2162696 | tf_op jit(solution)/shard_map/ppermute | solution.py:29
  121.1 18.1 %collective-permute-start.27 = (bf16[4,704,128]{2,1,0:T(8,128)(2,1)S(1)}, bf16[4,704,128]{2,1,0:T(8,128)(2,1)S(1)}, u32[]{:S(2)}, u32[]{:S(2)}) collective-permute-start(bf16[4,704,128]{2,1,0:T(8,128)(2,1)S(1)} %get-tuple-element.162), channel_id=1, source_target_pairs={{0,4},{4,0},{8,12},{12,8},{16,20},{20,16},{24,28},{28,24},{1,5},{5... | collective-permute-start | bytes 2162696 | tf_op jit(solution)/shard_map/ppermute | solution.py:29
  128.7 18.2 %collective-permute-start.25 = (bf16[256,1024]{1,0:T(8,128)(2,1)S(1)}, bf16[256,1024]{1,0:T(8,128)(2,1)S(1)}, u32[]{:S(2)}, u32[]{:S(2)}) collective-permute-start(bf16[256,1024]{1,0:T(8,128)(2,1)S(1)} %get-tuple-element.176.refs_0_), channel_id=1, source_target_pairs={{0,1},{1,0},{2,3},{3,2},{4,5},{5,4},{6,7},{7,6},{8,9},{9,8},{10,11... | collective-permute-start | bytes 1572872 | tf_op jit(solution)/shard_map/ppermute | solution.py:29
  149.4 30.8 %collective-permute-start.30 = (bf16[1088,256]{1,0:T(8,128)(2,1)S(1)}, bf16[1088,256]{1,0:T(8,128)(2,1)S(1)}, u32[]{:S(2)}, u32[]{:S(2)}) collective-permute-start(bf16[1088,256]{1,0:T(8,128)(2,1)S(1)} %get-tuple-element.182.ship_ref), channel_id=1, source_target_pairs={{0,4},{4,0},{8,12},{12,8},{16,20},{20,16},{24,28},{28,24},{1,5},{5... | collective-permute-start | bytes 1671176 | tf_op jit(solution)/shard_map/ppermute | solution.py:29
  150.0 30.2 %collective-permute-start.31 = (bf16[1088,256]{1,0:T(8,128)(2,1)S(1)}, bf16[1088,256]{1,0:T(8,128)(2,1)S(1)}, u32[]{:S(2)}, u32[]{:S(2)}) collective-permute-start(bf16[1088,256]{1,0:T(8,128)(2,1)S(1)} %get-tuple-element.182.ship_ref), channel_id=1, source_target_pairs={{0,8},{4,12},{8,0},{12,4},{16,24},{20,28},{24,16},{28,20},{1,9},{5... | collective-permute-start | bytes 1671176 | tf_op jit(solution)/shard_map/ppermute | solution.py:29
  150.0 30.2 %collective-permute-start.32 = (bf16[1088,256]{1,0:T(8,128)(2,1)S(1)}, bf16[1088,256]{1,0:T(8,128)(2,1)S(1)}, u32[]{:S(2)}, u32[]{:S(2)}) collective-permute-start(bf16[1088,256]{1,0:T(8,128)(2,1)S(1)} %get-tuple-element.182.ship_ref), channel_id=1, source_target_pairs={{0,16},{4,20},{8,24},{12,28},{16,0},{20,4},{24,8},{28,12},{1,17},{... | collective-permute-start | bytes 1671176 | tf_op jit(solution)/shard_map/ppermute | solution.py:29
  153.8 26.2 %collective-permute-start.35 = (bf16[4,704,128]{2,1,0:T(8,128)(2,1)S(1)}, bf16[4,704,128]{2,1,0:T(8,128)(2,1)S(1)}, u32[]{:S(2)}, u32[]{:S(2)}) collective-permute-start(bf16[4,704,128]{2,1,0:T(8,128)(2,1)S(1)} %get-tuple-element.191), channel_id=1, source_target_pairs={{0,4},{4,0},{8,12},{12,8},{16,20},{20,16},{24,28},{28,24},{1,5},{5... | collective-permute-start | bytes 2162696 | tf_op jit(solution)/shard_map/ppermute | solution.py:29
  188.2 34.4 %collective-permute-start.36 = (bf16[1024,256]{1,0:T(8,128)(2,1)S(1)}, bf16[1024,256]{1,0:T(8,128)(2,1)S(1)}, u32[]{:S(2)}, u32[]{:S(2)}) collective-permute-start(bf16[1024,256]{1,0:T(8,128)(2,1)S(1)} %their_backward.1), channel_id=1, source_target_pairs={{0,4},{4,0},{8,12},{12,8},{16,20},{20,16},{24,28},{28,24},{1,5},{5... | collective-permute-start | bytes 1572872 | tf_op jit(solution)/shard_map/ppermute | solution.py:29
  188.3 35.5 %collective-permute-start.37 = (bf16[1024,256]{1,0:T(8,128)(2,1)S(1)}, bf16[1024,256]{1,0:T(8,128)(2,1)S(1)}, u32[]{:S(2)}, u32[]{:S(2)}) collective-permute-start(bf16[1024,256]{1,0:T(8,128)(2,1)S(1)} %their_backward.1), channel_id=1, source_target_pairs={{0,8},{4,12},{8,0},{12,4},{16,24},{20,28},{24,16},{28,20},{1,9},{5... | collective-permute-start | bytes 1572872 | tf_op jit(solution)/shard_map/ppermute | solution.py:29
  189.8 34.0 %collective-permute-start.38 = (bf16[1024,256]{1,0:T(8,128)(2,1)S(1)}, bf16[1024,256]{1,0:T(8,128)(2,1)S(1)}, u32[]{:S(2)}, u32[]{:S(2)}) collective-permute-start(bf16[1024,256]{1,0:T(8,128)(2,1)S(1)} %their_backward.1), channel_id=1, source_target_pairs={{0,16},{4,20},{8,24},{12,28},{16,0},{20,4},{24,8},{28,12},{1,17},{... | collective-permute-start | bytes 1572872 | tf_op jit(solution)/shard_map/ppermute | solution.py:29
  195.6 32.8 %collective-permute-start.43 = (bf16[4,128,768]{2,1,0:T(8,128)(2,1)S(1)}, bf16[4,128,768]{2,1,0:T(8,128)(2,1)S(1)}, u32[]{:S(2)}, u32[]{:S(2)}) collective-permute-start(bf16[4,128,768]{2,1,0:T(8,128)(2,1)S(1)} %get-tuple-element.212), channel_id=1, source_target_pairs={{0,4},{4,0},{8,12},{12,8},{16,20},{20,16},{24,28},{28,24},{1,5},{5... | collective-permute-start | bytes 2359304 | tf_op jit(solution)/shard_map/ppermute | solution.py:29
  197.5 25.1 %collective-permute-start.47 = (bf16[1,704,128]{2,1,0:T(8,128)(2,1)S(1)}, bf16[1,704,128]{2,1,0:T(8,128)(2,1)S(1)}, u32[]{:S(2)}, u32[]{:S(2)}) collective-permute-start(bf16[1,704,128]{2,1,0:T(8,128)(2,1)S(1)} %get-tuple-element.215), channel_id=1, source_target_pairs={{0,16},{4,20},{8,24},{12,28},{16,0},{20,4},{24,8},{28,12},{1,17},{... | collective-permute-start | bytes 540680 | tf_op jit(solution)/shard_map/ppermute | solution.py:29
  222.6 39.5 %collective-permute-start.48 = (bf16[1,704,128]{2,1,0:T(8,128)(2,1)}, bf16[1,704,128]{2,1,0:T(8,128)(2,1)}, u32[]{:S(2)}, u32[]{:S(2)}) collective-permute-start(bf16[1,704,128]{2,1,0:T(8,128)(2,1)} %get-tuple-element.217), channel_id=1, source_target_pairs={{0,16},{4,20},{8,24},{12,28},{16,0},{20,4},{24,8},{28,12},{1,17},{... | collective-permute-start | bytes 540680 | tf_op jit(solution)/shard_map/ppermute | solution.py:29
  228.3 30.8 %collective-permute-start.39 = (bf16[2,256,1024]{2,1,0:T(8,128)(2,1)}, bf16[2,256,1024]{2,1,0:T(8,128)(2,1)S(1)}, u32[]{:S(2)}, u32[]{:S(2)}) collective-permute-start(bf16[2,256,1024]{2,1,0:T(8,128)(2,1)} %get-tuple-element.206), channel_id=1, source_target_pairs={{0,1},{1,0},{2,3},{3,2},{4,5},{5,4},{6,7},{7,6},{8,9},{9,8},{10,11... | collective-permute-start | bytes 3145736 | tf_op jit(solution)/shard_map/ppermute | solution.py:29
  228.5 18.2 %collective-permute-start.44 = (bf16[2,128,768]{2,1,0:T(8,128)(2,1)S(1)}, bf16[2,128,768]{2,1,0:T(8,128)(2,1)S(1)}, u32[]{:S(2)}, u32[]{:S(2)}) collective-permute-start(bf16[2,128,768]{2,1,0:T(8,128)(2,1)S(1)} %get-tuple-element.213), channel_id=1, source_target_pairs={{0,8},{4,12},{8,0},{12,4},{16,24},{20,28},{24,16},{28,20},{1,9},{5... | collective-permute-start | bytes 1179656 | tf_op jit(solution)/shard_map/ppermute | solution.py:29
  (84 other events, 783.7 us)
